TPU v7x, 32 devices: a whole 2x2x4 slice. The times are simulated.
32 devices in a mesh: wide: 8 (over z, x), narrow: 4 (over y, core).
Axes of the slice: x: 2, y: 2, z: 4, core: 2. Of those that a mesh axis runs over, the one named last changes fastest.
Arguments:
- tokens: bfloat16 [65536, 768], P(('wide', 'narrow')), may hold values from -6 to 6
- timestep: int32 [64], P(('wide', 'narrow')), may hold values from 0 to 999
- span_start: int32 [64], P(('wide', 'narrow')), may hold values from 0 to 511
- span_length: int32 [64], P(('wide', 'narrow')), may hold values from 1 to 512
- mask_embed: bfloat16 [768], P('narrow'), may hold values from -6 to 6
- ada_weight: bfloat16 [128, 4608], P(None, 'narrow'), may hold values from -0.5 to 0.5
- ada_bias: bfloat16 [4608], P('narrow'), may hold values from -3 to 3
- norm_first: bfloat16 [768], P('narrow'), may hold values from 0.099609375 to 1.8984375
- query_key_value_weight: bfloat16 [768, 2304], P('narrow'), may hold values from -0.21875 to 0.21875
- output_weight: bfloat16 [768, 768], P('narrow'), may hold values from -1.25 to 1.25
- norm_second: bfloat16 [768], P('narrow'), may hold values from 0.099609375 to 1.8984375
- up_projection_weight: bfloat16 [768, 3072], P('narrow'), may hold values from -0.21875 to 0.21875
- up_projection_bias: bfloat16 [3072], P('narrow'), may hold values from -3 to 3
- down_projection_weight: bfloat16 [3072, 768], P('narrow'), may hold values from -0.109375 to 0.109375
- down_projection_bias: bfloat16 [768], P('narrow'), may hold values from -3 to 3
- cotangent: bfloat16 [65536, 768], P(('wide', 'narrow')), may hold values from -6 to 6
Outputs:
- block_out: bfloat16 [65536, 768], P(('wide', 'narrow'))
- grad_tokens: float32 [65536, 768], P(('wide', 'narrow'))
- grad_mask_embed: float32 [768], P('narrow')
- grad_ada_weight: float32 [128, 4608], P(None, 'narrow')
- grad_ada_bias: float32 [4608], P('narrow')
- grad_norm_first: float32 [768], P('narrow')
- grad_qkv_weight: float32 [768, 2304], P('narrow')
- grad_out_weight: float32 [768, 768], P('narrow')
- grad_norm_second: float32 [768], P('narrow')
- grad_up_weight: float32 [768, 3072], P('narrow')
- grad_up_bias: float32 [3072], P('narrow')
- grad_down_weight: float32 [3072, 768], P('narrow')
- grad_down_bias: float32 [768], P('narrow')
Inputs may be any that keep to these rules, and one draw needn't show every extreme that they name: `timestep`: one diffusion step index per sequence, below 1000. `span_start`: the masked span starts in the first half of its sequence. `span_length`: the masked span holds at least one position and ends inside its sequence.
All inputs are finite; a program needn't handle non-finite values.
Results may differ from a plain program's by a relative error of at most 0.012.
The roundings to bfloat16 on the way count: a program that leaves them out, or rounds other values in their place, can miss the bound.
Values may be sent and summed in bfloat16 or wider, within the bound.
A program may use at most 320 MiB of HBM per device.

v0:
```python
import math

import jax
import jax.numpy as jnp
import numpy as np
from jax import lax
from jax.experimental import pallas as pl
from jax.experimental.pallas import tpu as pltpu
from jax.sharding import PartitionSpec as P

HEAD = 64
PAIR = 2 * HEAD
GROUPS = 3
FINISH_TIMES = [
    [3, 5, 11, 12, 13, 16, 18], [6, 8, 12, 13, 15, 18, 20], [9, 10, 14, 16, 18, 20, 21],
]
EPSILON = 1e-05
FULL_PRECISION = lax.Precision.HIGHEST
F32 = jnp.float32
BF16 = jnp.bfloat16
SCALE = 1.0 / math.sqrt(HEAD)
SCALE2 = SCALE * math.log2(math.e)
VMEM_BYTES = 60 << 20
PLAIN = (((1,), (0,)), ((), ()))
TRANSPOSED = (((1,), (1,)), ((), ()))


def mxu(left, right, dims=PLAIN):
    return lax.dot_general(left, right, dims, preferred_element_type=F32)


def call(
    kernel, name, grid, in_specs, out_specs, out_shape, scratch, flops, moved, exps=0, ident=None
):
    return pl.pallas_call(
        kernel,
        name=name,
        grid=grid,
        in_specs=in_specs,
        out_specs=out_specs,
        out_shape=out_shape,
        scratch_shapes=scratch,
        compiler_params=pltpu.CompilerParams(
            vmem_limit_bytes=VMEM_BYTES, collective_id=ident, has_side_effects=ident is not None
        ),
        cost_estimate=pl.CostEstimate(flops=flops, bytes_accessed=moved, transcendentals=exps),
    )


def whole(shape):
    return pl.BlockSpec(shape, lambda *_: (0,) * len(shape), pipeline_mode=pl.Buffered(1))


def column_third(which, width):
    return pl.BlockSpec((width, width), lambda *_: (0, which), pipeline_mode=pl.Buffered(1))


def smem():
    return pl.BlockSpec(memory_space=pltpu.SMEM)


def time_features(step_ids, feature_count):
    halfway = feature_count // 2
    spacing = jnp.exp(-math.log(10000.0) * jnp.arange(halfway, dtype=F32) / halfway)
    angles = step_ids.astype(F32)[:, None] * spacing[None, :]
    return jax.nn.silu(jnp.concatenate([jnp.cos(angles), jnp.sin(angles)], axis=-1))


def rotary_tables(seq_length):
    halfway = HEAD // 2
    spacing = np.exp(-math.log(10000.0) * np.arange(halfway, dtype=np.float32) / halfway)
    angles = np.arange(seq_length, dtype=np.float32)[:, None] * spacing.astype(np.float32)
    cosine, sine = np.cos(angles), np.sin(angles)
    signed = np.concatenate([-sine, sine] * 2, axis=-1)
    return np.concatenate([cosine] * 4, axis=-1), signed


def partner_lanes(v):
    lane = lax.broadcasted_iota(jnp.int32, (1, PAIR), 1)
    return jnp.where(lax.rem(lane, HEAD) < HEAD // 2, from_ahead(v), from_behind(v))


def from_ahead(v):
    return pltpu.roll(v, PAIR - HEAD // 2, 1)


def from_behind(v):
    return pltpu.roll(v, HEAD // 2, 1)


def masked_rows(tokens, embed, start, length, first_row):
    rows = tokens.shape[0]
    position = lax.broadcasted_iota(jnp.int32, (rows, 1), 0) + first_row
    inside = (position >= start) & (position < start + length)
    return jnp.where(inside, embed, tokens.astype(F32)), inside


def normalized(rows):
    centre = rows - jnp.mean(rows, axis=-1, keepdims=True)
    spread = jnp.mean(centre * centre, axis=-1, keepdims=True)
    inverse = lax.rsqrt(spread + EPSILON)
    return centre * inverse, inverse


def norm_back(d_out, hat, inverse):
    return inverse * (
        d_out
        - jnp.mean(d_out, axis=-1, keepdims=True)
        - hat * jnp.mean(d_out * hat, axis=-1, keepdims=True)
    )


def column_sum(v):
    return jnp.sum(v, axis=0, keepdims=True)


def store_shares(target, value, cols):
    me, ways = lax.axis_index("narrow"), lax.axis_size("narrow")
    share = value.shape[0] // ways
    for place in range(ways):
        lower = pl.multiple_of(place_of(me, place) * share, share)
        target[pl.ds(lower, share), cols] = value[place * share : (place + 1) * share, :]


def place_of(me, other):
    core = lax.rem(me + other, 2)
    chip = lax.rem(me // 2 + other // 2, 2)
    return 2 * (1 - core) + 1 - chip


def owner_at(me, place):
    core, chip = 1 - place // 2, 1 - lax.rem(place, 2)
    return 2 * lax.rem(me // 2 + chip, 2) + lax.rem(me + core, 2)


def project(tokens, starts, lengths, embed, gain, modulation, weight, tables, seqs, block=512):
    rows, width = tokens.shape
    seq_length = rows // seqs
    block = min(block, seq_length)
    per_seq = seq_length // block
    pairs = width // PAIR

    def kernel(starts, lengths, tok, emb, gn, mod, w_q, w_k, w_v, cos, sin, out, nt):
        step = pl.program_id(0)
        seq = step // per_seq
        first = (step - seq * per_seq) * block
        start, _ = masked_rows(tok[...], emb[...], starts[seq], lengths[seq], first)
        hat, _ = normalized(start)
        shift = mod[pl.ds(seq, 1), 0:width]
        scale = mod[pl.ds(seq, 1), width : 2 * width]
        normed = (hat * (gn[...] * (1.0 + scale)) + shift).astype(BF16)
        store_shares(nt, jnp.transpose(normed), slice(None))
        for which, w in enumerate((w_q, w_k)):
            turned = mxu(normed, w[...])
            for part in range(pairs):
                v = turned[:, part * PAIR : (part + 1) * PAIR]
                v = v * cos[...] + partner_lanes(v) * sin[...]
                lower = which * width + part * PAIR
                out[:, lower : lower + PAIR] = v.astype(BF16)
        out[:, 2 * width :] = mxu(normed, w_v[...]).astype(BF16)

    table = pl.BlockSpec((block, PAIR), lambda i: (lax.rem(i, per_seq), 0))
    return call(
        kernel,
        "project",
        (rows // block,),
        [
            smem(),
            smem(),
            pl.BlockSpec((block, width), lambda i: (i, 0)),
            whole((1, width)),
            whole((1, width)),
            whole(modulation.shape),
            column_third(0, width),
            column_third(1, width),
            column_third(2, width),
            table,
            table,
        ],
        (
            pl.BlockSpec((block, 3 * width), lambda i: (i, 0)),
            pl.BlockSpec((width, block), lambda i: (0, i)),
        ),
        (
            jax.ShapeDtypeStruct((rows, 3 * width), BF16),
            jax.ShapeDtypeStruct((width, rows), BF16),
        ),
        [],
        2 * rows * width * 3 * width,
        rows * width * 10 + 6 * width * width,
    )(starts, lengths, tokens, embed, gain, modulation, weight, weight, weight, *tables)


def flip(index, stride):
    return index + stride * (1 - 2 * lax.rem(index // stride, 2))


def exchange_stages():
    count = lax.axis_size("wide")
    strides = [1 << bit for bit in range(1, count.bit_length() - 1)]
    return [("pair", "narrow", 1), ("chip", "narrow", 2), ("split", "wide", 1)] + [
        ("full", "wide", stride) for stride in strides
    ] + [("join", "wide", 1)]


class Steps:
    def in_specs(self):
        return [pl.BlockSpec(memory_space=pl.ANY)] * self.count

    out_specs = in_specs

    def locate(self):
        self.at = {axis: lax.axis_index(axis) for axis in ("wide", "narrow")}
        self.odd = lax.rem(self.at["wide"], 2)

    def half_of(self, rows, which, lower=0):
        side = self.odd if which == 0 else 1 - self.odd
        return pl.ds(pl.multiple_of(lower + side * (rows // 2), rows // 2), rows // 2)

    def greet(self):
        barrier = pltpu.get_barrier_semaphore()
        for axis, stride in self.partners:
            pl.semaphore_signal(
                barrier,
                inc=1,
                device_id={axis: flip(self.at[axis], stride)},
                device_id_type=pl.DeviceIdType.MESH,
            )
        pl.semaphore_wait(barrier, len(self.partners))

    def push(self, source, target, sent, got, axis, stride):
        return pltpu.make_async_remote_copy(
            src_ref=source,
            dst_ref=target,
            send_sem=sent,
            recv_sem=got,
            device_id={axis: flip(self.at[axis], stride)},
            device_id_type=pl.DeviceIdType.MESH,
        )

    def tick(self, now, last):
        planned = sorted(self.plan(), key=lambda item: item[:3])
        for when in sorted({item[0] for item in planned if item[0] < last}):

            @pl.when(now == when)
            def _(when=when):
                if when == 0:
                    self.greet()
                for item in planned:
                    if item[0] == when:
                        item[3]()

    def rest(self, last):
        for item in sorted(self.plan(), key=lambda item: item[:3]):
            if item[0] >= last:
                item[3]()


class Gather(Steps):
    partners = (("narrow", 1), ("narrow", 2), ("wide", 1))

    def __init__(self, shapes, begins, waits, columns=None):
        columns = columns or [(k, 0, shape[1]) for k, shape in enumerate(shapes)]
        self.arrays, self.columns = shapes, columns
        self.shapes = [(shapes[k][0], upper - lower) for k, lower, upper in columns]
        self.begins, self.waits = begins, waits
        self.count = len(columns)

    def in_specs(self):
        return [pl.BlockSpec(memory_space=pl.ANY)] * len(self.arrays)

    out_specs = in_specs

    def out_shape(self):
        return [jax.ShapeDtypeStruct((4 * rows, cols), BF16) for rows, cols in self.arrays]

    def scratch(self):
        dma, held = pltpu.SemaphoreType.DMA, []
        for shape in self.shapes:
            held += [dma((5,)), dma((5,)), dma((2,)), pltpu.VMEM(shape, BF16)]
        return held

    def bind(self, ins, outs, held):
        self.refs = [
            (ins[k].at[:, lower:upper], outs[k].at[:, lower:upper])
            + tuple(held[4 * part : 4 * part + 4])
            for part, (k, lower, upper) in enumerate(self.columns)
        ]
        self.locate()

    def block(self, k, index, which=None):
        rows = self.shapes[k][0]
        if which is None:
            return pl.ds(pl.multiple_of(index * rows, rows), rows)
        return self.half_of(rows, which, index * rows)

    def remote(self, k, step):
        source, out, sent, got, _, _ = self.refs[k]
        me, across = self.at["narrow"], flip(self.at["narrow"], 2)
        axis, stride = (("narrow", 1), ("narrow", 2), ("wide", 1), ("narrow", 1), ("narrow", 1))[step]
        if step == 0:
            ends = (source, out.at[self.block(k, me), :])
        elif step == 1:
            half = self.half_of(self.shapes[k][0], 0)
            ends = (source.at[half, :], out.at[self.block(k, me, 0), :])
        else:
            spot = self.block(k, across, 1 if step == 4 else 0)
            ends = (out.at[spot, :], out.at[spot, :])
        return self.push(*ends, sent.at[step], got.at[step], axis, stride)

    def local(self, k, which):
        source, out, _, _, near, kept = self.refs[k]
        if which == 0:
            return pltpu.make_async_copy(source, kept, near.at[0])
        return pltpu.make_async_copy(
            kept, out.at[self.block(k, self.at["narrow"]), :], near.at[1]
        )

    def begin(self, k):
        self.remote(k, 1).start()
        self.remote(k, 0).start()
        self.local(k, 0).start()

    def relay(self, k):
        self.local(k, 0).wait()
        self.local(k, 1).start()
        self.remote(k, 1).wait()
        self.remote(k, 2).start()
        self.remote(k, 3).start()

    def share(self, k):
        self.remote(k, 2).wait()
        self.remote(k, 4).start()

    def close(self, k):
        self.remote(k, 0).wait()
        self.remote(k, 3).wait()
        self.remote(k, 4).wait()
        self.local(k, 1).wait()

    def plan(self):
        planned = []
        for k in range(self.count):
            when = self.begins[k]
            planned.append((when, 0, k, lambda k=k: self.begin(k)))
            for wait, act in zip(self.waits, (self.relay, self.share, self.close)):
                when += wait
                planned.append((when, 1, k, lambda k=k, act=act: act(k)))
        return planned


class Exchange(Steps):
    def __init__(self, shapes, times, columns=None, spans=None):
        columns = columns or [(k, 0, shape[-1]) for k, shape in enumerate(shapes)]
        spans = spans or ["whole"] * len(shapes)
        self.stages = exchange_stages()
        self.arrays, self.columns = [shape[-2:] for shape in shapes], columns
        self.shapes = [(self.arrays[k][0], upper - lower) for k, lower, upper in columns]
        self.spans = [spans[k] for k, _, _ in columns]
        self.firsts = [2 if span == "tail" else 0 for span in self.spans]
        self.lasts = [1 if span == "head" else len(self.stages) - 1 for span in self.spans]
        self.times = times
        self.count = len(columns)
        self.partners = sorted({(axis, stride) for _, axis, stride in self.stages})

    def in_specs(self):
        return [pl.BlockSpec(memory_space=pl.ANY)] * len(self.arrays)

    out_specs = in_specs

    def out_shape(self):
        return [jax.ShapeDtypeStruct(shape, BF16) for shape in self.arrays]

    def scratch(self):
        held = []
        dma = pltpu.SemaphoreType.DMA
        for (rows, cols), span in zip(self.shapes, self.spans):
            early, late = span != "tail", span != "head"
            held += [
                pltpu.VMEM((2, rows, cols) if early else (2, 16, PAIR), BF16),
                pltpu.VMEM((2 if early else 1, rows, cols), BF16),
                pltpu.VMEM((rows, cols) if early else (16, PAIR), BF16),
                pltpu.VMEM((len(self.stages) - 3, rows // 2, cols) if late else (1, 16, PAIR), BF16),
                pltpu.VMEM((rows // 2, cols) if late else (16, PAIR), BF16),
                dma((len(self.stages),)),
                dma((len(self.stages),)),
                dma((2,)),
            ]
        return held

    def bind(self, ins, outs, held):
        self.refs = []
        for part, (k, lower, upper) in enumerate(self.columns):
            every = (slice(None),) * (1 if self.spans[part] == "tail" else 2)
            self.refs.append(
                (ins[k].at[every + (slice(lower, upper),)], outs[k].at[:, lower:upper])
                + tuple(held[8 * part : 8 * part + 8])
            )
        self.locate()

    def own(self, k):
        kept = self.refs[k][3]
        return kept.at[0 if self.spans[k] == "tail" else 1]

    def remote(self, k, step):
        source, out, pair, kept, chip, halves, mine, sent, got, _ = self.refs[k]
        kind, axis, stride = self.stages[step]
        rows = self.shapes[k][0]
        if kind == "pair":
            ends = (source.at[0:2], pair)
        elif kind == "chip":
            ends = (kept.at[0], chip)
        elif kind == "split":
            ends = (self.own(k).at[self.half_of(rows, 1), :], halves.at[0])
        elif kind == "full":
            ends = (mine, halves.at[step - 2])
        else:
            ends = (mine, out.at[self.half_of(rows, 0), :])
        return self.push(*ends, sent.at[step], got.at[step], axis, stride)

    def load(self, k):
        source, kept, near = self.refs[k][0], self.refs[k][3], self.refs[k][9]
        if self.spans[k] == "tail":
            return pltpu.make_async_copy(source, kept.at[0], near.at[0])
        return pltpu.make_async_copy(source.at[2:4], kept, near.at[0])

    def store(self, k):
        out, mine, near = self.refs[k][1], self.refs[k][6], self.refs[k][9]
        if self.spans[k] == "head":
            return pltpu.make_async_copy(self.own(k), out, near.at[1])
        half = self.half_of(self.shapes[k][0], 0)
        return pltpu.make_async_copy(mine, out.at[half, :], near.at[1])

    def begin(self, k):
        self.load(k).start()
        if self.spans[k] != "tail":
            self.remote(k, 0).start()

    def enter(self, k):
        self.load(k).wait()
        self.remote(k, 2).start()

    def end(self, k, step):
        _, _, pair, kept, chip, halves, mine, _, _, _ = self.refs[k]
        kind = self.stages[step][0]
        self.remote(k, step).wait()
        if kind == "pair":
            self.load(k).wait()
            kept[...] = (kept[...].astype(F32) + pair[...].astype(F32)).astype(BF16)
        elif kind == "chip":
            kept[1] = (kept[1].astype(F32) + chip[...].astype(F32)).astype(BF16)
        elif kind == "split":
            half = self.half_of(self.shapes[k][0], 0)
            own = self.own(k)[half, :].astype(F32)
            mine[...] = (own + halves[0].astype(F32)).astype(BF16)
        elif kind == "full":
            mine[...] = (mine[...].astype(F32) + halves[step - 2].astype(F32)).astype(BF16)
        if step < self.lasts[k]:
            self.remote(k, step + 1).start()
        if step == max(self.lasts[k] - 1, 1):
            self.store(k).start()
        if step == self.lasts[k]:
            self.store(k).wait()

    def plan(self):
        planned = []
        for k, (begin, *ends) in enumerate(self.times):
            first, last = self.firsts[k], self.lasts[k]
            planned.append((begin, 0, k, lambda k=k: self.begin(k)))
            if first:
                planned.append((ends[0], 1, k, lambda k=k: self.enter(k)))
                ends = [0] + ends
            for step in range(first, last + 1):
                when = ends[-1] if step == last else ends[min(step, 4)]
                planned.append((when, 1, k, lambda k=k, step=step: self.end(k, step)))
        return planned


def paced(begins, waits):
    return [[begin + sum(waits[:count]) for count in range(len(waits) + 1)] for begin in begins]


def head_mask(v, half):
    lane = lax.broadcasted_iota(jnp.int32, (1, PAIR), 1)
    keep = (lane < HEAD) if half == 0 else (lane >= HEAD)
    return jnp.where(keep, v, jnp.zeros_like(v))


def attend(qkv, shares, begins, waits, columns, ident, seqs, block=512, per=3):
    rows, width = qkv.shape[0], qkv.shape[1] // 3
    seq_length = rows // seqs
    block = min(block, seq_length)
    pairs = width // PAIR
    count = seq_length // block
    steps = pairs // per
    items = per * count
    wide = per * PAIR

    gathering = Gather([v.shape for v in shares], begins, waits, columns)
    many = len(shares)
    ticks = seqs * steps * items

    def kernel(*refs):
        q_ref, k_ref, v_ref = refs[:3]
        out, total = refs[3 + many : 5 + many]
        v_turned, out_turned, held = refs[5 + 2 * many : 8 + 2 * many]
        gathering.bind(refs[3 : 3 + many], refs[5 + many : 5 + 2 * many], refs[8 + 2 * many :])
        spot = pl.program_id(0) * steps + pl.program_id(1)
        v_turned[...] = jnp.transpose(v_ref[...])

        def place(i):
            pair = i // count
            part = i - pair * count
            return (
                pair,
                pl.ds(pl.multiple_of(pair * PAIR, PAIR), PAIR),
                pl.ds(pl.multiple_of(part * block, block), block),
            )

        def score(i, half):
            _, cols, part = place(i)
            held[half] = mxu(k_ref[:, cols], head_mask(q_ref[part, cols], half), TRANSPOSED)

        def finish(i, half):
            pair, _, part = place(i)
            scores = held[half]
            top = jnp.max(scores, axis=0, keepdims=True)
            exponent = jnp.exp2(scores * SCALE2 - top * SCALE2).astype(BF16)
            head = pl.ds(pl.multiple_of(pair * PAIR + half * HEAD, HEAD), HEAD)
            left = jnp.concatenate([v_turned[head, :], jnp.ones((16, seq_length), BF16)], axis=0)
            mixed = mxu(left, exponent)
            denominator = mixed[HEAD : HEAD + 1]
            out_turned[head, part] = mixed[:HEAD] * (1.0 / denominator)
            total[0, pair, half : half + 1, part] = top * SCALE2 + jnp.log2(denominator)

        score(0, 0)

        def body(i, carry):
            gathering.tick(spot * items + i, ticks)
            score(i, 1)
            finish(i, 0)
            score(jnp.minimum(i + 1, items - 1), 0)
            finish(i, 1)
            return carry

        lax.fori_loop(0, items, body, 0)
        out[...] = jnp.transpose(out_turned[...]).astype(BF16)

        @pl.when(spot == seqs * steps - 1)
        def _():
            gathering.rest(ticks)

    def part_of(which):
        return pl.BlockSpec((seq_length, wide), lambda s, p: (s, which * steps + p))

    return call(
        kernel,
        "attend",
        (seqs, steps),
        [part_of(0), part_of(1), part_of(2)] + gathering.in_specs(),
        [part_of(0), pl.BlockSpec((1, per, 2, seq_length), lambda s, p: (s, p, 0, 0))]
        + gathering.out_specs(),
        [
            jax.ShapeDtypeStruct((rows, width), BF16),
            jax.ShapeDtypeStruct((seqs, pairs, 2, seq_length), F32),
        ]
        + gathering.out_shape(),
        [
            pltpu.VMEM((wide, seq_length), BF16),
            pltpu.VMEM((wide, seq_length), F32),
            pltpu.VMEM((2, seq_length, block), F32),
        ]
        + gathering.scratch(),
        16 * rows * seq_length * width,
        rows * width * 8,
        rows * seq_length * width // HEAD,
        ident,
    )(qkv, qkv, qkv, *shares)


def attend_back(
    qkv, mixture, d_mixture, total, tables, pieces, spans, columns, times, ident, seqs, block=512,
    per=3,
):
    rows, width = mixture.shape
    seq_length = rows // seqs
    block = min(block, seq_length)
    pairs = width // PAIR
    count = seq_length // block
    steps = pairs // per
    items = per * count
    wide = per * PAIR
    exchange = Exchange([v.shape for v in pieces], times, columns, spans)
    many = len(pieces)
    ticks = seqs * steps * items

    def kernel(*refs):
        q_ref, k_ref, v_ref, mix, grad, tot, cos, sin = refs[:8]
        dq, dk, dv = refs[8 + many : 11 + many]
        k_turned, dq_turned, dk_sum, dv_sum, inner, s_held, p_held = refs[
            11 + 2 * many : 18 + 2 * many
        ]
        exchange.bind(refs[8 : 8 + many], refs[11 + many : 11 + 2 * many], refs[18 + 2 * many :])
        spot = pl.program_id(0) * steps + pl.program_id(1)
        k_turned[...] = jnp.transpose(k_ref[...])
        product = jnp.transpose(mix[...].astype(F32) * grad[...].astype(F32))
        for pair in range(per):
            for half in range(2):
                lower = pair * PAIR + half * HEAD
                inner[pair, half : half + 1, :] = column_sum(product[lower : lower + HEAD, :])
        dk_sum[...] = jnp.zeros_like(dk_sum)
        dv_sum[...] = jnp.zeros_like(dv_sum)

        def body(i, carry):
            exchange.tick(spot * items + i, ticks)
            pair = i // count
            part = i - pair * count
            cols = pl.ds(pl.multiple_of(pair * PAIR, PAIR), PAIR)
            part = pl.ds(pl.multiple_of(part * block, block), block)
            for half in range(2):
                head = pl.ds(pl.multiple_of(pair * PAIR + half * HEAD, HEAD), HEAD)
                query = head_mask(q_ref[part, cols], half)
                cot = head_mask(grad[part, cols], half)
                s_held[half] = mxu(k_ref[:, cols], query, TRANSPOSED)
                p_held[half] = mxu(v_ref[:, cols], cot, TRANSPOSED)
                probs = jnp.exp2(s_held[half] * SCALE2 - tot[0, pair, half : half + 1, part])
                d_scores = (probs * (p_held[half] - inner[pair, half : half + 1, part])).astype(BF16)
                dv_sum[:, cols] += mxu(probs.astype(BF16), cot)
                dk_sum[:, cols] += mxu(d_scores, query)
                dq_turned[head, part] = mxu(k_turned[head, :], d_scores)
            return carry

        lax.fori_loop(0, items, body, 0)
        d_queries = jnp.transpose(dq_turned[...])
        for source, target in ((d_queries, dq), (dk_sum, dk)):
            for pair in range(per):
                v = source[:, pair * PAIR : (pair + 1) * PAIR] * SCALE
                v = v * cos[...] - partner_lanes(v) * sin[...]
                target[:, pair * PAIR : (pair + 1) * PAIR] = v.astype(BF16)
        dv[...] = dv_sum[...].astype(BF16)

        @pl.when(spot == seqs * steps - 1)
        def _():
            exchange.rest(ticks)

    def part_of(which):
        return pl.BlockSpec((seq_length, wide), lambda s, p: (s, which * steps + p))

    table = whole((seq_length, PAIR))
    grads = jax.ShapeDtypeStruct((rows, width), BF16)
    return call(
        kernel,
        "attend_back",
        (seqs, steps),
        [part_of(0), part_of(1), part_of(2), part_of(0), part_of(0)]
        + [pl.BlockSpec((1, per, 2, seq_length), lambda s, p: (s, p, 0, 0))]
        + [table] * 2
        + exchange.in_specs(),
        [part_of(0), part_of(0), part_of(0)] + exchange.out_specs(),
        [grads, grads, grads] + exchange.out_shape(),
        [
            pltpu.VMEM((wide, seq_length), BF16),
            pltpu.VMEM((wide, seq_length), F32),
            pltpu.VMEM((seq_length, wide), F32),
            pltpu.VMEM((seq_length, wide), F32),
            pltpu.VMEM((per, 2, seq_length), F32),
            pltpu.VMEM((2, seq_length, block), F32),
            pltpu.VMEM((2, seq_length, block), F32),
        ]
        + exchange.scratch(),
        40 * rows * seq_length * width,
        rows * width * 16,
        rows * seq_length * width // HEAD,
        ident,
    )(qkv, qkv, qkv, mixture, d_mixture, total, *tables, *pieces)


def middle_norm(mixture, tokens, starts, lengths, embed, gain, modulation, weight, seqs, block=512):
    rows, width = tokens.shape
    seq_length = rows // seqs
    block = min(block, seq_length)
    per_seq = seq_length // block

    def kernel(starts, lengths, mix, tok, emb, gn, mod, w, out):
        step = pl.program_id(0)
        seq = step // per_seq
        first = (step - seq * per_seq) * block
        start, _ = masked_rows(tok[...], emb[...], starts[seq], lengths[seq], first)
        middle = start + mod[pl.ds(seq, 1), 2 * width : 3 * width] * mxu(mix[...], w[...])
        hat, _ = normalized(middle)
        shift = mod[pl.ds(seq, 1), 3 * width : 4 * width]
        scale = mod[pl.ds(seq, 1), 4 * width : 5 * width]
        out[...] = (hat * (gn[...] * (1.0 + scale)) + shift).astype(BF16)

    row = pl.BlockSpec((block, width), lambda i: (i, 0))
    return call(
        kernel,
        "middle_norm",
        (rows // block,),
        [smem(), smem(), row, row, whole((1, width)), whole((1, width)), whole(modulation.shape)]
        + [whole(weight.shape)],
        row,
        jax.ShapeDtypeStruct((rows, width), BF16),
        [],
        2 * rows * width * width,
        rows * width * 6,
    )(starts, lengths, mixture, tokens, embed, gain, modulation, weight)


def gelu_pair(v):
    root = math.sqrt(2.0 / math.pi)
    square = v * v
    bent = jnp.tanh(v * (root + (root * 0.044715) * square))
    near = 0.5 + 0.5 * bent
    slope = near + (0.5 * v) * (1.0 - bent * bent) * (root + (3.0 * root * 0.044715) * square)
    return v * near, slope


def group_rows(ref, group, ways):
    part = ref.shape[0] // (ways * GROUPS)
    lowers = [(way * GROUPS + group) * part for way in range(ways)]
    return jnp.concatenate([ref[lower : lower + part, :] for lower in lowers], axis=0)


def group_columns(ref, group, ways):
    part = ref.shape[1] // (ways * GROUPS)
    lowers = [(way * GROUPS + group) * part for way in range(ways)]
    return jnp.concatenate([ref[:, lower : lower + part] for lower in lowers], axis=1)


def grouped_rows(ref, ways):
    part = ref.shape[0] // (ways * GROUPS)
    lowers = [(way * GROUPS + group) * part for group in range(GROUPS) for way in range(ways)]
    return jnp.concatenate([ref[lower : lower + part, :] for lower in lowers], axis=0)


def grouped_columns(ref, ways):
    part = ref.shape[1] // (ways * GROUPS)
    lowers = [(way * GROUPS + group) * part for group in range(GROUPS) for way in range(ways)]
    return jnp.concatenate([ref[:, lower : lower + part] for lower in lowers], axis=1)


def halved(arrays):
    return [
        (k, half * v.shape[-1] // 2, (half + 1) * v.shape[-1] // 2)
        for k, v in enumerate(arrays)
        for half in range(2)
    ]


def hidden_units(normed, cot, modulation, up, up_bias, down, times, ident, seqs, block=512):
    rows, width = normed.shape
    ways = lax.axis_size("narrow")
    units = up.shape[1] // GROUPS
    share, part_units = width // ways, units // ways
    seq_length = rows // seqs
    block = min(block, seq_length)
    per_seq = seq_length // block
    steps = rows // block
    turn = steps + ways
    shape_up, shape_down = (ways, share, units), (ways, part_units, width)
    traded = [jax.ShapeDtypeStruct(v, BF16) for v in (shape_up, shape_down) * 2]
    exchange = Exchange(
        [v.shape for v in traded], times, halved(traded), ["whole"] * 2 + ["head"] * 2
    )

    def kernel(*refs):
        nrm, g, mod, b_up = refs[:4]
        w_ups, w_downs = refs[4 : 4 + ways], refs[4 + ways : 4 + 2 * ways]
        act, d_up, g_bias, d_gate, g_sum = refs[4 + 2 * ways : 9 + 2 * ways]
        outs, left = refs[9 + 2 * ways : 15 + 2 * ways], refs[15 + 2 * ways :]
        n_turned, g_turned, a_held, u_held, down_held, g_up, g_down, near = left[:8]
        exchange.bind(
            [g_up.at[0], g_down.at[0], g_up.at[1], g_down.at[1]], outs[:4], left[8:]
        )
        step = pl.program_id(0)
        group = step // turn
        at = step - group * turn

        @pl.when(step == 0)
        def _():
            exchange.greet()
            d_gate[...] = jnp.zeros_like(d_gate)
            g_sum[...] = jnp.zeros_like(g_sum)

        exchange.tick(step, GROUPS * turn)

        @pl.when(at == 0)
        def _():
            g_bias[...] = jnp.zeros_like(g_bias)
            for way in range(ways):
                down_held[way] = w_downs[way][...]

        part = pl.ds(pl.multiple_of(jnp.minimum(at, steps - 1) * block, block), block)

        @pl.when(at < steps)
        def _():
            seq = at // per_seq
            cotangent = g[...].astype(F32)
            d_branch = (mod[pl.ds(seq, 1), 5 * width : 6 * width] * cotangent).astype(BF16)
            for way in range(ways):
                cols = slice(way * part_units, (way + 1) * part_units)
                upper = mxu(nrm[...], w_ups[way][...]) + b_up[:, cols]
                d_active = mxu(d_branch, w_downs[way][...], TRANSPOSED)
                active, slope = gelu_pair(upper)
                active = active.astype(BF16)
                d_upper = (d_active * slope).astype(BF16)
                act[:, cols] = active
                a_held[part, cols] = active
                d_up[:, cols] = d_upper
                u_held[part, cols] = d_upper
                g_bias[:, cols] += column_sum(d_upper.astype(F32))

        @pl.when(step < steps)
        def _():
            store_shares(n_turned, jnp.transpose(nrm[...]), part)
            g_turned[:, part] = jnp.transpose(g[...])
            g_sum[pl.ds(at // per_seq, 1), :] += column_sum(g[...].astype(F32))

        @pl.when(at >= steps)
        def _():
            place = at - steps
            owner = owner_at(exchange.at["narrow"], place)
            cols = pl.ds(pl.multiple_of(owner * part_units, part_units), part_units)
            product = mxu(n_turned[...], u_held[:, cols]).astype(BF16)
            g_up[group, :, :, cols] = product.reshape(ways, share, part_units)
            own = down_held[owner].astype(F32)
            total = jnp.zeros((part_units, width), F32)
            for seq in range(seqs):
                lower, upper = seq * seq_length, (seq + 1) * seq_length
                product = mxu(g_turned[:, lower:upper], a_held[lower:upper, cols])
                product = jnp.transpose(product)
                total += product * mod[seq : seq + 1, 5 * width : 6 * width]
                d_gate[seq : seq + 1, :] += column_sum(product * own)
            g_down[group, place] = total.astype(BF16)

        @pl.when(step == GROUPS * turn - 1)
        def _():
            copies = [
                pltpu.make_async_copy(source.at[GROUPS - 1], target, near.at[k])
                for k, (source, target) in enumerate(((g_up, outs[4]), (g_down, outs[5])))
            ]
            for copy in copies:
                copy.start()
            exchange.rest(GROUPS * turn)
            for copy in copies:
                copy.wait()

    def early(i):
        return (jnp.minimum(lax.rem(i, turn), steps - 1), 0)

    def fixed(shape):
        return pl.BlockSpec(shape, lambda i: (0,) * len(shape))

    by_rows = pl.BlockSpec(
        (block, units), lambda i: (jnp.minimum(lax.rem(i, turn), steps - 1), i // turn)
    )
    by_group = pl.BlockSpec((1, units), lambda i: (0, i // turn))

    def up_piece(way):
        return pl.BlockSpec((width, part_units), lambda i: (0, way * GROUPS + i // turn))

    def down_piece(way):
        return pl.BlockSpec((part_units, width), lambda i: (way * GROUPS + i // turn, 0))

    assert GROUPS == 3
    anywhere = pl.BlockSpec(memory_space=pl.ANY)
    return call(
        kernel,
        "hidden_units",
        (GROUPS * turn,),
        [pl.BlockSpec((block, width), early)] * 2
        + [whole(modulation.shape), by_group]
        + [up_piece(way) for way in range(ways)]
        + [down_piece(way) for way in range(ways)],
        [by_rows, by_rows, by_group, fixed((seqs, width)), fixed((seqs, width))]
        + exchange.out_specs()
        + [anywhere] * 2,
        [
            jax.ShapeDtypeStruct((rows, units * GROUPS), BF16),
            jax.ShapeDtypeStruct((rows, units * GROUPS), BF16),
            jax.ShapeDtypeStruct((1, units * GROUPS), F32),
            jax.ShapeDtypeStruct((seqs, width), F32),
            jax.ShapeDtypeStruct((seqs, width), F32),
        ]
        + exchange.out_shape()
        + [jax.ShapeDtypeStruct(shape_up, BF16), jax.ShapeDtypeStruct(shape_down, BF16)],
        [
            pltpu.VMEM((width, rows), BF16),
            pltpu.VMEM((width, rows), BF16),
            pltpu.VMEM((rows, units), BF16),
            pltpu.VMEM((rows, units), BF16),
            pltpu.VMEM((ways, part_units, width), BF16),
            pltpu.VMEM((GROUPS,) + shape_up, BF16),
            pltpu.VMEM((GROUPS,) + shape_down, BF16),
            pltpu.SemaphoreType.DMA((2,)),
        ]
        + exchange.scratch(),
        8 * rows * width * units * GROUPS,
        GROUPS * (rows * (width * 4 + units * 4) + 8 * width * units),
        rows * units * GROUPS,
        ident,
    )(normed, cot, modulation, up_bias, *[up] * ways, *[down] * ways)


def middle_back(
    mixture, tokens, cot, starts, lengths, embed, gain, modulation, out_weight, d_upper, up, seqs,
    block=256,
):
    rows, width = tokens.shape
    ways = lax.axis_size("narrow")
    seq_length = rows // seqs
    block = min(block, seq_length)
    per_seq = seq_length // block
    steps = rows // block
    hidden_width = d_upper.shape[1]
    share = width // ways

    def kernel(
        starts, lengths, mix, tok, g, emb, gn, mod, w_out, w_up, d_ups, d_middle_out, d_mix, g_out,
        sums, g_sum,
    ):
        step = pl.program_id(0)
        seq = step // per_seq
        first = (step - seq * per_seq) * block

        @pl.when(step == 0)
        def _():
            g_sum[...] = jnp.zeros_like(g_sum)

        @pl.when(step == seq * per_seq)
        def _():
            sums[...] = jnp.zeros_like(sums)

        def vector(which):
            return mod[pl.ds(seq, 1), which * width : (which + 1) * width]

        attended = mxu(mix[...], w_out[...])
        start, _ = masked_rows(tok[...], emb[...], starts[seq], lengths[seq], first)
        hat, inverse = normalized(start + vector(2) * attended)
        d_normed = mxu(d_ups[...], grouped_columns(w_up, ways), TRANSPOSED)
        d_middle = g[...].astype(F32) + norm_back(
            d_normed * (gn[...] * (1.0 + vector(4))), hat, inverse
        )
        d_middle_out[...] = d_middle
        d_attended = (vector(2) * d_middle).astype(BF16)
        d_mix[...] = mxu(d_attended, w_out[...], TRANSPOSED).astype(BF16)
        g_sum[...] += mxu(jnp.transpose(mix[...]), d_attended)
        sums[0, 0:1, :] += column_sum(d_normed)
        sums[0, 1:2, :] += column_sum(d_normed * hat)
        sums[0, 2:3, :] += column_sum(d_middle * attended)

        @pl.when(step == steps - 1)
        def _():
            for place in range(ways):
                owner = owner_at(lax.axis_index("narrow"), place)
                spot = pl.ds(pl.multiple_of(owner * share, share), share)
                g_out[place] = g_sum[spot, :].astype(BF16)

    row = pl.BlockSpec((block, width), lambda i: (i, 0))
    return call(
        kernel,
        "middle_back",
        (steps,),
        [smem(), smem(), row, row, row, whole((1, width)), whole((1, width))]
        + [whole(modulation.shape), whole(out_weight.shape), whole(up.shape)]
        + [pl.BlockSpec((block, hidden_width), lambda i: (i, 0))],
        (
            row,
            row,
            pl.BlockSpec((ways, share, width), lambda i: (0, 0, 0)),
            pl.BlockSpec((1, 8, width), lambda i: (i // per_seq, 0, 0)),
        ),
        (
            jax.ShapeDtypeStruct((rows, width), F32),
            jax.ShapeDtypeStruct((rows, width), BF16),
            jax.ShapeDtypeStruct((ways, share, width), BF16),
            jax.ShapeDtypeStruct((seqs, 8, width), F32),
        ),
        [pltpu.VMEM((width, width), F32)],
        rows * width * (2 * hidden_width + 6 * width),
        rows * (width * 12 + hidden_width * 2) + 2 * width * hidden_width,
    )(
        starts, lengths, mixture, tokens, cot, embed, gain, modulation, out_weight, up, d_upper,
    )


class Finale(Steps):
    def __init__(self, ways):
        self.ways = ways
        self.wide = lax.axis_size("wide")

    def scratch(self, columns):
        dma = pltpu.SemaphoreType.DMA
        return [
            pltpu.VMEM((self.ways, 8, columns), F32),
            pltpu.VMEM((self.ways, 8, columns), F32),
            pltpu.VMEM((self.wide, 8, columns), F32),
            dma((self.ways,)),
            dma((self.ways,)),
            dma((self.wide,)),
            dma((self.wide,)),
        ]

    def bind(self, held):
        self.parts, self.narrow_got, self.wide_got, *self.sems = held
        self.locate()

    def others(self):
        targets = []
        for offset in range(1, self.ways):
            targets.append({"narrow": lax.rem(self.at["narrow"] + offset, self.ways)})
        for offset in range(1, self.wide):
            targets.append({"wide": lax.rem(self.at["wide"] + offset, self.wide)})
        return targets

    def greet(self):
        barrier = pltpu.get_barrier_semaphore()
        targets = self.others()
        for target in targets:
            pl.semaphore_signal(
                barrier, inc=1, device_id=target, device_id_type=pl.DeviceIdType.MESH
            )
        pl.semaphore_wait(barrier, len(targets))

    def along_narrow(self, offset):
        target = lax.rem(self.at["narrow"] + offset, self.ways)
        return pltpu.make_async_remote_copy(
            src_ref=self.parts.at[target],
            dst_ref=self.narrow_got.at[self.at["narrow"]],
            send_sem=self.sems[0].at[offset],
            recv_sem=self.sems[1].at[offset],
            device_id={"narrow": target},
            device_id_type=pl.DeviceIdType.MESH,
        )

    def along_wide(self, offset):
        me = self.at["wide"]
        return pltpu.make_async_remote_copy(
            src_ref=self.wide_got.at[me],
            dst_ref=self.wide_got.at[me],
            send_sem=self.sems[2].at[offset],
            recv_sem=self.sems[3].at[offset],
            device_id={"wide": lax.rem(me + offset, self.wide)},
            device_id_type=pl.DeviceIdType.MESH,
        )

    def begin(self):
        for offset in range(1, self.ways):
            self.along_narrow(offset).start()
        me = self.at["narrow"]
        self.narrow_got[pl.ds(me, 1)] = self.parts[pl.ds(me, 1)]

    def spread(self, seqs, row_lanes):
        for offset in range(1, self.ways):
            self.along_narrow(offset).wait()
        me = self.at["wide"]
        for way in range(self.ways):
            self.wide_got[pl.ds(me, 1), way * seqs : (way + 1) * seqs, 0:row_lanes] = (
                self.narrow_got[way : way + 1, 0:seqs, 0:row_lanes]
            )
        total = self.narrow_got[0:1, :, row_lanes:]
        for way in range(1, self.ways):
            total += self.narrow_got[way : way + 1, :, row_lanes:]
        self.wide_got[pl.ds(me, 1), :, row_lanes:] = total
        for offset in range(1, self.wide):
            self.along_wide(offset).start()

    def close(self):
        for offset in range(1, self.wide):
            self.along_wide(offset).wait()


def finish(
    turned, d_parts, tokens, d_middle, mixture, starts, lengths, embed, gain, modulation, weight,
    out_weight, down_bias, active, down, features, rows_two, vectors_two, times, ident, seqs,
    exchange_columns=None, tile=256, block=512, late_block=256,
):
    rows, width = tokens.shape
    ways = lax.axis_size("narrow")
    share = width // ways
    seq_length = rows // seqs
    block, late_block = min(block, seq_length), min(late_block, seq_length)
    per_seq, late_per_seq = seq_length // block, seq_length // late_block
    tiles = width // tile
    columns, hidden_width = modulation.shape[1] // ways, active.shape[1]
    time_width = features.shape[1]
    window = 2 * PAIR
    lanes = columns + time_width + window
    early, middle, late = 3 * tiles, rows // block, rows // late_block
    steps = early + middle + late
    exchange = Exchange([(ways, share, width)] * 3, times, exchange_columns)
    finale = Finale(ways)

    def kernel(*refs):
        (
            starts, lengths, left, c_q, c_k, c_v, tok, d_mid, r_q, r_k, r_v, emb, gn, mod, w_q, w_k, w_v,
            tok_late, mix, w_out, b_down, feat, two, vec,
        ) = refs[:24]
        act, w_down = refs[24:26]
        spot = 26
        g_tok, block_out, g_ada, g_ada_bias, g_vec = refs[spot : spot + 5]
        outs = refs[spot + 5 : spot + 8]
        grads, sums = refs[spot + 8 : spot + 10]
        small = 7
        exchange.bind(
            [grads.at[part] for part in range(3)], outs, refs[spot + 10 + small :]
        )
        finale.bind(refs[spot + 10 : spot + 10 + small])
        step = pl.program_id(0)

        @pl.when(step == 0)
        def _():
            finale.greet()
            sums[...] = jnp.zeros_like(sums)

        exchange.tick(step, steps)

        for part, source in enumerate((c_q, c_k, c_v)):

            @pl.when((step >= part * tiles) & (step < (part + 1) * tiles))
            def _(part=part, source=source):
                cols = pl.ds(pl.multiple_of((step - part * tiles) * tile, tile), tile)
                product = mxu(left[...], source[...]).astype(BF16)
                grads[part, :, :, cols] = product.reshape(ways, share, tile)

        @pl.when((step >= early) & (step < early + middle))
        def _():
            at = step - early
            seq = at // per_seq
            first = (at - seq * per_seq) * block
            start, inside = masked_rows(
                tok[...], emb[...], starts[seq], lengths[seq], first
            )
            hat, inverse = normalized(start)
            d_normed = mxu(r_q[...], w_q[...], TRANSPOSED)
            d_normed += mxu(r_k[...], w_k[...], TRANSPOSED)
            d_normed += mxu(r_v[...], w_v[...], TRANSPOSED)
            scale = mod[pl.ds(seq, 1), width : 2 * width]
            d_start = d_mid[...] + norm_back(d_normed * (gn[...] * (1.0 + scale)), hat, inverse)
            g_tok[...] = jnp.where(inside, 0.0, d_start)
            sums[seq, 0:1, :] += column_sum(d_normed)
            sums[seq, 1:2, :] += column_sum(d_normed * hat)
            sums[seq, 2:3, :] += column_sum(jnp.where(inside, d_start, 0.0))

        @pl.when(step == early + middle)
        def _():
            parts = finale.parts
            embed_sum = jnp.zeros((1, width), F32)
            gain_sum = jnp.zeros((1, width), F32)
            for seq in range(seqs):
                shift, scale = sums[seq, 0:1, :], sums[seq, 1:2, :]
                gain_sum += scale * (1.0 + mod[seq : seq + 1, width : 2 * width])
                embed_sum += sums[seq, 2:3, :]
                row = jnp.concatenate([shift, scale * gn[...], two[seq : seq + 1, :]], axis=1)
                for way in range(ways):
                    parts[way, seq : seq + 1, 0:columns] = row[
                        :, way * columns : (way + 1) * columns
                    ]
            for way in range(ways):
                parts[way, 0:seqs, columns : columns + time_width] = feat[...]
                lower = PAIR * (share * way // PAIR)
                parts[way, 0:1, columns + time_width :] = embed_sum[:, lower : lower + window]
                parts[way, 1:2, columns + time_width :] = gain_sum[:, lower : lower + window]
                parts[way, 2:8, columns + time_width :] = vec[way, 2:8, :]
            finale.begin()

        @pl.when(step == early + middle + 2)
        def _():
            finale.spread(seqs, columns + time_width)

        @pl.when(step >= early + middle)
        def _():
            at = step - early - middle
            seq = at // late_per_seq
            first = (at - seq * late_per_seq) * late_block
            start, _ = masked_rows(
                tok_late[...], emb[...], starts[seq], lengths[seq], first
            )
            attended = mxu(mix[...], w_out[...])
            branch = mxu(act[...], grouped_rows(w_down, ways)) + b_down[...]
            hidden = start + mod[pl.ds(seq, 1), 2 * width : 3 * width] * attended
            block_out[...] = (
                hidden + mod[pl.ds(seq, 1), 5 * width : 6 * width] * branch
            ).astype(BF16)

        @pl.when(step == steps - 1)
        def _():
            finale.close()
            got = finale.wide_got
            every = got[...].reshape(finale.wide * 8, lanes)
            d_mods, feats = every[:, 0:columns], every[:, columns : columns + time_width]
            g_ada[...] = lax.dot_general(
                jnp.transpose(feats), d_mods, PLAIN, precision=FULL_PRECISION,
                preferred_element_type=F32,
            )
            g_ada_bias[...] = column_sum(d_mods)
            total = got[0, :, columns + time_width :]
            for index in range(1, finale.wide):
                total += got[index, :, columns + time_width :]
            g_vec[...] = total
            exchange.rest(steps)

    def column(part):
        return pl.BlockSpec((rows, tile), lambda i: (0, jnp.clip(i - part * tiles, 0, tiles - 1)))

    row = pl.BlockSpec((block, width), lambda i: (jnp.clip(i - early, 0, middle - 1), 0))

    def late_row(wide):
        return pl.BlockSpec(
            (late_block, wide), lambda i: (jnp.maximum(i - early - middle, 0), 0)
        )

    def fixed(shape):
        return pl.BlockSpec(shape, lambda i: (0,) * len(shape))

    return call(
        kernel,
        "finish",
        (steps,),
        [smem(), smem(), whole(turned.shape), column(0), column(1), column(2), row, row, row, row, row]
        + [whole((1, width)), whole((1, width)), whole(modulation.shape)]
        + [column_third(which, width) for which in range(3)]
        + [late_row(width), late_row(width), whole((width, width)), whole((1, width))]
        + [whole(features.shape), whole(rows_two.shape), whole(vectors_two.shape)]
        + [late_row(hidden_width), whole(down.shape)],
        [
            row,
            late_row(width),
            fixed((time_width, columns)),
            fixed((1, columns)),
            fixed((8, window)),
        ]
        + exchange.out_specs(),
        [
            jax.ShapeDtypeStruct((rows, width), F32),
            jax.ShapeDtypeStruct((rows, width), BF16),
            jax.ShapeDtypeStruct((time_width, columns), F32),
            jax.ShapeDtypeStruct((1, columns), F32),
            jax.ShapeDtypeStruct((8, window), F32),
        ]
        + exchange.out_shape(),
        [pltpu.VMEM((3, ways, share, width), BF16), pltpu.VMEM((seqs, 8, width), F32)]
        + finale.scratch(lanes)
        + exchange.scratch(),
        2 * rows * width * (7 * width + hidden_width),
        rows * (width * 24 + 2 * hidden_width),
        0,
        ident,
    )(
        starts, lengths, turned, *d_parts, tokens, d_middle, *d_parts, embed, gain, modulation, weight, weight,
        weight,        tokens, mixture, out_weight, down_bias, features, rows_two, vectors_two, active, down,
    )


def gather_first(small, ada, weight, ident):
    share, wide = weight.shape
    width = wide // 3
    columns = [(0, 0, small.shape[1]), (1, 0, ada.shape[1])]
    columns += [(2, k * width, (k + 1) * width) for k in range(3)]
    gathering = Gather([small.shape, ada.shape, weight.shape], [0] * 5, [0] * 3, columns)

    def kernel(*refs):
        gathering.bind(refs[0:3], refs[3:6], refs[6:])
        gathering.greet()
        gathering.begin(0)
        gathering.begin(1)
        gathering.begin(2)
        for k in range(5):
            gathering.relay(k)
            if k + 3 < 5:
                gathering.begin(k + 3)
            if k > 0:
                gathering.share(k - 1)
        gathering.share(4)
        for k in range(5):
            gathering.close(k)

    return call(
        kernel,
        "gather_first",
        (),
        gathering.in_specs(),
        gathering.out_specs(),
        gathering.out_shape(),
        gathering.scratch(),
        0,
        8 * share * wide,
        0,
        ident,
    )(small, ada, weight)


def assemble(ups, downs, out, qkv):
    share, units = ups[0].shape
    part, width = downs[0].shape
    ways = units // part
    groups = len(ups)

    def kernel(*refs):
        up_in, down_in = refs[:groups], refs[groups : 2 * groups]
        out_in, qkv_in = refs[2 * groups], refs[2 * groups + 1 : 2 * groups + 4]
        g_up, g_down, g_out, g_qkv = refs[2 * groups + 4 :]
        for group in range(groups):
            for way in range(ways):
                lower = (way * groups + group) * part
                g_up[:, lower : lower + part] = up_in[group][
                    :, way * part : (way + 1) * part
                ].astype(F32)
            g_down[group] = down_in[group][...].astype(F32)
        g_out[...] = out_in[...].astype(F32)
        for which in range(3):
            g_qkv[:, which * width : (which + 1) * width] = qkv_in[which][...].astype(F32)

    pace = 4
    small, tall = share // pace, part // pace

    def rows(count, columns):
        return pl.BlockSpec((count, columns), lambda i: (i, 0))

    g_up, g_down, g_out, g_qkv = call(
        kernel,
        "assemble",
        (pace,),
        [rows(small, units)] * groups
        + [rows(tall, width)] * groups
        + [rows(small, width)] * 4,
        (
            rows(small, units * groups),
            pl.BlockSpec((groups, tall, width), lambda i: (0, i, 0)),
            rows(small, width),
            rows(small, 3 * width),
        ),
        (
            jax.ShapeDtypeStruct((share, units * groups), F32),
            jax.ShapeDtypeStruct((groups, part, width), F32),
            jax.ShapeDtypeStruct((share, width), F32),
            jax.ShapeDtypeStruct((share, 3 * width), F32),
        ),
        [],
        0,
        12 * share * units * groups,
    )(*ups, *downs, out, *qkv)
    return g_up, g_down.reshape(groups * part, width), g_out, g_qkv


def per_device(
    tokens,
    timestep,
    span_start,
    span_length,
    mask_embed,
    ada_weight,
    ada_bias,
    norm_first,
    query_key_value_weight,
    output_weight,
    norm_second,
    up_projection_weight,
    up_projection_bias,
    down_projection_weight,
    down_projection_bias,
    cotangent,
):
    seqs = timestep.shape[0]
    rows, width = tokens.shape
    seq_length = rows // seqs
    ways = lax.axis_size("narrow")
    me = lax.axis_index("narrow")
    share = width // ways
    unit_share = down_projection_weight.shape[0]
    part = unit_share // GROUPS
    units = ways * part
    time_width, columns = ada_weight.shape

    vectors = (
        ada_bias, mask_embed, norm_first, norm_second, down_projection_bias, up_projection_bias,
    )
    filled, lower = jnp.zeros((32 * PAIR,), BF16), 0
    for v in vectors:
        filled += jnp.pad(v, (lower, filled.shape[0] - lower - v.shape[0]))
        lower += v.shape[0]
    small = filled.reshape(32, PAIR)
    small, ada, w_qkv = gather_first(small, ada_weight, query_key_value_weight, 0)

    small = small.reshape(ways, -1).astype(F32)
    smalls, lower = [], 0
    for v in vectors:
        smalls.append(small[:, lower : lower + v.shape[0]].reshape(1, -1))
        lower += v.shape[0]
    bias_ada, embed, gain_one, gain_two, bias_down, bias_up = smalls
    features = time_features(timestep, time_width)
    modulation = jnp.einsum(
        "sf,wfc->swc",
        features,
        ada.reshape(ways, time_width, columns).astype(F32),
        precision=FULL_PRECISION,
    ).reshape(seqs, -1) + bias_ada
    tables = rotary_tables(seq_length)

    qkv, turned_one = project(
        tokens, span_start, span_length, embed, gain_one, modulation, w_qkv, tables, seqs
    )
    thirds = [
        (which, third * size, (third + 1) * size)
        for which, size in ((1, unit_share * ways // 3), (2, width // 3))
        for third in range(3)
    ]
    mixture, total, w_out, w_up, w_down = attend(
        qkv,
        [output_weight, up_projection_weight, down_projection_weight],
        [0, 1, 3, 6, 8, 11, 13],
        [5, 5, 2],
        [(0, 0, width)] + thirds,
        1,
        seqs,
    )
    normed_two = middle_norm(
        mixture, tokens, span_start, span_length, embed, gain_two, modulation, w_out, seqs
    )
    bias_up = jnp.swapaxes(bias_up.reshape(ways, GROUPS, part), 0, 1).reshape(1, -1)
    head_times = paced([8, 9, 10, 11], [1, 3, 2, 2, 2, 1]) + paced([16, 17, 18, 19], [1, 3])
    active, d_upper, g_bias, d_gate_two, g_sum, *swaps = hidden_units(
        normed_two, cotangent, modulation, w_up, bias_up, w_down, head_times, 2, seqs
    )
    d_gate_two += bias_down * g_sum
    d_middle, d_mixture, g_out, sums_two = middle_back(
        mixture, tokens, cotangent, span_start, span_length, embed, gain_two, modulation, w_out,
        d_upper, w_up, seqs,
    )
    d_q, d_k, d_v, *done = attend_back(
        qkv, mixture, d_mixture, total, tables, swaps[2:] + [g_out],
        ["tail"] * 2 + ["whole"] * 3, halved(swaps[2:] + [g_out]),
        [[k, k + 1] + [k + 1 + n for n in (3, 5, 7, 9)] for k in range(4)]
        + paced([0, 1, 2, 4, 5, 7], [2, 3, 2, 2, 3, 2]),
        3, seqs,
    )
    scale_two = modulation[:, 4 * width : 5 * width]
    rows_two = jnp.concatenate(
        [sums_two[:, 2], sums_two[:, 0], sums_two[:, 1] * gain_two, d_gate_two], axis=1
    )
    g_norm_two = jnp.sum(sums_two[:, 1] * (1.0 + scale_two), axis=0)
    g_bias_down = jnp.sum(modulation[:, 5 * width :] * g_sum, axis=0)
    lowers = [PAIR * (share * way // PAIR) for way in range(ways)]
    vectors_two = jnp.stack(
        [
            jnp.stack([v[lower : lower + 2 * PAIR] for lower in lowers])
            for v in (g_norm_two, g_norm_two, g_norm_two, g_bias_down)
        ]
        + [g_bias[0].reshape(GROUPS, ways, part)[group] for group in range(GROUPS)]
        + [jnp.zeros((ways, 2 * PAIR), F32)],
        axis=1,
    )
    grad_tokens, block_out, grad_ada_weight, grad_ada_bias, vectors, *g_qkv = finish(
        turned_one, (d_q, d_k, d_v), tokens, d_middle, mixture, span_start, span_length, embed,
        gain_one, modulation, w_qkv, w_out, bias_down, active, w_down, features, rows_two,
        vectors_two,
        FINISH_TIMES, 4, seqs,
    )
    skip = lax.rem(share * me, PAIR)
    own = lax.dynamic_slice_in_dim(vectors[:4], skip, share, 1)
    g_ups, g_downs = (swaps[0], *done[0:4:2]), (swaps[1], *done[1:4:2])
    g_up, g_down, g_out, g_qkv = assemble(g_ups, g_downs, done[4], g_qkv)
    return (
        block_out,
        grad_tokens,
        own[0],
        grad_ada_weight,
        grad_ada_bias[0],
        own[1],
        g_qkv,
        g_out,
        own[2],
        g_up,
        vectors[4 : 4 + GROUPS].reshape(-1),
        g_down,
        own[3],
    )


def solution(mesh):
    rows = P(("wide", "narrow"), None)
    per_seq = P(("wide", "narrow"))
    vector, matrix, columns = P("narrow"), P("narrow", None), P(None, "narrow")
    return jax.shard_map(
        per_device,
        mesh=mesh,
        in_specs=(
            rows, per_seq, per_seq, per_seq, vector, columns, vector, vector,
            matrix, matrix, vector, matrix, vector, matrix, vector, rows,
        ),
        out_specs=(
            rows, rows, vector, columns, vector, vector, matrix, matrix, vector, matrix,
            vector, matrix, vector,
        ),
        check_vma=False,
    )
```

profile of v0, /device:TPU:0, one launch (start us, length us, event | category | flops | bytes accessed | tf_op | source)
XLA Modules:
  0.0 412.8 jit_solution(2716285029500924672)
XLA Ops:
  0.6 1.4 add_bitcast_fusion.refs_0_
  2.1 24.8 %gather_first.1 = (bf16[128,128]{1,0:T(8,128)(2,1)}, bf16[512,1152]{1,0:T(8,128)(2,1)}, bf16[768,2304]{1,0:T(8,128)(2,1)}) custom-call(bf16[32,128]{1,0:T(8,128)(2,1)} %add_bitcast_fusion.refs_0_, bf16[128,1152]{1,0:T(8,128)(2,1)} %refs_1_.3, bf16[192,2304]{1,0:T(8,128)(2,1)} %refs_2_.1), custom_call_target="tpu_custom_call" | custom-call | bytes 3538944 | tf_op jit(solution)/shard_map/gather_first/pallas_call | solution.py:1279
  27.0 0.8 reshape.83
  27.7 0.7 fusion.4
  29.7 0.7 convert_element_type.24
  30.6 1.7 copy.35
  32.3 1.6 convolution_add_fusion.mod.refs_2_.refs_13_
  34.0 14.5 %project.1 = (bf16[2048,2304]{1,0:T(8,128)(2,1)}, bf16[768,2048]{1,0:T(8,128)(2,1)}) custom-call(s32[2]{0:T(128)} %refs_0_.1, s32[2]{0:T(128)} %refs_1_.5, bf16[2048,768]{1,0:T(8,128)(2,1)} %refs_17_.1, f32[1,768]{1,0:T(1,128)} %reshape.75.emb.refs_11_, f32[1,768]{1,0:T(1,128)} %reshape.76.gn.refs_12_, f32[2,4608]{1,0:T(2,128)} %convolution_add_fusion.mod.refs_2_.refs_13_, ...), custom_call_target="tpu_custom_call" | custom-call | flops 7247757312 | bytes 19267584 | tf_op jit(solution)/shard_map/project/pallas_call | solution.py:163
  48.5 45.7 %attend.1 = (bf16[2048,768]{1,0:T(8,128)(2,1)}, f32[2,6,2,1024]{3,2,1,0:T(2,128)}, bf16[768,768]{1,0:T(8,128)(2,1)}, bf16[768,3072]{1,0:T(8,128)(2,1)}, bf16[3072,768]{1,0:T(8,128)(2,1)}) custom-call(bf16[2048,2304]{1,0:T(8,128)(2,1)} %get-tuple-element.62.refs_0_.refs_1_.refs_2_, bf16[2048,2304]{1,0:T(8,128)(2,1)} %get-tuple-element.62.refs_0_.refs_1_.refs_2_, ...), custom_call_target="tpu_custom_call" | custom-call | flops 25769803776 | bytes 12582912 | tf_op jit(solution)/shard_map/attend/pallas_call | solution.py:556
  94.2 0.7 reshape.78.gn
  94.9 8.2 %middle_norm.1.refs_0_ = bf16[2048,768]{1,0:T(8,128)(2,1)} custom-call(s32[2]{0:T(128)} %refs_0_.1, s32[2]{0:T(128)} %refs_1_.5, bf16[2048,768]{1,0:T(8,128)(2,1)} %get-tuple-element.63.mix.refs_3_.refs_18_, bf16[2048,768]{1,0:T(8,128)(2,1)} %refs_17_.1, f32[1,768]{1,0:T(1,128)} %reshape.75.emb.refs_11_, f32[1,768]{1,0:T(1,128)} %reshape.78.gn, ...), custom_call_target="tpu_custom_call" | custom-call | flops 2415919104 | bytes 9437184 | tf_op jit(solution)/shard_map/middle_norm/pallas_call | solution.py:696
  103.7 85.4 %hidden_units.1 = (bf16[2048,3072]{1,0:T(8,128)(2,1)}, bf16[2048,3072]{1,0:T(8,128)(2,1)}, f32[1,3072]{1,0:T(1,128)}, f32[2,768]{1,0:T(2,128)}, f32[2,768]{1,0:T...) custom-call(bf16[2048,768]{1,0:T(8,128)(2,1)} %middle_norm.1.refs_0_, ...), custom_call_target="tpu_custom_call" | custom-call | flops 38654705664 | bytes 62914560 | tf_op jit(solution)/shard_map/hidden_units/pallas_call | solution.py:868
  189.2 31.9 %middle_back.1 = (f32[2048,768]{1,0:T(8,128)}, bf16[2048,768]{1,0:T(8,128)(2,1)}, bf16[4,192,768]{2,1,0:T(8,128)(2,1)}, f32[2,8,768]{2,1,0:T(8,128)}) custom-call(s32[2]{0:T(128)} %refs_0_.1, s32[2]{0:T(128)} %refs_1_.5, bf16[2048,768]{1,0:T(8,128)(2,1)} %get-tuple-element.63.mix.refs_3_.refs_18_, bf16[2048,768]{1,0:T(8,128)(2,1)} %refs_17_.1, ...), custom_call_target="tpu_custom_call" | custom-call | flops 16911433728 | bytes 36175872 | tf_op jit(solution)/shard_map/middle_back/pallas_call | solution.py:961
  221.2 99.0 %attend_back.1 = (bf16[2048,768]{1,0:T(8,128)(2,1)}, bf16[2048,768]{1,0:T(8,128)(2,1)}, bf16[2048,768]{1,0:T(8,128)(2,1)}, bf16[192,1024]{1,0:T(8,128)(2,1)}, bf...) custom-call(bf16[2048,2304]{1,0:T(8,128)(2,1)} %get-tuple-element.62.re, ...), custom_call_target="tpu_custom_call" | custom-call | flops 64424509440 | bytes 25165824 | tf_op jit(solution)/shard_map/attend_back/pallas_call | solution.py:651
  321.0 0.7 fusion
  322.5 0.7 stack.63.refs_23_
  323.2 73.3 %finish.1 = (f32[2048,768]{1,0:T(8,128)}, bf16[2048,768]{1,0:T(8,128)(2,1)}, f32[128,1152]{1,0:T(8,128)}, f32[1,1152]{1,0:T(1,128)}, f32[8,256]{1,0:T(8,128)}, /...) custom-call(s32[2]{0:T(128)} %refs_0_.1, s32[2]{0:T(128)} %refs_1_.5, ...), custom_call_target="tpu_custom_call" | custom-call | flops 26575110144 | bytes 50331648 | tf_op jit(solution)/shard_map/finish/pallas_call | solution.py:1217
  396.5 0.8 slice.118
  398.0 1.3 reduce
  399.3 5.4 %assemble.1 = (f32[192,3072]{1,0:T(8,128)}, f32[3,256,768]{2,1,0:T(8,128)}, f32[192,768]{1,0:T(8,128)}, f32[192,2304]{1,0:T(8,128)}) custom-call(bf16[192,1024]{1,0:T(8,128)(2,1)} %get-tuple-element.89.refs_0_, bf16[192,1024]{1,0:T(8,128)(2,1)} %get-tuple-element.90.refs_1_, bf16[192,1024]{1,0:T(8,128)(2,1)} %get-tuple-element.91.refs_2_, ...), custom_call_target="tpu_custom_call" | custom-call | bytes 7077888 | tf_op jit(solution)/shard_map/assemble/pallas_call | solution.py:1321
  405.3 1.7 copy.42
  407.0 2.3 copy-done
  409.2 2.7 copy.43
  411.9 0.8 copy.44
  (44 shorter events, 5.0 us)
Async XLA Ops:
  30.6 17.9 %copy-start.9 = (f32[2,128]{1,0:T(2,128)}, f32[2,128]{1,0:T(2,128)S(1)}, u32[]{:S(2)}) copy-start(f32[2,128]{1,0:T(2,128)S(1)} %divide_multiply_fusion.refs_21_) | copy-start | bytes 3076
  221.1 99.1 %copy-start.4 = (f32[4,192]{1,0:T(4,128)S(1)}, f32[4,192]{1,0:T(4,128)}, u32[]{:S(2)}) copy-start(f32[4,192]{1,0:T(4,128)} %get-tuple-element.105) | copy-start | bytes 9220
  221.1 99.7 %copy-start.3 = (f32[2,8,768]{2,1,0:T(8,128)S(1)}, f32[2,8,768]{2,1,0:T(8,128)}, u32[]{:S(2)}) copy-start(f32[2,8,768]{2,1,0:T(8,128)} %get-tuple-element.79) | copy-start | bytes 147460
  221.1 99.9 %copy-start.7 = (f32[2,768]{1,0:T(2,128)S(1)}, f32[2,768]{1,0:T(2,128)}, u32[]{:S(2)}) copy-start(f32[2,768]{1,0:T(2,128)} %get-tuple-element.80) | copy-start | bytes 18436
  221.1 99.9 %copy-start.8 = (f32[2,768]{1,0:T(2,128)S(1)}, f32[2,768]{1,0:T(2,128)}, u32[]{:S(2)}) copy-start(f32[2,768]{1,0:T(2,128)} %get-tuple-element.81) | copy-start | bytes 18436
  221.2 101.3 %copy-start.5 = (f32[1,3072]{1,0:T(1,128)S(1)}, f32[1,3072]{1,0:T(1,128)}, u32[]{:S(2)}) copy-start(f32[1,3072]{1,0:T(1,128)} %get-tuple-element.82) | copy-start | bytes 36868
  396.5 8.2 %copy-start.6 = (f32[8,256]{1,0:T(8,128)S(1)}, f32[8,256]{1,0:T(8,128)}, u32[]{:S(2)}) copy-start(f32[8,256]{1,0:T(8,128)} %get-tuple-element.86) | copy-start | bytes 24580
  396.5 8.8 %copy-start.1 = (bf16[2048,768]{1,0:T(8,128)(2,1)S(1)}, bf16[2048,768]{1,0:T(8,128)(2,1)}, u32[]{:S(2)}) copy-start(bf16[2048,768]{1,0:T(8,128)(2,1)} %get-tuple-element.147) | copy-start | bytes 9437188
  405.3 3.9 copy-start
  409.2 2.7 copy-start.2
where the time goes:
time: 413 us
  Pallas kernels  388 us (94%)
  local copies, waits for them, and re-layouts  16.9 us (4%)
  other arithmetic  5 us (1%)
    pallas_call x1, Pallas kernels, attend_back(): call(kernel, 'attend_back', (seqs, steps), [part_of(0), part_of(1), part_...  99 us
    pallas_call x1, Pallas kernels, hidden_units(): call(kernel, 'hidden_units', (GROUPS * turn,), [pl.BlockSpec((block, widt...  85.4 us
    pallas_call x1, Pallas kernels, finish(): call(kernel, 'finish', (steps,), [smem(), smem(), whole(turned.shape), co...  73.3 us
    pallas_call x1, Pallas kernels, attend(): call(kernel, 'attend', (seqs, steps), [part_of(0), part_of(1), part_of(2)...  45.7 us
    pallas_call x1, Pallas kernels, middle_back(): call(kernel, 'middle_back', (steps,), [smem(), smem(), row, row, row, who...  31.9 us
    pallas_call x1, Pallas kernels, gather_first(): call(kernel, 'gather_first', (), gathering.in_specs(), gathering.out_spec...  24.8 us
    pallas_call x1, Pallas kernels, project(): call(kernel, 'project', (rows // block,), [smem(), smem(), pl.BlockSpec((...  14.5 us

commit v1 on v0

--- a/solution.py
+++ b/solution.py
@@ -12,7 +12,8 @@
 PAIR = 2 * HEAD
 GROUPS = 3
 FINISH_TIMES = [
-    [3, 5, 11, 12, 13, 16, 18], [6, 8, 12, 13, 15, 18, 20], [9, 10, 14, 16, 18, 20, 21],
+    [1, 3, 7, 8, 9, 11, 13], [2, 4, 8, 9, 10, 13, 15], [3, 5, 9, 10, 12, 15, 17],
+    [4, 6, 10, 12, 14, 17, 18], [5, 6, 10, 12, 14, 17, 18], [6, 7, 12, 14, 16, 18, 18],
 ]
 EPSILON = 1e-05
 FULL_PRECISION = lax.Precision.HIGHEST
@@ -238,17 +239,23 @@
             device_id_type=pl.DeviceIdType.MESH,
         )
 
-    def tick(self, now, last):
+    def tick(self, now, last, bunch=6):
         planned = sorted(self.plan(), key=lambda item: item[:3])
-        for when in sorted({item[0] for item in planned if item[0] < last}):
-
-            @pl.when(now == when)
-            def _(when=when):
-                if when == 0:
-                    self.greet()
-                for item in planned:
-                    if item[0] == when:
-                        item[3]()
+        times = sorted({item[0] for item in planned if item[0] < last})
+        for lower in sorted({when - when % bunch for when in times}):
+
+            @pl.when((now >= lower) & (now < lower + bunch))
+            def _(lower=lower):
+                for when in times:
+                    if lower <= when < lower + bunch:
+                        pl.when(now == when)(lambda when=when: self.take(planned, when))
+
+    def take(self, planned, when):
+        if when == 0:
+            self.greet()
+        for item in planned:
+            if item[0] == when:
+                item[3]()
 
     def rest(self, last):
         for item in sorted(self.plan(), key=lambda item: item[:3]):
@@ -710,22 +717,10 @@
 def gelu_pair(v):
     root = math.sqrt(2.0 / math.pi)
     square = v * v
-    bent = jnp.tanh(v * (root + (root * 0.044715) * square))
-    near = 0.5 + 0.5 * bent
-    slope = near + (0.5 * v) * (1.0 - bent * bent) * (root + (3.0 * root * 0.044715) * square)
-    return v * near, slope
-
-
-def group_rows(ref, group, ways):
-    part = ref.shape[0] // (ways * GROUPS)
-    lowers = [(way * GROUPS + group) * part for way in range(ways)]
-    return jnp.concatenate([ref[lower : lower + part, :] for lower in lowers], axis=0)
-
-
-def group_columns(ref, group, ways):
-    part = ref.shape[1] // (ways * GROUPS)
-    lowers = [(way * GROUPS + group) * part for way in range(ways)]
-    return jnp.concatenate([ref[:, lower : lower + part] for lower in lowers], axis=1)
+    near = 0.5 + 0.5 * jnp.tanh(v * (root + (root * 0.044715) * square))
+    active = v * near
+    bend = 2.0 * root + (6.0 * root * 0.044715) * square
+    return active, near + (active * (1.0 - near)) * bend
 
 
 def grouped_rows(ref, ways):
@@ -780,6 +775,7 @@
         @pl.when(step == 0)
         def _():
             exchange.greet()
+            n_turned[width:, :] = jnp.ones((16, rows), BF16)
             d_gate[...] = jnp.zeros_like(d_gate)
             g_sum[...] = jnp.zeros_like(g_sum)
 
@@ -787,7 +783,6 @@
 
         @pl.when(at == 0)
         def _():
-            g_bias[...] = jnp.zeros_like(g_bias)
             for way in range(ways):
                 down_held[way] = w_downs[way][...]
 
@@ -809,7 +804,6 @@
                 a_held[part, cols] = active
                 d_up[:, cols] = d_upper
                 u_held[part, cols] = d_upper
-                g_bias[:, cols] += column_sum(d_upper.astype(F32))
 
         @pl.when(step < steps)
         def _():
@@ -822,8 +816,11 @@
             place = at - steps
             owner = owner_at(exchange.at["narrow"], place)
             cols = pl.ds(pl.multiple_of(owner * part_units, part_units), part_units)
-            product = mxu(n_turned[...], u_held[:, cols]).astype(BF16)
-            g_up[group, :, :, cols] = product.reshape(ways, share, part_units)
+            product = mxu(n_turned[...], u_held[:, cols])
+            g_bias[:, cols] = product[width : width + 1]
+            g_up[group, :, :, cols] = product[:width].astype(BF16).reshape(
+                ways, share, part_units
+            )
             own = down_held[owner].astype(F32)
             total = jnp.zeros((part_units, width), F32)
             for seq in range(seqs):
@@ -886,7 +883,7 @@
         + exchange.out_shape()
         + [jax.ShapeDtypeStruct(shape_up, BF16), jax.ShapeDtypeStruct(shape_down, BF16)],
         [
-            pltpu.VMEM((width, rows), BF16),
+            pltpu.VMEM((width + 16, rows), BF16),
             pltpu.VMEM((width, rows), BF16),
             pltpu.VMEM((rows, units), BF16),
             pltpu.VMEM((rows, units), BF16),
@@ -1074,7 +1071,7 @@
 def finish(
     turned, d_parts, tokens, d_middle, mixture, starts, lengths, embed, gain, modulation, weight,
     out_weight, down_bias, active, down, features, rows_two, vectors_two, times, ident, seqs,
-    exchange_columns=None, tile=256, block=512, late_block=256,
+    tile=384, block=512, late_block=256,
 ):
     rows, width = tokens.shape
     ways = lax.axis_size("narrow")
@@ -1089,40 +1086,59 @@
     lanes = columns + time_width + window
     early, middle, late = 3 * tiles, rows // block, rows // late_block
     steps = early + middle + late
-    exchange = Exchange([(ways, share, width)] * 3, times, exchange_columns)
+    parts = [jax.ShapeDtypeStruct((ways, share, width), BF16)] * 3
+    exchange = Exchange([v.shape for v in parts], times, halved(parts))
     finale = Finale(ways)
 
     def kernel(*refs):
         (
-            starts, lengths, left, c_q, c_k, c_v, tok, d_mid, r_q, r_k, r_v, emb, gn, mod, w_q, w_k, w_v,
-            tok_late, mix, w_out, b_down, feat, two, vec,
-        ) = refs[:24]
-        act, w_down = refs[24:26]
-        spot = 26
+            starts, lengths, left, q_all, k_all, v_all, tok, d_mid, emb, gn, mod, w_qkv_all,
+            tok_late, mix, w_out_all, b_down, feat, two, vec, act, w_down_all,
+        ) = refs[:21]
+        spot = 21
         g_tok, block_out, g_ada, g_ada_bias, g_vec = refs[spot : spot + 5]
         outs = refs[spot + 5 : spot + 8]
         grads, sums = refs[spot + 8 : spot + 10]
-        small = 7
-        exchange.bind(
-            [grads.at[part] for part in range(3)], outs, refs[spot + 10 + small :]
-        )
-        finale.bind(refs[spot + 10 : spot + 10 + small])
+        d_held, w_qkv, w_out, w_down, near = refs[spot + 10 : spot + 15]
+        small = spot + 15 + 7
+        exchange.bind([grads.at[part] for part in range(3)], outs, refs[small:])
+        finale.bind(refs[spot + 15 : small])
         step = pl.program_id(0)
+        loads = [
+            pltpu.make_async_copy(source, d_held.at[part], near.at[part])
+            for part, source in enumerate((q_all, k_all, v_all))
+        ]
+        loads += [
+            pltpu.make_async_copy(source, target, near.at[3 + which])
+            for which, (source, target) in enumerate(
+                ((w_qkv_all, w_qkv), (w_out_all, w_out), (w_down_all, w_down))
+            )
+        ]
 
         @pl.when(step == 0)
         def _():
+            for load in loads:
+                load.start()
             finale.greet()
             sums[...] = jnp.zeros_like(sums)
 
         exchange.tick(step, steps)
 
-        for part, source in enumerate((c_q, c_k, c_v)):
-
-            @pl.when((step >= part * tiles) & (step < (part + 1) * tiles))
-            def _(part=part, source=source):
-                cols = pl.ds(pl.multiple_of((step - part * tiles) * tile, tile), tile)
-                product = mxu(left[...], source[...]).astype(BF16)
-                grads[part, :, :, cols] = product.reshape(ways, share, tile)
+        for part in range(3):
+            pl.when(step == part * tiles)(loads[part].wait)
+        pl.when(step == early)(loads[3].wait)
+
+        @pl.when(step == early + middle)
+        def _():
+            loads[4].wait()
+            loads[5].wait()
+
+        @pl.when(step < early)
+        def _():
+            part = step // tiles
+            cols = pl.ds(pl.multiple_of((step - part * tiles) * tile, tile), tile)
+            product = mxu(left[...], d_held[part, :, cols]).astype(BF16)
+            grads[part, :, :, cols] = product.reshape(ways, share, tile)
 
         @pl.when((step >= early) & (step < early + middle))
         def _():
@@ -1133,9 +1149,10 @@
                 tok[...], emb[...], starts[seq], lengths[seq], first
             )
             hat, inverse = normalized(start)
-            d_normed = mxu(r_q[...], w_q[...], TRANSPOSED)
-            d_normed += mxu(r_k[...], w_k[...], TRANSPOSED)
-            d_normed += mxu(r_v[...], w_v[...], TRANSPOSED)
+            here = pl.ds(pl.multiple_of(at * block, block), block)
+            d_normed = mxu(d_held[0, here, :], w_qkv[:, 0:width], TRANSPOSED)
+            d_normed += mxu(d_held[1, here, :], w_qkv[:, width : 2 * width], TRANSPOSED)
+            d_normed += mxu(d_held[2, here, :], w_qkv[:, 2 * width :], TRANSPOSED)
             scale = mod[pl.ds(seq, 1), width : 2 * width]
             d_start = d_mid[...] + norm_back(d_normed * (gn[...] * (1.0 + scale)), hat, inverse)
             g_tok[...] = jnp.where(inside, 0.0, d_start)
@@ -1201,9 +1218,6 @@
             g_vec[...] = total
             exchange.rest(steps)
 
-    def column(part):
-        return pl.BlockSpec((rows, tile), lambda i: (0, jnp.clip(i - part * tiles, 0, tiles - 1)))
-
     row = pl.BlockSpec((block, width), lambda i: (jnp.clip(i - early, 0, middle - 1), 0))
 
     def late_row(wide):
@@ -1214,16 +1228,17 @@
     def fixed(shape):
         return pl.BlockSpec(shape, lambda i: (0,) * len(shape))
 
+    anywhere = pl.BlockSpec(memory_space=pl.ANY)
     return call(
         kernel,
         "finish",
         (steps,),
-        [smem(), smem(), whole(turned.shape), column(0), column(1), column(2), row, row, row, row, row]
-        + [whole((1, width)), whole((1, width)), whole(modulation.shape)]
-        + [column_third(which, width) for which in range(3)]
-        + [late_row(width), late_row(width), whole((width, width)), whole((1, width))]
+        [smem(), smem(), whole(turned.shape)]
+        + [anywhere] * 3
+        + [row, row, whole((1, width)), whole((1, width)), whole(modulation.shape), anywhere]
+        + [late_row(width), late_row(width), anywhere, whole((1, width))]
         + [whole(features.shape), whole(rows_two.shape), whole(vectors_two.shape)]
-        + [late_row(hidden_width), whole(down.shape)],
+        + [late_row(hidden_width), anywhere],
         [
             row,
             late_row(width),
@@ -1240,7 +1255,15 @@
             jax.ShapeDtypeStruct((8, window), F32),
         ]
         + exchange.out_shape(),
-        [pltpu.VMEM((3, ways, share, width), BF16), pltpu.VMEM((seqs, 8, width), F32)]
+        [
+            pltpu.VMEM((3, ways, share, width), BF16),
+            pltpu.VMEM((seqs, 8, width), F32),
+            pltpu.VMEM((3, rows, width), BF16),
+            pltpu.VMEM(weight.shape, BF16),
+            pltpu.VMEM(out_weight.shape, BF16),
+            pltpu.VMEM(down.shape, BF16),
+            pltpu.SemaphoreType.DMA((6,)),
+        ]
         + finale.scratch(lanes)
         + exchange.scratch(),
         2 * rows * width * (7 * width + hidden_width),
@@ -1248,8 +1271,7 @@
         0,
         ident,
     )(
-        starts, lengths, turned, *d_parts, tokens, d_middle, *d_parts, embed, gain, modulation, weight, weight,
-        weight,        tokens, mixture, out_weight, down_bias, features, rows_two, vectors_two, active, down,
+        starts, lengths, turned, *d_parts, tokens, d_middle, embed, gain, modulation, weight,        tokens, mixture, out_weight, down_bias, features, rows_two, vectors_two, active, down,
     )
 
 
@@ -1419,7 +1441,7 @@
         mixture, tokens, span_start, span_length, embed, gain_two, modulation, w_out, seqs
     )
     bias_up = jnp.swapaxes(bias_up.reshape(ways, GROUPS, part), 0, 1).reshape(1, -1)
-    head_times = paced([8, 9, 10, 11], [1, 3, 2, 2, 2, 1]) + paced([16, 17, 18, 19], [1, 3])
+    head_times = paced([8, 9, 10, 11], [1, 5, 2, 2, 2, 1]) + paced([17, 17, 18, 19], [1, 4])
     active, d_upper, g_bias, d_gate_two, g_sum, *swaps = hidden_units(
         normed_two, cotangent, modulation, w_up, bias_up, w_down, head_times, 2, seqs
     )
@@ -1431,8 +1453,8 @@
     d_q, d_k, d_v, *done = attend_back(
         qkv, mixture, d_mixture, total, tables, swaps[2:] + [g_out],
         ["tail"] * 2 + ["whole"] * 3, halved(swaps[2:] + [g_out]),
-        [[k, k + 1] + [k + 1 + n for n in (3, 5, 7, 9)] for k in range(4)]
-        + paced([0, 1, 2, 4, 5, 7], [2, 3, 2, 2, 3, 2]),
+        [[1, 2, 5, 8, 11, 13], [2, 3, 6, 9, 12, 14], [3, 4, 7, 10, 13, 15], [4, 5, 8, 11, 14, 16]]
+        + paced([0, 1, 3, 5, 6, 8], [1, 4, 3, 3, 4, 2]),
         3, seqs,
     )
     scale_two = modulation[:, 4 * width : 5 * width]

time: 413 us -> 396 us (0.959)
  Pallas kernels: 388 us -> 370 us
    pallas_call x1, Pallas kernels: 99 us -> 92.3 us  [attend_back(): call(kernel, 'attend_back', (seqs, steps), [part_of(0), part_of(1), part_...]
    pallas_call x1, Pallas kernels: 85.4 us -> 79.8 us  [hidden_units(): call(kernel, 'hidden_units', (GROUPS * turn,), [pl.BlockSpec((block, widt...]
    pallas_call x1, Pallas kernels: 73.3 us -> 68.9 us  [finish(): call(kernel, 'finish', (steps,), [smem(), smem(), whole(turned.shape)] +...]
where the time goes in v1:
time: 396 us; the launch traced here: 395 us
  Pallas kernels  370 us (93%)
  local copies, waits for them, and re-layouts  16.9 us (4%)
  other arithmetic  5 us (1%)
    pallas_call x1, Pallas kernels, attend_back(): call(kernel, 'attend_back', (seqs, steps), [part_of(0), part_of(1), part_...  92.3 us
    pallas_call x1, Pallas kernels, hidden_units(): call(kernel, 'hidden_units', (GROUPS * turn,), [pl.BlockSpec((block, widt...  79.8 us
    pallas_call x1, Pallas kernels, finish(): call(kernel, 'finish', (steps,), [smem(), smem(), whole(turned.shape)] +...  68.9 us
    pallas_call x1, Pallas kernels, attend(): call(kernel, 'attend', (seqs, steps), [part_of(0), part_of(1), part_of(2)...  44.5 us
    pallas_call x1, Pallas kernels, middle_back(): call(kernel, 'middle_back', (steps,), [smem(), smem(), row, row, row, who...  31.9 us
    pallas_call x1, Pallas kernels, gather_first(): call(kernel, 'gather_first', (), gathering.in_specs(), gathering.out_spec...  24.8 us
    pallas_call x1, Pallas kernels, project(): call(kernel, 'project', (rows // block,), [smem(), smem(), pl.BlockSpec((...  14.5 us
    pallas_call x1, Pallas kernels, middle_norm(): call(kernel, 'middle_norm', (rows // block,), [smem(), smem(), row, row,...  8.23 us

profile of v1, /device:TPU:0, one launch (start us, length us, event | category | flops | bytes accessed | tf_op | source)
XLA Modules:
  0.0 394.9 jit_solution(15772793025144472068)
XLA Ops:
  0.6 1.4 add_bitcast_fusion.refs_0_
  2.1 24.8 %gather_first.1 = (bf16[128,128]{1,0:T(8,128)(2,1)}, bf16[512,1152]{1,0:T(8,128)(2,1)}, bf16[768,2304]{1,0:T(8,128)(2,1)}) custom-call(bf16[32,128]{1,0:T(8,128)(2,1)} %add_bitcast_fusion.refs_0_, bf16[128,1152]{1,0:T(8,128)(2,1)} %refs_1_.3, bf16[192,2304]{1,0:T(8,128)(2,1)} %refs_2_.1), custom_call_target="tpu_custom_call" | custom-call | bytes 3538944 | tf_op jit(solution)/shard_map/gather_first/pallas_call | solution.py:1301
  27.0 0.8 reshape.83
  27.7 0.7 fusion.4
  29.7 0.7 convert_element_type.24
  30.6 1.7 copy.35
  32.3 1.6 convolution_add_fusion.mod.refs_2_.refs_10_
  34.0 14.5 %project.1 = (bf16[2048,2304]{1,0:T(8,128)(2,1)}, bf16[768,2048]{1,0:T(8,128)(2,1)}) custom-call(s32[2]{0:T(128)} %refs_0_.1, s32[2]{0:T(128)} %refs_1_.5, bf16[2048,768]{1,0:T(8,128)(2,1)} %refs_12_.1, f32[1,768]{1,0:T(1,128)} %reshape.75.emb.refs_8_, f32[1,768]{1,0:T(1,128)} %reshape.76.gn.refs_9_, f32[2,4608]{1,0:T(2,128)} %convolution_add_fusion.mod.refs_2_.refs_10_, ...), custom_call_target="tpu_custom_call" | custom-call | flops 7247757312 | bytes 19267584 | tf_op jit(solution)/shard_map/project/pallas_call | solution.py:164
  48.5 44.5 %attend.1 = (bf16[2048,768]{1,0:T(8,128)(2,1)}, f32[2,6,2,1024]{3,2,1,0:T(2,128)}, bf16[768,768]{1,0:T(8,128)(2,1)}, bf16[768,3072]{1,0:T(8,128)(2,1)}, bf16[3072,768]{1,0:T(8,128)(2,1)}) custom-call(bf16[2048,2304]{1,0:T(8,128)(2,1)} %get-tuple-element.62.refs_0_.refs_1_.refs_2_, bf16[2048,2304]{1,0:T(8,128)(2,1)} %get-tuple-element.62.refs_0_.refs_1_.refs_2_, ...), custom_call_target="tpu_custom_call" | custom-call | flops 25769803776 | bytes 12582912 | tf_op jit(solution)/shard_map/attend/pallas_call | solution.py:563
  93.1 0.7 reshape.78.gn
  93.7 8.2 %middle_norm.1.refs_0_ = bf16[2048,768]{1,0:T(8,128)(2,1)} custom-call(s32[2]{0:T(128)} %refs_0_.1, s32[2]{0:T(128)} %refs_1_.5, bf16[2048,768]{1,0:T(8,128)(2,1)} %get-tuple-element.63.mix.refs_3_.refs_13_, bf16[2048,768]{1,0:T(8,128)(2,1)} %refs_12_.1, f32[1,768]{1,0:T(1,128)} %reshape.75.emb.refs_8_, f32[1,768]{1,0:T(1,128)} %reshape.78.gn, ...), custom_call_target="tpu_custom_call" | custom-call | flops 2415919104 | bytes 9437184 | tf_op jit(solution)/shard_map/middle_norm/pallas_call | solution.py:703
  102.6 79.8 %hidden_units.1 = (bf16[2048,3072]{1,0:T(8,128)(2,1)}, bf16[2048,3072]{1,0:T(8,128)(2,1)}, f32[1,3072]{1,0:T(1,128)}, f32[2,768]{1,0:T(2,128)}, f32[2,768]{1,0:T...) custom-call(bf16[2048,768]{1,0:T(8,128)(2,1)} %middle_norm.1.refs_0_, ...), custom_call_target="tpu_custom_call" | custom-call | flops 38654705664 | bytes 62914560 | tf_op jit(solution)/shard_map/hidden_units/pallas_call | solution.py:865
  182.4 31.9 %middle_back.1 = (f32[2048,768]{1,0:T(8,128)}, bf16[2048,768]{1,0:T(8,128)(2,1)}, bf16[4,192,768]{2,1,0:T(8,128)(2,1)}, f32[2,8,768]{2,1,0:T(8,128)}) custom-call(s32[2]{0:T(128)} %refs_0_.1, s32[2]{0:T(128)} %refs_1_.5, bf16[2048,768]{1,0:T(8,128)(2,1)} %get-tuple-element.63.mix.refs_3_.refs_13_, bf16[2048,768]{1,0:T(8,128)(2,1)} %refs_12_.1, ...), custom_call_target="tpu_custom_call" | custom-call | flops 16911433728 | bytes 36175872 | tf_op jit(solution)/shard_map/middle_back/pallas_call | solution.py:958
  214.4 92.3 %attend_back.1 = (bf16[2048,768]{1,0:T(8,128)(2,1)}, bf16[2048,768]{1,0:T(8,128)(2,1)}, bf16[2048,768]{1,0:T(8,128)(2,1)}, bf16[192,1024]{1,0:T(8,128)(2,1)}, bf...) custom-call(bf16[2048,2304]{1,0:T(8,128)(2,1)} %get-tuple-element.62.re, ...), custom_call_target="tpu_custom_call" | custom-call | flops 64424509440 | bytes 25165824 | tf_op jit(solution)/shard_map/attend_back/pallas_call | solution.py:658
  307.6 0.7 fusion
  309.0 0.7 stack.63.refs_18_
  309.7 68.9 %finish.1 = (f32[2048,768]{1,0:T(8,128)}, bf16[2048,768]{1,0:T(8,128)(2,1)}, f32[128,1152]{1,0:T(8,128)}, f32[1,1152]{1,0:T(1,128)}, f32[8,256]{1,0:T(8,128)}, /...) custom-call(s32[2]{0:T(128)} %refs_0_.1, s32[2]{0:T(128)} %refs_1_.5, ...), custom_call_target="tpu_custom_call" | custom-call | flops 26575110144 | bytes 50331648 | tf_op jit(solution)/shard_map/finish/pallas_call | solution.py:1232
  378.6 0.8 slice.118
  380.1 1.3 reduce
  381.4 5.4 %assemble.1 = (f32[192,3072]{1,0:T(8,128)}, f32[3,256,768]{2,1,0:T(8,128)}, f32[192,768]{1,0:T(8,128)}, f32[192,2304]{1,0:T(8,128)}) custom-call(bf16[192,1024]{1,0:T(8,128)(2,1)} %get-tuple-element.89.refs_0_, bf16[192,1024]{1,0:T(8,128)(2,1)} %get-tuple-element.90.refs_1_, bf16[192,1024]{1,0:T(8,128)(2,1)} %get-tuple-element.91.refs_2_, ...), custom_call_target="tpu_custom_call" | custom-call | bytes 7077888 | tf_op jit(solution)/shard_map/assemble/pallas_call | solution.py:1343
  387.4 1.7 copy.42
  389.1 2.3 copy-done
  391.4 2.7 copy.43
  394.1 0.8 copy.44
  (44 shorter events, 5.0 us)
Async XLA Ops:
  30.6 17.9 %copy-start.9 = (f32[2,128]{1,0:T(2,128)}, f32[2,128]{1,0:T(2,128)S(1)}, u32[]{:S(2)}) copy-start(f32[2,128]{1,0:T(2,128)S(1)} %divide_multiply_fusion.refs_16_) | copy-start | bytes 3076
  214.3 92.4 %copy-start.4 = (f32[4,192]{1,0:T(4,128)S(1)}, f32[4,192]{1,0:T(4,128)}, u32[]{:S(2)}) copy-start(f32[4,192]{1,0:T(4,128)} %get-tuple-element.105) | copy-start | bytes 9220
  214.3 93.1 %copy-start.3 = (f32[2,8,768]{2,1,0:T(8,128)S(1)}, f32[2,8,768]{2,1,0:T(8,128)}, u32[]{:S(2)}) copy-start(f32[2,8,768]{2,1,0:T(8,128)} %get-tuple-element.79) | copy-start | bytes 147460
  214.3 93.2 %copy-start.7 = (f32[2,768]{1,0:T(2,128)S(1)}, f32[2,768]{1,0:T(2,128)}, u32[]{:S(2)}) copy-start(f32[2,768]{1,0:T(2,128)} %get-tuple-element.80) | copy-start | bytes 18436
  214.3 93.2 %copy-start.8 = (f32[2,768]{1,0:T(2,128)S(1)}, f32[2,768]{1,0:T(2,128)}, u32[]{:S(2)}) copy-start(f32[2,768]{1,0:T(2,128)} %get-tuple-element.81) | copy-start | bytes 18436
  214.3 94.7 %copy-start.5 = (f32[1,3072]{1,0:T(1,128)S(1)}, f32[1,3072]{1,0:T(1,128)}, u32[]{:S(2)}) copy-start(f32[1,3072]{1,0:T(1,128)} %get-tuple-element.82) | copy-start | bytes 36868
  378.6 8.2 %copy-start.6 = (f32[8,256]{1,0:T(8,128)S(1)}, f32[8,256]{1,0:T(8,128)}, u32[]{:S(2)}) copy-start(f32[8,256]{1,0:T(8,128)} %get-tuple-element.86) | copy-start | bytes 24580
  378.6 8.8 %copy-start.1 = (bf16[2048,768]{1,0:T(8,128)(2,1)S(1)}, bf16[2048,768]{1,0:T(8,128)(2,1)}, u32[]{:S(2)}) copy-start(bf16[2048,768]{1,0:T(8,128)(2,1)} %get-tuple-element.147) | copy-start | bytes 9437188
  387.4 3.9 copy-start
  391.4 2.7 copy-start.2

commit v2 on v1

--- a/solution.py
+++ b/solution.py
@@ -12,8 +12,7 @@
 PAIR = 2 * HEAD
 GROUPS = 3
 FINISH_TIMES = [
-    [1, 3, 7, 8, 9, 11, 13], [2, 4, 8, 9, 10, 13, 15], [3, 5, 9, 10, 12, 15, 17],
-    [4, 6, 10, 12, 14, 17, 18], [5, 6, 10, 12, 14, 17, 18], [6, 7, 12, 14, 16, 18, 18],
+    [1, 3, 5, 6, 7, 10, 12], [2, 4, 6, 7, 9, 12, 14], [3, 4, 7, 9, 11, 14, 15],
 ]
 EPSILON = 1e-05
 FULL_PRECISION = lax.Precision.HIGHEST
@@ -586,8 +585,8 @@
 
 
 def attend_back(
-    qkv, mixture, d_mixture, total, tables, pieces, spans, columns, times, ident, seqs, block=512,
-    per=3,
+    qkv, mixture, d_mixture, total, tables, turned, pieces, spans, columns, times, ident, seqs,
+    block=512, per=3,
 ):
     rows, width = mixture.shape
     seq_length = rows // seqs
@@ -597,18 +596,44 @@
     steps = pairs // per
     items = per * count
     wide = per * PAIR
-    exchange = Exchange([v.shape for v in pieces], times, columns, spans)
-    many = len(pieces)
+    ways = lax.axis_size("narrow")
+    share = width // ways
+    own = [jax.ShapeDtypeStruct((ways, share, wide), BF16)] * 3
+    traded = list(pieces) + own
+    exchange = Exchange(
+        [v.shape for v in traded],
+        times,
+        list(columns) + [(len(pieces) + part, 0, wide) for part in range(3)],
+        list(spans) + ["whole"] * 3,
+    )
+    many, outs = len(pieces), len(traded)
+    assert steps == 2
     ticks = seqs * steps * items
 
     def kernel(*refs):
-        q_ref, k_ref, v_ref, mix, grad, tot, cos, sin = refs[:8]
-        dq, dk, dv = refs[8 + many : 11 + many]
-        k_turned, dq_turned, dk_sum, dv_sum, inner, s_held, p_held = refs[
-            11 + 2 * many : 18 + 2 * many
-        ]
-        exchange.bind(refs[8 : 8 + many], refs[11 + many : 11 + 2 * many], refs[18 + 2 * many :])
-        spot = pl.program_id(0) * steps + pl.program_id(1)
+        q_ref, k_ref, v_ref, mix, grad, tot, cos, sin, turned_all = refs[:9]
+        lower = 9 + many
+        dq, dk, dv = refs[lower : lower + 3]
+        out_refs, lower = refs[lower + 3 : lower + 3 + outs], lower + 3 + outs
+        k_turned, dq_turned, dk_sum, dv_sum, inner, s_held, p_held = refs[lower : lower + 7]
+        left, d_held, grads, near = refs[lower + 7 : lower + 11]
+        exchange.bind(
+            list(refs[9 : 9 + many]) + [grads.at[part] for part in range(3)],
+            out_refs,
+            refs[lower + 11 :],
+        )
+        seq = pl.program_id(1)
+        spot = pl.program_id(0) * seqs + seq
+        load = pltpu.make_async_copy(turned_all, left, near.at[0])
+        pl.when(spot == 0)(load.start)
+
+        @pl.when(spot == seqs)
+        def _():
+            load.wait()
+            for part in range(3):
+                product = mxu(left[...], d_held[part]).astype(BF16)
+                grads[part] = product.reshape(ways, share, wide)
+
         k_turned[...] = jnp.transpose(k_ref[...])
         product = jnp.transpose(mix[...].astype(F32) * grad[...].astype(F32))
         for pair in range(per):
@@ -646,23 +671,29 @@
                 target[:, pair * PAIR : (pair + 1) * PAIR] = v.astype(BF16)
         dv[...] = dv_sum[...].astype(BF16)
 
+        @pl.when(spot < seqs)
+        def _():
+            here = pl.ds(pl.multiple_of(seq * seq_length, seq_length), seq_length)
+            for part, target in enumerate((dq, dk, dv)):
+                d_held[part, here, :] = target[...]
+
         @pl.when(spot == seqs * steps - 1)
         def _():
             exchange.rest(ticks)
 
     def part_of(which):
-        return pl.BlockSpec((seq_length, wide), lambda s, p: (s, which * steps + p))
+        return pl.BlockSpec((seq_length, wide), lambda p, s: (s, which * steps + p))
 
     table = whole((seq_length, PAIR))
     grads = jax.ShapeDtypeStruct((rows, width), BF16)
     return call(
         kernel,
         "attend_back",
-        (seqs, steps),
+        (steps, seqs),
         [part_of(0), part_of(1), part_of(2), part_of(0), part_of(0)]
-        + [pl.BlockSpec((1, per, 2, seq_length), lambda s, p: (s, p, 0, 0))]
+        + [pl.BlockSpec((1, per, 2, seq_length), lambda p, s: (s, p, 0, 0))]
         + [table] * 2
-        + exchange.in_specs(),
+        + [pl.BlockSpec(memory_space=pl.ANY)] * (1 + many),
         [part_of(0), part_of(0), part_of(0)] + exchange.out_specs(),
         [grads, grads, grads] + exchange.out_shape(),
         [
@@ -673,13 +704,17 @@
             pltpu.VMEM((per, 2, seq_length), F32),
             pltpu.VMEM((2, seq_length, block), F32),
             pltpu.VMEM((2, seq_length, block), F32),
+            pltpu.VMEM(turned.shape, BF16),
+            pltpu.VMEM((3, rows, wide), BF16),
+            pltpu.VMEM((3, ways, share, wide), BF16),
+            pltpu.SemaphoreType.DMA((1,)),
         ]
         + exchange.scratch(),
         40 * rows * seq_length * width,
         rows * width * 16,
         rows * seq_length * width // HEAD,
         ident,
-    )(qkv, qkv, qkv, mixture, d_mixture, total, *tables, *pieces)
+    )(qkv, qkv, qkv, mixture, d_mixture, total, *tables, turned, *pieces)
 
 
 def middle_norm(mixture, tokens, starts, lengths, embed, gain, modulation, weight, seqs, block=512):
@@ -1071,7 +1106,7 @@
 def finish(
     turned, d_parts, tokens, d_middle, mixture, starts, lengths, embed, gain, modulation, weight,
     out_weight, down_bias, active, down, features, rows_two, vectors_two, times, ident, seqs,
-    tile=384, block=512, late_block=256,
+    wide=384, block=512, late_block=256,
 ):
     rows, width = tokens.shape
     ways = lax.axis_size("narrow")
@@ -1079,15 +1114,13 @@
     seq_length = rows // seqs
     block, late_block = min(block, seq_length), min(late_block, seq_length)
     per_seq, late_per_seq = seq_length // block, seq_length // late_block
-    tiles = width // tile
     columns, hidden_width = modulation.shape[1] // ways, active.shape[1]
     time_width = features.shape[1]
     window = 2 * PAIR
     lanes = columns + time_width + window
-    early, middle, late = 3 * tiles, rows // block, rows // late_block
+    early, middle, late = 3, rows // block, rows // late_block
     steps = early + middle + late
-    parts = [jax.ShapeDtypeStruct((ways, share, width), BF16)] * 3
-    exchange = Exchange([v.shape for v in parts], times, halved(parts))
+    exchange = Exchange([(ways, share, wide)] * 3, times)
     finale = Finale(ways)
 
     def kernel(*refs):
@@ -1125,7 +1158,7 @@
         exchange.tick(step, steps)
 
         for part in range(3):
-            pl.when(step == part * tiles)(loads[part].wait)
+            pl.when(step == part)(loads[part].wait)
         pl.when(step == early)(loads[3].wait)
 
         @pl.when(step == early + middle)
@@ -1135,10 +1168,8 @@
 
         @pl.when(step < early)
         def _():
-            part = step // tiles
-            cols = pl.ds(pl.multiple_of((step - part * tiles) * tile, tile), tile)
-            product = mxu(left[...], d_held[part, :, cols]).astype(BF16)
-            grads[part, :, :, cols] = product.reshape(ways, share, tile)
+            product = mxu(left[...], d_held[step, :, width - wide :]).astype(BF16)
+            grads[step] = product.reshape(ways, share, wide)
 
         @pl.when((step >= early) & (step < early + middle))
         def _():
@@ -1256,7 +1287,7 @@
         ]
         + exchange.out_shape(),
         [
-            pltpu.VMEM((3, ways, share, width), BF16),
+            pltpu.VMEM((3, ways, share, wide), BF16),
             pltpu.VMEM((seqs, 8, width), F32),
             pltpu.VMEM((3, rows, width), BF16),
             pltpu.VMEM(weight.shape, BF16),
@@ -1321,8 +1352,8 @@
 
     def kernel(*refs):
         up_in, down_in = refs[:groups], refs[groups : 2 * groups]
-        out_in, qkv_in = refs[2 * groups], refs[2 * groups + 1 : 2 * groups + 4]
-        g_up, g_down, g_out, g_qkv = refs[2 * groups + 4 :]
+        out_in, qkv_in = refs[2 * groups], refs[2 * groups + 1 : 2 * groups + 7]
+        g_up, g_down, g_out, g_qkv = refs[2 * groups + 7 :]
         for group in range(groups):
             for way in range(ways):
                 lower = (way * groups + group) * part
@@ -1331,8 +1362,9 @@
                 ].astype(F32)
             g_down[group] = down_in[group][...].astype(F32)
         g_out[...] = out_in[...].astype(F32)
-        for which in range(3):
-            g_qkv[:, which * width : (which + 1) * width] = qkv_in[which][...].astype(F32)
+        for which in range(6):
+            lower = (which % 3) * width + (which // 3) * (width // 2)
+            g_qkv[:, lower : lower + width // 2] = qkv_in[which][...].astype(F32)
 
     pace = 4
     small, tall = share // pace, part // pace
@@ -1346,7 +1378,8 @@
         (pace,),
         [rows(small, units)] * groups
         + [rows(tall, width)] * groups
-        + [rows(small, width)] * 4,
+        + [rows(small, width)]
+        + [rows(small, width // 2)] * 6,
         (
             rows(small, units * groups),
             pl.BlockSpec((groups, tall, width), lambda i: (0, i, 0)),
@@ -1451,10 +1484,12 @@
         d_upper, w_up, seqs,
     )
     d_q, d_k, d_v, *done = attend_back(
-        qkv, mixture, d_mixture, total, tables, swaps[2:] + [g_out],
+        qkv, mixture, d_mixture, total, tables, turned_one, swaps[2:] + [g_out],
         ["tail"] * 2 + ["whole"] * 3, halved(swaps[2:] + [g_out]),
         [[1, 2, 5, 8, 11, 13], [2, 3, 6, 9, 12, 14], [3, 4, 7, 10, 13, 15], [4, 5, 8, 11, 14, 16]]
-        + paced([0, 1, 3, 5, 6, 8], [1, 4, 3, 3, 4, 2]),
+        + paced([0, 1, 3, 5], [1, 4, 3, 3, 4, 2])
+        + paced([6, 8], [1, 3, 3, 3, 3, 2])
+        + paced([12, 12, 13], [1, 3, 2, 2, 3, 1]),
         3, seqs,
     )
     scale_two = modulation[:, 4 * width : 5 * width]
@@ -1482,7 +1517,7 @@
     skip = lax.rem(share * me, PAIR)
     own = lax.dynamic_slice_in_dim(vectors[:4], skip, share, 1)
     g_ups, g_downs = (swaps[0], *done[0:4:2]), (swaps[1], *done[1:4:2])
-    g_up, g_down, g_out, g_qkv = assemble(g_ups, g_downs, done[4], g_qkv)
+    g_up, g_down, g_out, g_qkv = assemble(g_ups, g_downs, done[4], done[5:] + g_qkv)
     return (
         block_out,
         grad_tokens,

time: 396 us -> 395 us (level); the launches traced: 395 us -> 389 us
  Pallas kernels: 370 us -> 364 us
    pallas_call x1, Pallas kernels: 68.9 us -> 51.3 us  [finish(): call(kernel, 'finish', (steps,), [smem(), smem(), whole(turned.shape)] +...]
    pallas_call x1, Pallas kernels: 92.3 us -> 103 us  [attend_back(): call(kernel, 'attend_back', (steps, seqs), [part_of(0), part_of(1), part_...]
where the time goes in v2:
time: 395 us; the launch traced here: 389 us
  Pallas kernels  364 us (92%)
  local copies, waits for them, and re-layouts  16.9 us (4%)
  other arithmetic  5 us (1%)
    pallas_call x1, Pallas kernels, attend_back(): call(kernel, 'attend_back', (steps, seqs), [part_of(0), part_of(1), part_...  103 us
    pallas_call x1, Pallas kernels, hidden_units(): call(kernel, 'hidden_units', (GROUPS * turn,), [pl.BlockSpec((block, widt...  79.7 us
    pallas_call x1, Pallas kernels, finish(): call(kernel, 'finish', (steps,), [smem(), smem(), whole(turned.shape)] +...  51.3 us
    pallas_call x1, Pallas kernels, attend(): call(kernel, 'attend', (seqs, steps), [part_of(0), part_of(1), part_of(2)...  44.5 us
    pallas_call x1, Pallas kernels, middle_back(): call(kernel, 'middle_back', (steps,), [smem(), smem(), row, row, row, who...  31.9 us
    pallas_call x1, Pallas kernels, gather_first(): call(kernel, 'gather_first', (), gathering.in_specs(), gathering.out_spec...  24.8 us
    pallas_call x1, Pallas kernels, project(): call(kernel, 'project', (rows // block,), [smem(), smem(), pl.BlockSpec((...  14.5 us
    pallas_call x1, Pallas kernels, middle_norm(): call(kernel, 'middle_norm', (rows // block,), [smem(), smem(), row, row,...  8.23 us

profile of v2, /device:TPU:0, one launch (start us, length us, event | category | flops | bytes accessed | tf_op | source)
XLA Modules:
  0.0 388.6 jit_solution(7847046352924401945)
XLA Ops:
  0.6 1.4 add_bitcast_fusion.refs_0_
  2.1 24.8 %gather_first.1 = (bf16[128,128]{1,0:T(8,128)(2,1)}, bf16[512,1152]{1,0:T(8,128)(2,1)}, bf16[768,2304]{1,0:T(8,128)(2,1)}) custom-call(bf16[32,128]{1,0:T(8,128)(2,1)} %add_bitcast_fusion.refs_0_, bf16[128,1152]{1,0:T(8,128)(2,1)} %refs_1_.3, bf16[192,2304]{1,0:T(8,128)(2,1)} %refs_2_.1), custom_call_target="tpu_custom_call" | custom-call | bytes 3538944 | tf_op jit(solution)/shard_map/gather_first/pallas_call | solution.py:1332
  27.0 0.8 reshape.83
  27.7 0.7 fusion.4
  29.7 0.7 convert_element_type.24
  30.6 1.7 copy.35
  32.3 1.6 convolution_add_fusion.mod.refs_2_.refs_10_
  34.0 14.5 %project.1 = (bf16[2048,2304]{1,0:T(8,128)(2,1)}, bf16[768,2048]{1,0:T(8,128)(2,1)}) custom-call(s32[2]{0:T(128)} %refs_0_.1, s32[2]{0:T(128)} %refs_1_.5, bf16[2048,768]{1,0:T(8,128)(2,1)} %refs_12_.1, f32[1,768]{1,0:T(1,128)} %reshape.75.emb.refs_8_, f32[1,768]{1,0:T(1,128)} %reshape.76.gn.refs_9_, f32[2,4608]{1,0:T(2,128)} %convolution_add_fusion.mod.refs_2_.refs_10_, ...), custom_call_target="tpu_custom_call" | custom-call | flops 7247757312 | bytes 19267584 | tf_op jit(solution)/shard_map/project/pallas_call | solution.py:163
  48.5 44.5 %attend.1 = (bf16[2048,768]{1,0:T(8,128)(2,1)}, f32[2,6,2,1024]{3,2,1,0:T(2,128)}, bf16[768,768]{1,0:T(8,128)(2,1)}, bf16[768,3072]{1,0:T(8,128)(2,1)}, bf16[3072,768]{1,0:T(8,128)(2,1)}) custom-call(bf16[2048,2304]{1,0:T(8,128)(2,1)} %get-tuple-element.65.refs_0_.refs_1_.refs_2_, bf16[2048,2304]{1,0:T(8,128)(2,1)} %get-tuple-element.65.refs_0_.refs_1_.refs_2_, ...), custom_call_target="tpu_custom_call" | custom-call | flops 25769803776 | bytes 12582912 | tf_op jit(solution)/shard_map/attend/pallas_call | solution.py:562
  93.1 0.7 reshape.78.gn
  93.7 8.2 %middle_norm.1.refs_0_ = bf16[2048,768]{1,0:T(8,128)(2,1)} custom-call(s32[2]{0:T(128)} %refs_0_.1, s32[2]{0:T(128)} %refs_1_.5, bf16[2048,768]{1,0:T(8,128)(2,1)} %get-tuple-element.66.mix.refs_3_.refs_13_, bf16[2048,768]{1,0:T(8,128)(2,1)} %refs_12_.1, f32[1,768]{1,0:T(1,128)} %reshape.75.emb.refs_8_, f32[1,768]{1,0:T(1,128)} %reshape.78.gn, ...), custom_call_target="tpu_custom_call" | custom-call | flops 2415919104 | bytes 9437184 | tf_op jit(solution)/shard_map/middle_norm/pallas_call | solution.py:738
  102.6 79.7 %hidden_units.1 = (bf16[2048,3072]{1,0:T(8,128)(2,1)}, bf16[2048,3072]{1,0:T(8,128)(2,1)}, f32[1,3072]{1,0:T(1,128)}, f32[2,768]{1,0:T(2,128)}, f32[2,768]{1,0:T...) custom-call(bf16[2048,768]{1,0:T(8,128)(2,1)} %middle_norm.1.refs_0_, ...), custom_call_target="tpu_custom_call" | custom-call | flops 38654705664 | bytes 62914560 | tf_op jit(solution)/shard_map/hidden_units/pallas_call | solution.py:900
  182.3 31.9 %middle_back.1 = (f32[2048,768]{1,0:T(8,128)}, bf16[2048,768]{1,0:T(8,128)(2,1)}, bf16[4,192,768]{2,1,0:T(8,128)(2,1)}, f32[2,8,768]{2,1,0:T(8,128)}) custom-call(s32[2]{0:T(128)} %refs_0_.1, s32[2]{0:T(128)} %refs_1_.5, bf16[2048,768]{1,0:T(8,128)(2,1)} %get-tuple-element.66.mix.refs_3_.refs_13_, bf16[2048,768]{1,0:T(8,128)(2,1)} %refs_12_.1, ...), custom_call_target="tpu_custom_call" | custom-call | flops 16911433728 | bytes 36175872 | tf_op jit(solution)/shard_map/middle_back/pallas_call | solution.py:993
  214.3 103.2 %attend_back.1 = (bf16[2048,768]{1,0:T(8,128)(2,1)}, bf16[2048,768]{1,0:T(8,128)(2,1)}, bf16[2048,768]{1,0:T(8,128)(2,1)}, bf16[192,1024]{1,0:T(8,128)(2,1)}, bf...) custom-call(bf16[2048,2304]{1,0:T(8,128)(2,1)} %get-tuple-element.65, ...), custom_call_target="tpu_custom_call" | custom-call | flops 64424509440 | bytes 25165824 | tf_op jit(solution)/shard_map/attend_back/pallas_call | solution.py:689
  318.4 0.7 fusion
  319.9 0.7 stack.63.refs_18_
  320.6 51.3 %finish.1 = (f32[2048,768]{1,0:T(8,128)}, bf16[2048,768]{1,0:T(8,128)(2,1)}, f32[128,1152]{1,0:T(8,128)}, f32[1,1152]{1,0:T(1,128)}, f32[8,256]{1,0:T(8,128)}, /...) custom-call(s32[2]{0:T(128)} %refs_0_.1, s32[2]{0:T(128)} %refs_1_.5, ...), custom_call_target="tpu_custom_call" | custom-call | flops 26575110144 | bytes 50331648 | tf_op jit(solution)/shard_map/finish/pallas_call | solution.py:1263
  371.9 0.8 slice.118
  373.4 1.3 reduce
  374.7 5.3 %assemble.1 = (f32[192,3072]{1,0:T(8,128)}, f32[3,256,768]{2,1,0:T(8,128)}, f32[192,768]{1,0:T(8,128)}, f32[192,2304]{1,0:T(8,128)}) custom-call(bf16[192,1024]{1,0:T(8,128)(2,1)} %get-tuple-element.92.refs_0_, bf16[192,1024]{1,0:T(8,128)(2,1)} %get-tuple-element.93.refs_1_, bf16[192,1024]{1,0:T(8,128)(2,1)} %get-tuple-element.94.refs_2_, ...), custom_call_target="tpu_custom_call" | custom-call | bytes 7077888 | tf_op jit(solution)/shard_map/assemble/pallas_call | solution.py:1375
  380.7 1.7 copy.42
  382.3 2.3 copy-done
  384.6 2.7 copy.43
  387.3 0.8 copy.44
  (44 shorter events, 5.0 us)
Async XLA Ops:
  30.6 17.9 %copy-start.9 = (f32[2,128]{1,0:T(2,128)}, f32[2,128]{1,0:T(2,128)S(1)}, u32[]{:S(2)}) copy-start(f32[2,128]{1,0:T(2,128)S(1)} %divide_multiply_fusion.refs_16_) | copy-start | bytes 3076
  214.3 103.3 %copy-start.4 = (f32[4,192]{1,0:T(4,128)S(1)}, f32[4,192]{1,0:T(4,128)}, u32[]{:S(2)}) copy-start(f32[4,192]{1,0:T(4,128)} %get-tuple-element.111) | copy-start | bytes 9220
  214.3 103.9 %copy-start.3 = (f32[2,8,768]{2,1,0:T(8,128)S(1)}, f32[2,8,768]{2,1,0:T(8,128)}, u32[]{:S(2)}) copy-start(f32[2,8,768]{2,1,0:T(8,128)} %get-tuple-element.82) | copy-start | bytes 147460
  214.3 104.1 %copy-start.7 = (f32[2,768]{1,0:T(2,128)S(1)}, f32[2,768]{1,0:T(2,128)}, u32[]{:S(2)}) copy-start(f32[2,768]{1,0:T(2,128)} %get-tuple-element.83) | copy-start | bytes 18436
  214.3 104.1 %copy-start.8 = (f32[2,768]{1,0:T(2,128)S(1)}, f32[2,768]{1,0:T(2,128)}, u32[]{:S(2)}) copy-start(f32[2,768]{1,0:T(2,128)} %get-tuple-element.84) | copy-start | bytes 18436
  214.3 105.5 %copy-start.5 = (f32[1,3072]{1,0:T(1,128)S(1)}, f32[1,3072]{1,0:T(1,128)}, u32[]{:S(2)}) copy-start(f32[1,3072]{1,0:T(1,128)} %get-tuple-element.85) | copy-start | bytes 36868
  371.9 8.2 %copy-start.6 = (f32[8,256]{1,0:T(8,128)S(1)}, f32[8,256]{1,0:T(8,128)}, u32[]{:S(2)}) copy-start(f32[8,256]{1,0:T(8,128)} %get-tuple-element.89) | copy-start | bytes 24580
  371.9 8.8 %copy-start.1 = (bf16[2048,768]{1,0:T(8,128)(2,1)S(1)}, bf16[2048,768]{1,0:T(8,128)(2,1)}, u32[]{:S(2)}) copy-start(bf16[2048,768]{1,0:T(8,128)(2,1)} %get-tuple-element.153) | copy-start | bytes 9437188
  380.7 3.9 %copy-start = (f32[2048,768]{1,0:T(8,128)S(1)}, f32[2048,768]{1,0:T(8,128)}, u32[]{:S(2)}) copy-start(f32[2048,768]{1,0:T(8,128)} %get-tuple-element.154) | copy-start | bytes 18874372
  384.6 2.7 copy-start.2

commit v3 on v2

--- a/solution.py
+++ b/solution.py
@@ -11,8 +11,22 @@
 HEAD = 64
 PAIR = 2 * HEAD
 GROUPS = 3
+HIDDEN_TIMES = [
+    [8, 10, 13, 16, 18, 21, 24], [8, 10, 15, 17, 19, 23, 24], [9, 11, 17], [10, 12, 18],
+    [16, 18, 21], [16, 18, 23], [17, 19, 24], [18, 20, 24],
+]
+MIDDLE_TIMES = [
+    [0, 1, 3, 5, 7, 8], [0, 1, 3, 5, 8, 8],
+]
+BACK_TIMES = [
+    [0, 1, 3, 5, 8, 10], [0, 1, 4, 6, 9, 11], [1, 2, 4, 7, 10, 12], [1, 2, 5, 7, 11, 14],
+    [0, 2, 5, 7, 9, 13, 15], [1, 3, 6, 8, 10, 14, 16], [2, 4, 7, 9, 11, 15, 17],
+    [3, 5, 8, 11, 13, 17, 19], [4, 6, 9, 12, 14, 17, 20], [5, 7, 10, 13, 15, 18, 20],
+    [12, 14, 16], [12, 14, 17], [13, 15, 18],
+]
 FINISH_TIMES = [
-    [1, 3, 5, 6, 7, 10, 12], [2, 4, 6, 7, 9, 12, 14], [3, 4, 7, 9, 11, 14, 15],
+    [0, 2, 4, 6, 9, 12], [0, 2, 5, 7, 10, 13], [0, 2, 5, 7, 12, 15], [1, 4, 6, 8, 11, 14, 15],
+    [2, 4, 7, 10, 13, 15, 15], [3, 4, 8, 11, 14, 15, 15],
 ]
 EPSILON = 1e-05
 FULL_PRECISION = lax.Precision.HIGHEST
@@ -238,7 +252,7 @@
             device_id_type=pl.DeviceIdType.MESH,
         )
 
-    def tick(self, now, last, bunch=6):
+    def tick(self, now, last, bunch=6, greet=True):
         planned = sorted(self.plan(), key=lambda item: item[:3])
         times = sorted({item[0] for item in planned if item[0] < last})
         for lower in sorted({when - when % bunch for when in times}):
@@ -247,10 +261,12 @@
             def _(lower=lower):
                 for when in times:
                     if lower <= when < lower + bunch:
-                        pl.when(now == when)(lambda when=when: self.take(planned, when))
-
-    def take(self, planned, when):
-        if when == 0:
+                        pl.when(now == when)(
+                            lambda when=when: self.take(planned, when, greet)
+                        )
+
+    def take(self, planned, when, greet):
+        if when == 0 and greet:
             self.greet()
         for item in planned:
             if item[0] == when:
@@ -452,15 +468,14 @@
         self.remote(k, step).wait()
         if kind == "pair":
             self.load(k).wait()
-            kept[...] = (kept[...].astype(F32) + pair[...].astype(F32)).astype(BF16)
+            kept[...] = kept[...] + pair[...]
         elif kind == "chip":
-            kept[1] = (kept[1].astype(F32) + chip[...].astype(F32)).astype(BF16)
+            kept[1] = kept[1] + chip[...]
         elif kind == "split":
             half = self.half_of(self.shapes[k][0], 0)
-            own = self.own(k)[half, :].astype(F32)
-            mine[...] = (own + halves[0].astype(F32)).astype(BF16)
+            mine[...] = self.own(k)[half, :] + halves[0]
         elif kind == "full":
-            mine[...] = (mine[...].astype(F32) + halves[step - 2].astype(F32)).astype(BF16)
+            mine[...] = mine[...] + halves[step - 2]
         if step < self.lasts[k]:
             self.remote(k, step + 1).start()
         if step == max(self.lasts[k] - 1, 1):
@@ -604,7 +619,7 @@
         [v.shape for v in traded],
         times,
         list(columns) + [(len(pieces) + part, 0, wide) for part in range(3)],
-        list(spans) + ["whole"] * 3,
+        list(spans) + ["head"] * 3,
     )
     many, outs = len(pieces), len(traded)
     assert steps == 2
@@ -791,7 +806,7 @@
     shape_up, shape_down = (ways, share, units), (ways, part_units, width)
     traded = [jax.ShapeDtypeStruct(v, BF16) for v in (shape_up, shape_down) * 2]
     exchange = Exchange(
-        [v.shape for v in traded], times, halved(traded), ["whole"] * 2 + ["head"] * 2
+        [v.shape for v in traded], times, halved(traded), ["whole"] + ["head"] * 3
     )
 
     def kernel(*refs):
@@ -936,8 +951,8 @@
 
 
 def middle_back(
-    mixture, tokens, cot, starts, lengths, embed, gain, modulation, out_weight, d_upper, up, seqs,
-    block=256,
+    mixture, tokens, cot, starts, lengths, embed, gain, modulation, out_weight, d_upper, up, pieces, times,
+    ident, seqs, block=256,
 ):
     rows, width = tokens.shape
     ways = lax.axis_size("narrow")
@@ -948,13 +963,18 @@
     hidden_width = d_upper.shape[1]
     share = width // ways
 
-    def kernel(
-        starts, lengths, mix, tok, g, emb, gn, mod, w_out, w_up, d_ups, d_middle_out, d_mix, g_out,
-        sums, g_sum,
-    ):
+    many = len(pieces)
+    exchange = Exchange([v.shape for v in pieces], times, halved(pieces), ["tail"] * many)
+
+    def kernel(*refs):
+        starts, lengths, mix, tok, g, emb, gn, mod, w_out, w_up, d_ups = refs[:11]
+        d_middle_out, d_mix, g_out, sums = refs[11 + many : 15 + many]
+        g_sum = refs[15 + 2 * many]
+        exchange.bind(refs[11 : 11 + many], refs[15 + many : 15 + 2 * many], refs[16 + 2 * many :])
         step = pl.program_id(0)
         seq = step // per_seq
         first = (step - seq * per_seq) * block
+        exchange.tick(step, steps)
 
         @pl.when(step == 0)
         def _():
@@ -985,9 +1005,10 @@
         @pl.when(step == steps - 1)
         def _():
             for place in range(ways):
-                owner = owner_at(lax.axis_index("narrow"), place)
+                owner = owner_at(exchange.at["narrow"], place)
                 spot = pl.ds(pl.multiple_of(owner * share, share), share)
                 g_out[place] = g_sum[spot, :].astype(BF16)
+            exchange.rest(steps)
 
     row = pl.BlockSpec((block, width), lambda i: (i, 0))
     return call(
@@ -996,24 +1017,30 @@
         (steps,),
         [smem(), smem(), row, row, row, whole((1, width)), whole((1, width))]
         + [whole(modulation.shape), whole(out_weight.shape), whole(up.shape)]
-        + [pl.BlockSpec((block, hidden_width), lambda i: (i, 0))],
-        (
+        + [pl.BlockSpec((block, hidden_width), lambda i: (i, 0))]
+        + exchange.in_specs(),
+        [
             row,
             row,
             pl.BlockSpec((ways, share, width), lambda i: (0, 0, 0)),
             pl.BlockSpec((1, 8, width), lambda i: (i // per_seq, 0, 0)),
-        ),
-        (
+        ]
+        + exchange.out_specs(),
+        [
             jax.ShapeDtypeStruct((rows, width), F32),
             jax.ShapeDtypeStruct((rows, width), BF16),
             jax.ShapeDtypeStruct((ways, share, width), BF16),
             jax.ShapeDtypeStruct((seqs, 8, width), F32),
-        ),
-        [pltpu.VMEM((width, width), F32)],
+        ]
+        + exchange.out_shape(),
+        [pltpu.VMEM((width, width), F32)] + exchange.scratch(),
         rows * width * (2 * hidden_width + 6 * width),
         rows * (width * 12 + hidden_width * 2) + 2 * width * hidden_width,
+        0,
+        ident,
     )(
         starts, lengths, mixture, tokens, cot, embed, gain, modulation, out_weight, up, d_upper,
+        *pieces,
     )
 
 
@@ -1105,7 +1132,8 @@
 
 def finish(
     turned, d_parts, tokens, d_middle, mixture, starts, lengths, embed, gain, modulation, weight,
-    out_weight, down_bias, active, down, features, rows_two, vectors_two, times, ident, seqs,
+    out_weight, down_bias, active, down, features, rows_two, vectors_two, pieces, times,
+    ident, seqs,
     wide=384, block=512, late_block=256,
 ):
     rows, width = tokens.shape
@@ -1120,7 +1148,12 @@
     lanes = columns + time_width + window
     early, middle, late = 3, rows // block, rows // late_block
     steps = early + middle + late
-    exchange = Exchange([(ways, share, wide)] * 3, times)
+    exchange = Exchange(
+        [v.shape for v in pieces] + [(ways, share, wide)] * 3,
+        times,
+        None,
+        ["tail"] * 3 + ["whole"] * 3,
+    )
     finale = Finale(ways)
 
     def kernel(*refs):
@@ -1128,14 +1161,16 @@
             starts, lengths, left, q_all, k_all, v_all, tok, d_mid, emb, gn, mod, w_qkv_all,
             tok_late, mix, w_out_all, b_down, feat, two, vec, act, w_down_all,
         ) = refs[:21]
-        spot = 21
+        spot = 24
         g_tok, block_out, g_ada, g_ada_bias, g_vec = refs[spot : spot + 5]
-        outs = refs[spot + 5 : spot + 8]
-        grads, sums = refs[spot + 8 : spot + 10]
-        d_held, w_qkv, w_out, w_down, near = refs[spot + 10 : spot + 15]
-        small = spot + 15 + 7
-        exchange.bind([grads.at[part] for part in range(3)], outs, refs[small:])
-        finale.bind(refs[spot + 15 : small])
+        outs = refs[spot + 5 : spot + 11]
+        grads, sums = refs[spot + 11 : spot + 13]
+        d_held, w_qkv, w_out, w_down, near = refs[spot + 13 : spot + 18]
+        small = spot + 18 + 7
+        exchange.bind(
+            list(refs[21:24]) + [grads.at[part] for part in range(3)], outs, refs[small:]
+        )
+        finale.bind(refs[spot + 18 : small])
         step = pl.program_id(0)
         loads = [
             pltpu.make_async_copy(source, d_held.at[part], near.at[part])
@@ -1155,7 +1190,7 @@
             finale.greet()
             sums[...] = jnp.zeros_like(sums)
 
-        exchange.tick(step, steps)
+        exchange.tick(step, steps, greet=False)
 
         for part in range(3):
             pl.when(step == part)(loads[part].wait)
@@ -1269,7 +1304,8 @@
         + [row, row, whole((1, width)), whole((1, width)), whole(modulation.shape), anywhere]
         + [late_row(width), late_row(width), anywhere, whole((1, width))]
         + [whole(features.shape), whole(rows_two.shape), whole(vectors_two.shape)]
-        + [late_row(hidden_width), anywhere],
+        + [late_row(hidden_width)]
+        + [anywhere] * 4,
         [
             row,
             late_row(width),
@@ -1302,7 +1338,7 @@
         0,
         ident,
     )(
-        starts, lengths, turned, *d_parts, tokens, d_middle, embed, gain, modulation, weight,        tokens, mixture, out_weight, down_bias, features, rows_two, vectors_two, active, down,
+        starts, lengths, turned, *d_parts, tokens, d_middle, embed, gain, modulation, weight,        tokens, mixture, out_weight, down_bias, features, rows_two, vectors_two, active, down, *pieces,
     )
 
 
@@ -1474,22 +1510,19 @@
         mixture, tokens, span_start, span_length, embed, gain_two, modulation, w_out, seqs
     )
     bias_up = jnp.swapaxes(bias_up.reshape(ways, GROUPS, part), 0, 1).reshape(1, -1)
-    head_times = paced([8, 9, 10, 11], [1, 5, 2, 2, 2, 1]) + paced([17, 17, 18, 19], [1, 4])
+    head_times = HIDDEN_TIMES
     active, d_upper, g_bias, d_gate_two, g_sum, *swaps = hidden_units(
         normed_two, cotangent, modulation, w_up, bias_up, w_down, head_times, 2, seqs
     )
     d_gate_two += bias_down * g_sum
-    d_middle, d_mixture, g_out, sums_two = middle_back(
+    d_middle, d_mixture, g_out, sums_two, g_down_first = middle_back(
         mixture, tokens, cotangent, span_start, span_length, embed, gain_two, modulation, w_out,
-        d_upper, w_up, seqs,
+        d_upper, w_up, swaps[1:2], MIDDLE_TIMES, 5, seqs,
     )
     d_q, d_k, d_v, *done = attend_back(
         qkv, mixture, d_mixture, total, tables, turned_one, swaps[2:] + [g_out],
         ["tail"] * 2 + ["whole"] * 3, halved(swaps[2:] + [g_out]),
-        [[1, 2, 5, 8, 11, 13], [2, 3, 6, 9, 12, 14], [3, 4, 7, 10, 13, 15], [4, 5, 8, 11, 14, 16]]
-        + paced([0, 1, 3, 5], [1, 4, 3, 3, 4, 2])
-        + paced([6, 8], [1, 3, 3, 3, 3, 2])
-        + paced([12, 12, 13], [1, 3, 2, 2, 3, 1]),
+        BACK_TIMES,
         3, seqs,
     )
     scale_two = modulation[:, 4 * width : 5 * width]
@@ -1512,12 +1545,12 @@
         turned_one, (d_q, d_k, d_v), tokens, d_middle, mixture, span_start, span_length, embed,
         gain_one, modulation, w_qkv, w_out, bias_down, active, w_down, features, rows_two,
         vectors_two,
-        FINISH_TIMES, 4, seqs,
+        done[5:], FINISH_TIMES, 4, seqs,
     )
     skip = lax.rem(share * me, PAIR)
     own = lax.dynamic_slice_in_dim(vectors[:4], skip, share, 1)
-    g_ups, g_downs = (swaps[0], *done[0:4:2]), (swaps[1], *done[1:4:2])
-    g_up, g_down, g_out, g_qkv = assemble(g_ups, g_downs, done[4], done[5:] + g_qkv)
+    g_ups, g_downs = (swaps[0], *done[0:4:2]), (g_down_first, *done[1:4:2])
+    g_up, g_down, g_out, g_qkv = assemble(g_ups, g_downs, done[4], g_qkv)
     return (
         block_out,
         grad_tokens,

time: 395 us -> 399 us (1.010); the launches traced: 389 us -> 398 us
  Pallas kernels: 364 us -> 374 us
    pallas_call x1, Pallas kernels: 31.9 us -> 41.1 us  [middle_back(): call(kernel, 'middle_back', (steps,), [smem(), smem(), row, row, row, who...]
    pallas_call x1, Pallas kernels: 51.3 us -> 60.5 us  [finish(): call(kernel, 'finish', (steps,), [smem(), smem(), whole(turned.shape)] +...]
    pallas_call x1, Pallas kernels: 103 us -> 98.8 us  [attend_back(): call(kernel, 'attend_back', (steps, seqs), [part_of(0), part_of(1), part_...]
where the time goes in v3:
time: 399 us; the launch traced here: 398 us
  Pallas kernels  374 us (94%)
  local copies, waits for them, and re-layouts  16.9 us (4%)
  other arithmetic  5 us (1%)
    pallas_call x1, Pallas kernels, attend_back(): call(kernel, 'attend_back', (steps, seqs), [part_of(0), part_of(1), part_...  98.8 us
    pallas_call x1, Pallas kernels, hidden_units(): call(kernel, 'hidden_units', (GROUPS * turn,), [pl.BlockSpec((block, widt...  75.8 us
    pallas_call x1, Pallas kernels, finish(): call(kernel, 'finish', (steps,), [smem(), smem(), whole(turned.shape)] +...  60.5 us
    pallas_call x1, Pallas kernels, attend(): call(kernel, 'attend', (seqs, steps), [part_of(0), part_of(1), part_of(2)...  44.5 us
    pallas_call x1, Pallas kernels, middle_back(): call(kernel, 'middle_back', (steps,), [smem(), smem(), row, row, row, who...  41.1 us
    pallas_call x1, Pallas kernels, gather_first(): call(kernel, 'gather_first', (), gathering.in_specs(), gathering.out_spec...  24.8 us
    pallas_call x1, Pallas kernels, project(): call(kernel, 'project', (rows // block,), [smem(), smem(), pl.BlockSpec((...  14.5 us
    pallas_call x1, Pallas kernels, middle_norm(): call(kernel, 'middle_norm', (rows // block,), [smem(), smem(), row, row,...  8.23 us

profile of v3, /device:TPU:0, one launch (start us, length us, event | category | flops | bytes accessed | tf_op | source)
XLA Modules:
  0.0 398.1 jit_solution(14101025910426602429)
XLA Ops:
  0.6 1.4 add_bitcast_fusion.refs_0_
  2.1 24.8 %gather_first.1 = (bf16[128,128]{1,0:T(8,128)(2,1)}, bf16[512,1152]{1,0:T(8,128)(2,1)}, bf16[768,2304]{1,0:T(8,128)(2,1)}) custom-call(bf16[32,128]{1,0:T(8,128)(2,1)} %add_bitcast_fusion.refs_0_, bf16[128,1152]{1,0:T(8,128)(2,1)} %refs_1_.4, bf16[192,2304]{1,0:T(8,128)(2,1)} %refs_2_.1), custom_call_target="tpu_custom_call" | custom-call | bytes 3538944 | tf_op jit(solution)/shard_map/gather_first/pallas_call | solution.py:1368
  27.0 0.8 reshape.83
  27.7 0.7 fusion.4
  29.7 0.7 convert_element_type.24
  30.6 1.7 copy.35
  32.3 1.6 convolution_add_fusion.mod.refs_2_.refs_7_.refs_10_
  34.0 14.5 %project.1 = (bf16[2048,2304]{1,0:T(8,128)(2,1)}, bf16[768,2048]{1,0:T(8,128)(2,1)}) custom-call(s32[2]{0:T(128)} %refs_0_.3, s32[2]{0:T(128)} %refs_1_.7, bf16[2048,768]{1,0:T(8,128)(2,1)} %refs_12_.1, f32[1,768]{1,0:T(1,128)} %reshape.75.emb.refs_5_.refs_8_, f32[1,768]{1,0:T(1,128)} %reshape.76.gn.refs_9_, ...), custom_call_target="tpu_custom_call" | custom-call | flops 7247757312 | bytes 19267584 | tf_op jit(solution)/shard_map/project/pallas_call | solution.py:177
  48.5 44.5 %attend.1 = (bf16[2048,768]{1,0:T(8,128)(2,1)}, f32[2,6,2,1024]{3,2,1,0:T(2,128)}, bf16[768,768]{1,0:T(8,128)(2,1)}, bf16[768,3072]{1,0:T(8,128)(2,1)}, bf16[3072,768]{1,0:T(8,128)(2,1)}) custom-call(bf16[2048,2304]{1,0:T(8,128)(2,1)} %get-tuple-element.69.refs_0_.refs_1_.refs_2_, bf16[2048,2304]{1,0:T(8,128)(2,1)} %get-tuple-element.69.refs_0_.refs_1_.refs_2_, ...), custom_call_target="tpu_custom_call" | custom-call | flops 25769803776 | bytes 12582912 | tf_op jit(solution)/shard_map/attend/pallas_call | solution.py:577
  93.0 0.7 reshape.78.gn.refs_6_
  93.7 8.2 %middle_norm.1.refs_0_ = bf16[2048,768]{1,0:T(8,128)(2,1)} custom-call(s32[2]{0:T(128)} %refs_0_.3, s32[2]{0:T(128)} %refs_1_.7, bf16[2048,768]{1,0:T(8,128)(2,1)} %get-tuple-element.70.mix.refs_2_.refs_3_.refs_13_, bf16[2048,768]{1,0:T(8,128)(2,1)} %refs_12_.1, f32[1,768]{1,0:T(1,128)} %reshape.75.emb.refs_5_.refs_8_, f32[1,768]{1,0:T(1,128)} %reshape.78.gn.refs_6_, ...), custom_call_target="tpu_custom_call" | custom-call | flops 2415919104 | bytes 9437184 | tf_op jit(solution)/shard_map/middle_norm/pallas_call | solution.py:753
  102.5 75.8 %hidden_units.1 = (bf16[2048,3072]{1,0:T(8,128)(2,1)}, bf16[2048,3072]{1,0:T(8,128)(2,1)}, f32[1,3072]{1,0:T(1,128)}, f32[2,768]{1,0:T(2,128)}, f32[2,768]{1,0:T...) custom-call(bf16[2048,768]{1,0:T(8,128)(2,1)} %middle_norm.1.refs_0_, ...), custom_call_target="tpu_custom_call" | custom-call | flops 38654705664 | bytes 62914560 | tf_op jit(solution)/shard_map/hidden_units/pallas_call | solution.py:915
  178.4 41.1 %middle_back.1 = (f32[2048,768]{1,0:T(8,128)}, bf16[2048,768]{1,0:T(8,128)(2,1)}, bf16[4,192,768]{2,1,0:T(8,128)(2,1)}, f32[2,8,768]{2,1,0:T(8,128)}, bf16[256,768]{1,0:T(8,128)(2,1)}) custom-call(s32[2]{0:T(128)} %refs_0_.3, s32[2]{0:T(128)} %refs_1_.7, bf16[2048,768]{1,0:T(8,128)(2,1)} %get-tuple-element.70.mix.refs_2_.refs_3_.refs_13_, ...), custom_call_target="tpu_custom_call" | custom-call | flops 16911433728 | bytes 36175872 | tf_op jit(solution)/shard_map/middle_back/pallas_call | solution.py:1014
  219.5 98.8 %attend_back.1 = (bf16[2048,768]{1,0:T(8,128)(2,1)}, bf16[2048,768]{1,0:T(8,128)(2,1)}, bf16[2048,768]{1,0:T(8,128)(2,1)}, bf16[192,1024]{1,0:T(8,128)(2,1)}, bf...) custom-call(bf16[2048,2304]{1,0:T(8,128)(2,1)} %get-tuple-element.69, ...), custom_call_target="tpu_custom_call" | custom-call | flops 64424509440 | bytes 25165824 | tf_op jit(solution)/shard_map/attend_back/pallas_call | solution.py:704
  319.2 0.7 fusion
  320.7 0.7 stack.63.refs_18_
  321.3 60.5 %finish.1 = (f32[2048,768]{1,0:T(8,128)}, bf16[2048,768]{1,0:T(8,128)(2,1)}, f32[128,1152]{1,0:T(8,128)}, f32[1,1152]{1,0:T(1,128)}, f32[8,256]{1,0:T(8,128)}, /...) custom-call(s32[2]{0:T(128)} %refs_0_.3, ...), custom_call_target="tpu_custom_call" | custom-call | flops 26575110144 | bytes 50331648 | tf_op jit(solution)/shard_map/finish/pallas_call | solution.py:1298
  381.8 0.8 slice.118
  383.3 1.3 reduce
  384.6 5.3 %assemble.1 = (f32[192,3072]{1,0:T(8,128)}, f32[3,256,768]{2,1,0:T(8,128)}, f32[192,768]{1,0:T(8,128)}, f32[192,2304]{1,0:T(8,128)}) custom-call(bf16[192,1024]{1,0:T(8,128)(2,1)} %get-tuple-element.100.refs_0_, bf16[192,1024]{1,0:T(8,128)(2,1)} %get-tuple-element.101.refs_1_, bf16[192,1024]{1,0:T(8,128)(2,1)} %get-tuple-element.102.refs_2_, ...), custom_call_target="tpu_custom_call" | custom-call | bytes 7077888 | tf_op jit(solution)/shard_map/assemble/pallas_call | solution.py:1411
  390.6 1.7 copy.42
  392.3 2.3 copy-done
  394.5 2.7 copy.43
  397.2 0.8 copy.44
  (44 shorter events, 5.0 us)
Async XLA Ops:
  30.6 17.9 %copy-start.9 = (f32[2,128]{1,0:T(2,128)}, f32[2,128]{1,0:T(2,128)S(1)}, u32[]{:S(2)}) copy-start(f32[2,128]{1,0:T(2,128)S(1)} %divide_multiply_fusion.refs_16_) | copy-start | bytes 3076
  219.5 98.9 %copy-start.4 = (f32[4,192]{1,0:T(4,128)S(1)}, f32[4,192]{1,0:T(4,128)}, u32[]{:S(2)}) copy-start(f32[4,192]{1,0:T(4,128)} %get-tuple-element.119) | copy-start | bytes 9220
  219.5 99.5 %copy-start.3 = (f32[2,8,768]{2,1,0:T(8,128)S(1)}, f32[2,8,768]{2,1,0:T(8,128)}, u32[]{:S(2)}) copy-start(f32[2,8,768]{2,1,0:T(8,128)} %get-tuple-element.87) | copy-start | bytes 147460
  219.5 99.7 %copy-start.7 = (f32[2,768]{1,0:T(2,128)S(1)}, f32[2,768]{1,0:T(2,128)}, u32[]{:S(2)}) copy-start(f32[2,768]{1,0:T(2,128)} %get-tuple-element.88) | copy-start | bytes 18436
  219.5 99.7 %copy-start.8 = (f32[2,768]{1,0:T(2,128)S(1)}, f32[2,768]{1,0:T(2,128)}, u32[]{:S(2)}) copy-start(f32[2,768]{1,0:T(2,128)} %get-tuple-element.89) | copy-start | bytes 18436
  219.5 101.1 %copy-start.5 = (f32[1,3072]{1,0:T(1,128)S(1)}, f32[1,3072]{1,0:T(1,128)}, u32[]{:S(2)}) copy-start(f32[1,3072]{1,0:T(1,128)} %get-tuple-element.90) | copy-start | bytes 36868
  381.8 8.2 %copy-start.6 = (f32[8,256]{1,0:T(8,128)S(1)}, f32[8,256]{1,0:T(8,128)}, u32[]{:S(2)}) copy-start(f32[8,256]{1,0:T(8,128)} %get-tuple-element.97) | copy-start | bytes 24580
  381.8 8.8 %copy-start.1 = (bf16[2048,768]{1,0:T(8,128)(2,1)S(1)}, bf16[2048,768]{1,0:T(8,128)(2,1)}, u32[]{:S(2)}) copy-start(bf16[2048,768]{1,0:T(8,128)(2,1)} %get-tuple-element.161) | copy-start | bytes 9437188
  390.6 3.9 copy-start
  394.5 2.7 copy-start.2

commit v4 on v2

--- a/solution.py
+++ b/solution.py
@@ -356,13 +356,14 @@
 
 
 class Exchange(Steps):
-    def __init__(self, shapes, times, columns=None, spans=None):
+    def __init__(self, shapes, times, columns=None, spans=None, near=()):
         columns = columns or [(k, 0, shape[-1]) for k, shape in enumerate(shapes)]
         spans = spans or ["whole"] * len(shapes)
         self.stages = exchange_stages()
         self.arrays, self.columns = [shape[-2:] for shape in shapes], columns
         self.shapes = [(self.arrays[k][0], upper - lower) for k, lower, upper in columns]
         self.spans = [spans[k] for k, _, _ in columns]
+        self.near = [k in near for k, _, _ in columns]
         self.firsts = [2 if span == "tail" else 0 for span in self.spans]
         self.lasts = [1 if span == "head" else len(self.stages) - 1 for span in self.spans]
         self.times = times
@@ -380,11 +381,11 @@
     def scratch(self):
         held = []
         dma = pltpu.SemaphoreType.DMA
-        for (rows, cols), span in zip(self.shapes, self.spans):
+        for (rows, cols), span, near in zip(self.shapes, self.spans, self.near):
             early, late = span != "tail", span != "head"
             held += [
                 pltpu.VMEM((2, rows, cols) if early else (2, 16, PAIR), BF16),
-                pltpu.VMEM((2 if early else 1, rows, cols), BF16),
+                pltpu.VMEM((2, 16, PAIR) if near else (2 if early else 1, rows, cols), BF16),
                 pltpu.VMEM((rows, cols) if early else (16, PAIR), BF16),
                 pltpu.VMEM((len(self.stages) - 3, rows // 2, cols) if late else (1, 16, PAIR), BF16),
                 pltpu.VMEM((rows // 2, cols) if late else (16, PAIR), BF16),
@@ -398,10 +399,10 @@
         self.refs = []
         for part, (k, lower, upper) in enumerate(self.columns):
             every = (slice(None),) * (1 if self.spans[part] == "tail" else 2)
-            self.refs.append(
-                (ins[k].at[every + (slice(lower, upper),)], outs[k].at[:, lower:upper])
-                + tuple(held[8 * part : 8 * part + 8])
-            )
+            source, own = ins[k].at[every + (slice(lower, upper),)], held[8 * part : 8 * part + 8]
+            if self.near[part]:
+                own = [own[0], source.at[2:4]] + list(own[2:])
+            self.refs.append((source, outs[k].at[:, lower:upper], *own))
         self.locate()
 
     def own(self, k):
@@ -438,7 +439,8 @@
         return pltpu.make_async_copy(mine, out.at[half, :], near.at[1])
 
     def begin(self, k):
-        self.load(k).start()
+        if not self.near[k]:
+            self.load(k).start()
         if self.spans[k] != "tail":
             self.remote(k, 0).start()
 
@@ -451,16 +453,16 @@
         kind = self.stages[step][0]
         self.remote(k, step).wait()
         if kind == "pair":
-            self.load(k).wait()
-            kept[...] = (kept[...].astype(F32) + pair[...].astype(F32)).astype(BF16)
+            if not self.near[k]:
+                self.load(k).wait()
+            kept[...] = kept[...] + pair[...]
         elif kind == "chip":
-            kept[1] = (kept[1].astype(F32) + chip[...].astype(F32)).astype(BF16)
+            kept[1] = kept[1] + chip[...]
         elif kind == "split":
             half = self.half_of(self.shapes[k][0], 0)
-            own = self.own(k)[half, :].astype(F32)
-            mine[...] = (own + halves[0].astype(F32)).astype(BF16)
+            mine[...] = self.own(k)[half, :] + halves[0]
         elif kind == "full":
-            mine[...] = (mine[...].astype(F32) + halves[step - 2].astype(F32)).astype(BF16)
+            mine[...] = mine[...] + halves[step - 2]
         if step < self.lasts[k]:
             self.remote(k, step + 1).start()
         if step == max(self.lasts[k] - 1, 1):
@@ -605,6 +607,7 @@
         times,
         list(columns) + [(len(pieces) + part, 0, wide) for part in range(3)],
         list(spans) + ["whole"] * 3,
+        [len(pieces) + part for part in range(3)],
     )
     many, outs = len(pieces), len(traded)
     assert steps == 2
@@ -717,38 +720,6 @@
     )(qkv, qkv, qkv, mixture, d_mixture, total, *tables, turned, *pieces)
 
 
-def middle_norm(mixture, tokens, starts, lengths, embed, gain, modulation, weight, seqs, block=512):
-    rows, width = tokens.shape
-    seq_length = rows // seqs
-    block = min(block, seq_length)
-    per_seq = seq_length // block
-
-    def kernel(starts, lengths, mix, tok, emb, gn, mod, w, out):
-        step = pl.program_id(0)
-        seq = step // per_seq
-        first = (step - seq * per_seq) * block
-        start, _ = masked_rows(tok[...], emb[...], starts[seq], lengths[seq], first)
-        middle = start + mod[pl.ds(seq, 1), 2 * width : 3 * width] * mxu(mix[...], w[...])
-        hat, _ = normalized(middle)
-        shift = mod[pl.ds(seq, 1), 3 * width : 4 * width]
-        scale = mod[pl.ds(seq, 1), 4 * width : 5 * width]
-        out[...] = (hat * (gn[...] * (1.0 + scale)) + shift).astype(BF16)
-
-    row = pl.BlockSpec((block, width), lambda i: (i, 0))
-    return call(
-        kernel,
-        "middle_norm",
-        (rows // block,),
-        [smem(), smem(), row, row, whole((1, width)), whole((1, width)), whole(modulation.shape)]
-        + [whole(weight.shape)],
-        row,
-        jax.ShapeDtypeStruct((rows, width), BF16),
-        [],
-        2 * rows * width * width,
-        rows * width * 6,
-    )(starts, lengths, mixture, tokens, embed, gain, modulation, weight)
-
-
 def gelu_pair(v):
     root = math.sqrt(2.0 / math.pi)
     square = v * v
@@ -778,8 +749,11 @@
     ]
 
 
-def hidden_units(normed, cot, modulation, up, up_bias, down, times, ident, seqs, block=512):
-    rows, width = normed.shape
+def hidden_units(
+    mixture, tokens, cot, starts, lengths, embed, gain, modulation, out_weight, up, up_bias, down,
+    times, ident, seqs, block=512,
+):
+    rows, width = tokens.shape
     ways = lax.axis_size("narrow")
     units = up.shape[1] // GROUPS
     share, part_units = width // ways, units // ways
@@ -791,17 +765,17 @@
     shape_up, shape_down = (ways, share, units), (ways, part_units, width)
     traded = [jax.ShapeDtypeStruct(v, BF16) for v in (shape_up, shape_down) * 2]
     exchange = Exchange(
-        [v.shape for v in traded], times, halved(traded), ["whole"] * 2 + ["head"] * 2
+        [v.shape for v in traded], times, halved(traded), ["whole"] * 2 + ["head"] * 2, range(4)
     )
 
     def kernel(*refs):
-        nrm, g, mod, b_up = refs[:4]
-        w_ups, w_downs = refs[4 : 4 + ways], refs[4 + ways : 4 + 2 * ways]
-        act, d_up, g_bias, d_gate, g_sum = refs[4 + 2 * ways : 9 + 2 * ways]
-        outs, left = refs[9 + 2 * ways : 15 + 2 * ways], refs[15 + 2 * ways :]
-        n_turned, g_turned, a_held, u_held, down_held, g_up, g_down, near = left[:8]
+        starts, lengths, mix, tok, emb, gn, w_out, g, mod, b_up = refs[:10]
+        w_ups, w_downs = refs[10 : 10 + ways], refs[10 + ways : 10 + 2 * ways]
+        act, d_up, g_bias, d_gate, g_sum = refs[10 + 2 * ways : 15 + 2 * ways]
+        outs, left = refs[15 + 2 * ways : 21 + 2 * ways], refs[21 + 2 * ways :]
+        n_turned, g_turned, a_held, u_held, down_held, g_up, g_down, near, n_held = left[:9]
         exchange.bind(
-            [g_up.at[0], g_down.at[0], g_up.at[1], g_down.at[1]], outs[:4], left[8:]
+            [g_up.at[0], g_down.at[0], g_up.at[1], g_down.at[1]], outs[:4], left[9:]
         )
         step = pl.program_id(0)
         group = step // turn
@@ -823,14 +797,30 @@
 
         part = pl.ds(pl.multiple_of(jnp.minimum(at, steps - 1) * block, block), block)
 
+        @pl.when(step < steps)
+        def _():
+            seq = at // per_seq
+            first = (at - seq * per_seq) * block
+            start, _ = masked_rows(tok[...], emb[...], starts[seq], lengths[seq], first)
+            gate = mod[pl.ds(seq, 1), 2 * width : 3 * width]
+            hat, _ = normalized(start + gate * mxu(mix[...], w_out[...]))
+            shift = mod[pl.ds(seq, 1), 3 * width : 4 * width]
+            scale = mod[pl.ds(seq, 1), 4 * width : 5 * width]
+            normed = (hat * (gn[...] * (1.0 + scale)) + shift).astype(BF16)
+            n_held[part, :] = normed
+            store_shares(n_turned, jnp.transpose(normed), part)
+            g_turned[:, part] = jnp.transpose(g[...])
+            g_sum[pl.ds(seq, 1), :] += column_sum(g[...].astype(F32))
+
         @pl.when(at < steps)
         def _():
             seq = at // per_seq
+            nrm = n_held[part, :]
             cotangent = g[...].astype(F32)
             d_branch = (mod[pl.ds(seq, 1), 5 * width : 6 * width] * cotangent).astype(BF16)
             for way in range(ways):
                 cols = slice(way * part_units, (way + 1) * part_units)
-                upper = mxu(nrm[...], w_ups[way][...]) + b_up[:, cols]
+                upper = mxu(nrm, w_ups[way][...]) + b_up[:, cols]
                 d_active = mxu(d_branch, w_downs[way][...], TRANSPOSED)
                 active, slope = gelu_pair(upper)
                 active = active.astype(BF16)
@@ -839,12 +829,6 @@
                 a_held[part, cols] = active
                 d_up[:, cols] = d_upper
                 u_held[part, cols] = d_upper
-
-        @pl.when(step < steps)
-        def _():
-            store_shares(n_turned, jnp.transpose(nrm[...]), part)
-            g_turned[:, part] = jnp.transpose(g[...])
-            g_sum[pl.ds(at // per_seq, 1), :] += column_sum(g[...].astype(F32))
 
         @pl.when(at >= steps)
         def _():
@@ -881,6 +865,9 @@
     def early(i):
         return (jnp.minimum(lax.rem(i, turn), steps - 1), 0)
 
+    def once(i):
+        return (jnp.minimum(i, steps - 1), 0)
+
     def fixed(shape):
         return pl.BlockSpec(shape, lambda i: (0,) * len(shape))
 
@@ -901,7 +888,10 @@
         kernel,
         "hidden_units",
         (GROUPS * turn,),
-        [pl.BlockSpec((block, width), early)] * 2
+        [smem(), smem()]
+        + [pl.BlockSpec((block, width), once)] * 2
+        + [whole((1, width)), whole((1, width)), whole(out_weight.shape)]
+        + [pl.BlockSpec((block, width), early)]
         + [whole(modulation.shape), by_group]
         + [up_piece(way) for way in range(ways)]
         + [down_piece(way) for way in range(ways)],
@@ -926,13 +916,17 @@
             pltpu.VMEM((GROUPS,) + shape_up, BF16),
             pltpu.VMEM((GROUPS,) + shape_down, BF16),
             pltpu.SemaphoreType.DMA((2,)),
+            pltpu.VMEM((rows, width), BF16),
         ]
         + exchange.scratch(),
         8 * rows * width * units * GROUPS,
         GROUPS * (rows * (width * 4 + units * 4) + 8 * width * units),
         rows * units * GROUPS,
         ident,
-    )(normed, cot, modulation, up_bias, *[up] * ways, *[down] * ways)
+    )(
+        starts, lengths, mixture, tokens, embed, gain, out_weight, cot, modulation, up_bias,
+        *[up] * ways, *[down] * ways,
+    )
 
 
 def middle_back(
@@ -1120,7 +1114,7 @@
     lanes = columns + time_width + window
     early, middle, late = 3, rows // block, rows // late_block
     steps = early + middle + late
-    exchange = Exchange([(ways, share, wide)] * 3, times)
+    exchange = Exchange([(ways, share, wide)] * 3, times, near=range(3))
     finale = Finale(ways)
 
     def kernel(*refs):
@@ -1470,13 +1464,11 @@
         1,
         seqs,
     )
-    normed_two = middle_norm(
-        mixture, tokens, span_start, span_length, embed, gain_two, modulation, w_out, seqs
-    )
     bias_up = jnp.swapaxes(bias_up.reshape(ways, GROUPS, part), 0, 1).reshape(1, -1)
     head_times = paced([8, 9, 10, 11], [1, 5, 2, 2, 2, 1]) + paced([17, 17, 18, 19], [1, 4])
     active, d_upper, g_bias, d_gate_two, g_sum, *swaps = hidden_units(
-        normed_two, cotangent, modulation, w_up, bias_up, w_down, head_times, 2, seqs
+        mixture, tokens, cotangent, span_start, span_length, embed, gain_two, modulation, w_out,
+        w_up, bias_up, w_down, head_times, 2, seqs,
     )
     d_gate_two += bias_down * g_sum
     d_middle, d_mixture, g_out, sums_two = middle_back(

time: 395 us -> 385 us (0.975); the launches traced: 389 us -> 384 us
  Pallas kernels: 364 us -> 360 us
    pallas_call x2 -> x1, Pallas kernels: 88 us -> 85 us  [hidden_units(): call(kernel, 'hidden_units', (GROUPS * turn,), [smem(), smem()] + [pl.Blo...]
where the time goes in v4:
time: 385 us; the launch traced here: 384 us
  Pallas kernels  360 us (94%)
  local copies, waits for them, and re-layouts  16.9 us (4%)
  other arithmetic  5 us (1%)
    pallas_call x1, Pallas kernels, attend_back(): call(kernel, 'attend_back', (steps, seqs), [part_of(0), part_of(1), part_...  103 us
    pallas_call x1, Pallas kernels, hidden_units(): call(kernel, 'hidden_units', (GROUPS * turn,), [smem(), smem()] + [pl.Blo...  85 us
    pallas_call x1, Pallas kernels, finish(): call(kernel, 'finish', (steps,), [smem(), smem(), whole(turned.shape)] +...  51 us
    pallas_call x1, Pallas kernels, attend(): call(kernel, 'attend', (seqs, steps), [part_of(0), part_of(1), part_of(2)...  44.5 us
    pallas_call x1, Pallas kernels, middle_back(): call(kernel, 'middle_back', (steps,), [smem(), smem(), row, row, row, who...  31.9 us
    pallas_call x1, Pallas kernels, gather_first(): call(kernel, 'gather_first', (), gathering.in_specs(), gathering.out_spec...  24.8 us
    pallas_call x1, Pallas kernels, project(): call(kernel, 'project', (rows // block,), [smem(), smem(), pl.BlockSpec((...  14.5 us

profile of v4, /device:TPU:0, one launch (start us, length us, event | category | flops | bytes accessed | tf_op | source)
XLA Modules:
  0.0 384.2 jit_solution(721312946625803145)
XLA Ops:
  0.6 1.4 add_bitcast_fusion.refs_0_
  2.1 24.8 %gather_first.1 = (bf16[128,128]{1,0:T(8,128)(2,1)}, bf16[512,1152]{1,0:T(8,128)(2,1)}, bf16[768,2304]{1,0:T(8,128)(2,1)}) custom-call(bf16[32,128]{1,0:T(8,128)(2,1)} %add_bitcast_fusion.refs_0_, bf16[128,1152]{1,0:T(8,128)(2,1)} %refs_1_.3, bf16[192,2304]{1,0:T(8,128)(2,1)} %refs_2_.1), custom_call_target="tpu_custom_call" | custom-call | bytes 3538944 | tf_op jit(solution)/shard_map/gather_first/pallas_call | solution.py:1326
  27.0 0.8 reshape.83
  27.7 0.7 fusion.4
  29.7 0.7 convert_element_type.24
  30.6 1.7 copy.35
  32.3 1.6 convolution_add_fusion.mod.refs_8_.refs_10_
  34.0 14.5 %project.1 = (bf16[2048,2304]{1,0:T(8,128)(2,1)}, bf16[768,2048]{1,0:T(8,128)(2,1)}) custom-call(s32[2]{0:T(128)} %refs_0_.3, s32[2]{0:T(128)} %refs_1_.5, bf16[2048,768]{1,0:T(8,128)(2,1)} %refs_12_.1, f32[1,768]{1,0:T(1,128)} %reshape.75.emb.refs_4_.refs_8_, f32[1,768]{1,0:T(1,128)} %reshape.76.gn.refs_9_, ...), custom_call_target="tpu_custom_call" | custom-call | flops 7247757312 | bytes 19267584 | tf_op jit(solution)/shard_map/project/pallas_call | solution.py:163
  48.5 44.5 %attend.1 = (bf16[2048,768]{1,0:T(8,128)(2,1)}, f32[2,6,2,1024]{3,2,1,0:T(2,128)}, bf16[768,768]{1,0:T(8,128)(2,1)}, bf16[768,3072]{1,0:T(8,128)(2,1)}, bf16[3072,768]{1,0:T(8,128)(2,1)}) custom-call(bf16[2048,2304]{1,0:T(8,128)(2,1)} %get-tuple-element.65.refs_0_.refs_1_.refs_2_, bf16[2048,2304]{1,0:T(8,128)(2,1)} %get-tuple-element.65.refs_0_.refs_1_.refs_2_, ...), custom_call_target="tpu_custom_call" | custom-call | flops 25769803776 | bytes 12582912 | tf_op jit(solution)/shard_map/attend/pallas_call | solution.py:564
  93.1 0.7 reshape.78.refs_5_.gn
  94.3 85.0 %hidden_units.1 = (bf16[2048,3072]{1,0:T(8,128)(2,1)}, bf16[2048,3072]{1,0:T(8,128)(2,1)}, f32[1,3072]{1,0:T(1,128)}, f32[2,768]{1,0:T(2,128)}, f32[2,768]{1,0:T...) custom-call(s32[2]{0:T(128)} %refs_0_.3, ...), custom_call_target="tpu_custom_call" | custom-call | flops 38654705664 | bytes 62914560 | tf_op jit(solution)/shard_map/hidden_units/pallas_call | solution.py:887
  179.4 31.9 %middle_back.1 = (f32[2048,768]{1,0:T(8,128)}, bf16[2048,768]{1,0:T(8,128)(2,1)}, bf16[4,192,768]{2,1,0:T(8,128)(2,1)}, f32[2,8,768]{2,1,0:T(8,128)}) custom-call(s32[2]{0:T(128)} %refs_0_.3, s32[2]{0:T(128)} %refs_1_.5, bf16[2048,768]{1,0:T(8,128)(2,1)} %get-tuple-element.66.refs_2_.mix.refs_3_.refs_13_, bf16[2048,768]{1,0:T(8,128)(2,1)} %refs_12_.1, ...), custom_call_target="tpu_custom_call" | custom-call | flops 16911433728 | bytes 36175872 | tf_op jit(solution)/shard_map/middle_back/pallas_call | solution.py:987
  211.4 102.6 %attend_back.1 = (bf16[2048,768]{1,0:T(8,128)(2,1)}, bf16[2048,768]{1,0:T(8,128)(2,1)}, bf16[2048,768]{1,0:T(8,128)(2,1)}, bf16[192,1024]{1,0:T(8,128)(2,1)}, bf...) custom-call(bf16[2048,2304]{1,0:T(8,128)(2,1)} %get-tuple-element.65, ...), custom_call_target="tpu_custom_call" | custom-call | flops 64424509440 | bytes 25165824 | tf_op jit(solution)/shard_map/attend_back/pallas_call | solution.py:692
  314.0 0.7 reshape.80.refs_15_
  314.8 0.7 fusion
  316.3 0.7 stack.63.refs_18_
  317.0 51.0 %finish.1 = (f32[2048,768]{1,0:T(8,128)}, bf16[2048,768]{1,0:T(8,128)(2,1)}, f32[128,1152]{1,0:T(8,128)}, f32[1,1152]{1,0:T(1,128)}, f32[8,256]{1,0:T(8,128)}, /...) custom-call(s32[2]{0:T(128)} %refs_0_.3, s32[2]{0:T(128)} %refs_1_.5, ...), custom_call_target="tpu_custom_call" | custom-call | flops 26575110144 | bytes 50331648 | tf_op jit(solution)/shard_map/finish/pallas_call | solution.py:1257
  368.0 0.8 slice.118
  369.5 1.3 reduce
  370.8 5.3 %assemble.1 = (f32[192,3072]{1,0:T(8,128)}, f32[3,256,768]{2,1,0:T(8,128)}, f32[192,768]{1,0:T(8,128)}, f32[192,2304]{1,0:T(8,128)}) custom-call(bf16[192,1024]{1,0:T(8,128)(2,1)} %get-tuple-element.92.refs_0_, bf16[192,1024]{1,0:T(8,128)(2,1)} %get-tuple-element.93.refs_1_, bf16[192,1024]{1,0:T(8,128)(2,1)} %get-tuple-element.94.refs_2_, ...), custom_call_target="tpu_custom_call" | custom-call | bytes 7077888 | tf_op jit(solution)/shard_map/assemble/pallas_call | solution.py:1369
  376.7 1.7 copy.42
  378.4 2.3 copy-done
  380.7 2.7 copy.43
  383.4 0.8 copy.44
  (43 shorter events, 4.3 us)
Async XLA Ops:
  30.6 17.9 %copy-start.9 = (f32[2,128]{1,0:T(2,128)}, f32[2,128]{1,0:T(2,128)S(1)}, u32[]{:S(2)}) copy-start(f32[2,128]{1,0:T(2,128)S(1)} %divide_multiply_fusion.refs_16_) | copy-start | bytes 3076
  211.3 102.6 %copy-start.4 = (f32[4,192]{1,0:T(4,128)S(1)}, f32[4,192]{1,0:T(4,128)}, u32[]{:S(2)}) copy-start(f32[4,192]{1,0:T(4,128)} %get-tuple-element.111) | copy-start | bytes 9220
  211.3 103.3 %copy-start.3 = (f32[2,8,768]{2,1,0:T(8,128)S(1)}, f32[2,8,768]{2,1,0:T(8,128)}, u32[]{:S(2)}) copy-start(f32[2,8,768]{2,1,0:T(8,128)} %get-tuple-element.82) | copy-start | bytes 147460
  211.4 103.5 %copy-start.7 = (f32[2,768]{1,0:T(2,128)S(1)}, f32[2,768]{1,0:T(2,128)}, u32[]{:S(2)}) copy-start(f32[2,768]{1,0:T(2,128)} %get-tuple-element.83) | copy-start | bytes 18436
  211.4 103.5 %copy-start.8 = (f32[2,768]{1,0:T(2,128)S(1)}, f32[2,768]{1,0:T(2,128)}, u32[]{:S(2)}) copy-start(f32[2,768]{1,0:T(2,128)} %get-tuple-element.84) | copy-start | bytes 18436
  211.4 104.9 %copy-start.5 = (f32[1,3072]{1,0:T(1,128)S(1)}, f32[1,3072]{1,0:T(1,128)}, u32[]{:S(2)}) copy-start(f32[1,3072]{1,0:T(1,128)} %get-tuple-element.85) | copy-start | bytes 36868
  367.9 8.2 %copy-start.6 = (f32[8,256]{1,0:T(8,128)S(1)}, f32[8,256]{1,0:T(8,128)}, u32[]{:S(2)}) copy-start(f32[8,256]{1,0:T(8,128)} %get-tuple-element.89) | copy-start | bytes 24580
  367.9 8.8 %copy-start.1 = (bf16[2048,768]{1,0:T(8,128)(2,1)S(1)}, bf16[2048,768]{1,0:T(8,128)(2,1)}, u32[]{:S(2)}) copy-start(bf16[2048,768]{1,0:T(8,128)(2,1)} %get-tuple-element.153) | copy-start | bytes 9437188
  376.7 3.9 %copy-start = (f32[2048,768]{1,0:T(8,128)S(1)}, f32[2048,768]{1,0:T(8,128)}, u32[]{:S(2)}) copy-start(f32[2048,768]{1,0:T(8,128)} %get-tuple-element.154) | copy-start | bytes 18874372
  380.7 2.7 copy-start.2

commit v5 on v4

--- a/solution.py
+++ b/solution.py
@@ -11,6 +11,7 @@
 HEAD = 64
 PAIR = 2 * HEAD
 GROUPS = 3
+EMBED, GAIN_ONE, GAIN_TWO, BIAS_DOWN, BIAS_UP = range(5)
 FINISH_TIMES = [
     [1, 3, 5, 6, 7, 10, 12], [2, 4, 6, 7, 9, 12, 14], [3, 4, 7, 9, 11, 14, 15],
 ]
@@ -55,6 +56,10 @@
     return pl.BlockSpec((width, width), lambda *_: (0, which), pipeline_mode=pl.Buffered(1))
 
 
+def row_of(ref, which, width):
+    return ref.at[which : which + 1, 0:width]
+
+
 def smem():
     return pl.BlockSpec(memory_space=pltpu.SMEM)
 
@@ -141,6 +146,7 @@
     pairs = width // PAIR
 
     def kernel(starts, lengths, tok, emb, gn, mod, w_q, w_k, w_v, cos, sin, out, nt):
+        emb, gn = row_of(emb, EMBED, width), row_of(gn, GAIN_ONE, width)
         step = pl.program_id(0)
         seq = step // per_seq
         first = (step - seq * per_seq) * block
@@ -168,8 +174,8 @@
             smem(),
             smem(),
             pl.BlockSpec((block, width), lambda i: (i, 0)),
-            whole((1, width)),
-            whole((1, width)),
+            whole(embed.shape),
+            whole(gain.shape),
             whole(modulation.shape),
             column_third(0, width),
             column_third(1, width),
@@ -265,12 +271,13 @@
 class Gather(Steps):
     partners = (("narrow", 1), ("narrow", 2), ("wide", 1))
 
-    def __init__(self, shapes, begins, waits, columns=None):
+    def __init__(self, shapes, begins, waits, columns=None, sideways=()):
         columns = columns or [(k, 0, shape[1]) for k, shape in enumerate(shapes)]
         self.arrays, self.columns = shapes, columns
         self.shapes = [(shapes[k][0], upper - lower) for k, lower, upper in columns]
         self.begins, self.waits = begins, waits
         self.count = len(columns)
+        self.sideways = sideways
 
     def in_specs(self):
         return [pl.BlockSpec(memory_space=pl.ANY)] * len(self.arrays)
@@ -278,7 +285,10 @@
     out_specs = in_specs
 
     def out_shape(self):
-        return [jax.ShapeDtypeStruct((4 * rows, cols), BF16) for rows, cols in self.arrays]
+        return [
+            jax.ShapeDtypeStruct((rows, 4 * cols) if k in self.sideways else (4 * rows, cols), BF16)
+            for k, (rows, cols) in enumerate(self.arrays)
+        ]
 
     def scratch(self):
         dma, held = pltpu.SemaphoreType.DMA, []
@@ -288,30 +298,36 @@
 
     def bind(self, ins, outs, held):
         self.refs = [
-            (ins[k].at[:, lower:upper], outs[k].at[:, lower:upper])
+            (
+                ins[k].at[:, lower:upper],
+                outs[k] if k in self.sideways else outs[k].at[:, lower:upper],
+            )
             + tuple(held[4 * part : 4 * part + 4])
             for part, (k, lower, upper) in enumerate(self.columns)
         ]
         self.locate()
 
     def block(self, k, index, which=None):
-        rows = self.shapes[k][0]
+        rows, cols = self.shapes[k]
+        if self.columns[k][0] in self.sideways:
+            down = slice(None) if which is None else self.half_of(rows, which)
+            return down, pl.ds(pl.multiple_of(index * cols, cols), cols)
         if which is None:
-            return pl.ds(pl.multiple_of(index * rows, rows), rows)
-        return self.half_of(rows, which, index * rows)
+            return pl.ds(pl.multiple_of(index * rows, rows), rows), slice(None)
+        return self.half_of(rows, which, index * rows), slice(None)
 
     def remote(self, k, step):
         source, out, sent, got, _, _ = self.refs[k]
         me, across = self.at["narrow"], flip(self.at["narrow"], 2)
         axis, stride = (("narrow", 1), ("narrow", 2), ("wide", 1), ("narrow", 1), ("narrow", 1))[step]
         if step == 0:
-            ends = (source, out.at[self.block(k, me), :])
+            ends = (source, out.at[self.block(k, me)])
         elif step == 1:
             half = self.half_of(self.shapes[k][0], 0)
-            ends = (source.at[half, :], out.at[self.block(k, me, 0), :])
+            ends = (source.at[half, :], out.at[self.block(k, me, 0)])
         else:
             spot = self.block(k, across, 1 if step == 4 else 0)
-            ends = (out.at[spot, :], out.at[spot, :])
+            ends = (out.at[spot], out.at[spot])
         return self.push(*ends, sent.at[step], got.at[step], axis, stride)
 
     def local(self, k, which):
@@ -319,7 +335,7 @@
         if which == 0:
             return pltpu.make_async_copy(source, kept, near.at[0])
         return pltpu.make_async_copy(
-            kept, out.at[self.block(k, self.at["narrow"]), :], near.at[1]
+            kept, out.at[self.block(k, self.at["narrow"])], near.at[1]
         )
 
     def begin(self, k):
@@ -770,6 +786,7 @@
 
     def kernel(*refs):
         starts, lengths, mix, tok, emb, gn, w_out, g, mod, b_up = refs[:10]
+        emb, gn = row_of(emb, EMBED, width), row_of(gn, GAIN_TWO, width)
         w_ups, w_downs = refs[10 : 10 + ways], refs[10 + ways : 10 + 2 * ways]
         act, d_up, g_bias, d_gate, g_sum = refs[10 + 2 * ways : 15 + 2 * ways]
         outs, left = refs[15 + 2 * ways : 21 + 2 * ways], refs[21 + 2 * ways :]
@@ -820,7 +837,7 @@
             d_branch = (mod[pl.ds(seq, 1), 5 * width : 6 * width] * cotangent).astype(BF16)
             for way in range(ways):
                 cols = slice(way * part_units, (way + 1) * part_units)
-                upper = mxu(nrm, w_ups[way][...]) + b_up[:, cols]
+                upper = mxu(nrm, w_ups[way][...]) + b_up[pl.ds(BIAS_UP + group, 1), cols]
                 d_active = mxu(d_branch, w_downs[way][...], TRANSPOSED)
                 active, slope = gelu_pair(upper)
                 active = active.astype(BF16)
@@ -890,9 +907,9 @@
         (GROUPS * turn,),
         [smem(), smem()]
         + [pl.BlockSpec((block, width), once)] * 2
-        + [whole((1, width)), whole((1, width)), whole(out_weight.shape)]
+        + [whole(embed.shape), whole(gain.shape), whole(out_weight.shape)]
         + [pl.BlockSpec((block, width), early)]
-        + [whole(modulation.shape), by_group]
+        + [whole(modulation.shape), whole(up_bias.shape)]
         + [up_piece(way) for way in range(ways)]
         + [down_piece(way) for way in range(ways)],
         [by_rows, by_rows, by_group, fixed((seqs, width)), fixed((seqs, width))]
@@ -946,6 +963,7 @@
         starts, lengths, mix, tok, g, emb, gn, mod, w_out, w_up, d_ups, d_middle_out, d_mix, g_out,
         sums, g_sum,
     ):
+        emb, gn = row_of(emb, EMBED, width), row_of(gn, GAIN_TWO, width)
         step = pl.program_id(0)
         seq = step // per_seq
         first = (step - seq * per_seq) * block
@@ -988,7 +1006,7 @@
         kernel,
         "middle_back",
         (steps,),
-        [smem(), smem(), row, row, row, whole((1, width)), whole((1, width))]
+        [smem(), smem(), row, row, row, whole(embed.shape), whole(gain.shape)]
         + [whole(modulation.shape), whole(out_weight.shape), whole(up.shape)]
         + [pl.BlockSpec((block, hidden_width), lambda i: (i, 0))],
         (
@@ -1122,6 +1140,8 @@
             starts, lengths, left, q_all, k_all, v_all, tok, d_mid, emb, gn, mod, w_qkv_all,
             tok_late, mix, w_out_all, b_down, feat, two, vec, act, w_down_all,
         ) = refs[:21]
+        emb, gn = row_of(emb, EMBED, width), row_of(gn, GAIN_ONE, width)
+        b_down = row_of(b_down, BIAS_DOWN, width)
         spot = 21
         g_tok, block_out, g_ada, g_ada_bias, g_vec = refs[spot : spot + 5]
         outs = refs[spot + 5 : spot + 8]
@@ -1260,8 +1280,8 @@
         (steps,),
         [smem(), smem(), whole(turned.shape)]
         + [anywhere] * 3
-        + [row, row, whole((1, width)), whole((1, width)), whole(modulation.shape), anywhere]
-        + [late_row(width), late_row(width), anywhere, whole((1, width))]
+        + [row, row, whole(embed.shape), whole(gain.shape), whole(modulation.shape), anywhere]
+        + [late_row(width), late_row(width), anywhere, whole(down_bias.shape)]
         + [whole(features.shape), whole(rows_two.shape), whole(vectors_two.shape)]
         + [late_row(hidden_width), anywhere],
         [
@@ -1305,7 +1325,9 @@
     width = wide // 3
     columns = [(0, 0, small.shape[1]), (1, 0, ada.shape[1])]
     columns += [(2, k * width, (k + 1) * width) for k in range(3)]
-    gathering = Gather([small.shape, ada.shape, weight.shape], [0] * 5, [0] * 3, columns)
+    gathering = Gather(
+        [small.shape, ada.shape, weight.shape], [0] * 5, [0] * 3, columns, (0, 1)
+    )
 
     def kernel(*refs):
         gathering.bind(refs[0:3], refs[3:6], refs[6:])
@@ -1422,33 +1444,27 @@
     units = ways * part
     time_width, columns = ada_weight.shape
 
-    vectors = (
-        ada_bias, mask_embed, norm_first, norm_second, down_projection_bias, up_projection_bias,
-    )
-    filled, lower = jnp.zeros((32 * PAIR,), BF16), 0
-    for v in vectors:
-        filled += jnp.pad(v, (lower, filled.shape[0] - lower - v.shape[0]))
-        lower += v.shape[0]
-    small = filled.reshape(32, PAIR)
+    spot = jnp.arange(32 * columns)
+    lane = lax.rem(spot, columns)
+    owner = jnp.where(spot < (BIAS_UP + 1) * columns, lane // share, lane // part)
+    vectors = [mask_embed, norm_first, norm_second, down_projection_bias]
+    vectors += [up_projection_bias[group * part : (group + 1) * part] for group in range(GROUPS)]
+    small = jnp.zeros((32 * columns,), BF16)
+    for row, v in enumerate(vectors):
+        for way in range(ways):
+            lower = (row + 1) * columns + way * v.shape[0]
+            small += jnp.pad(v, (lower, small.shape[0] - lower - v.shape[0]))
+    small = jnp.where(owner == me, small, jnp.zeros_like(small))
+    small += jnp.pad(ada_bias, (0, small.shape[0] - columns))
+    small = small.reshape(32, columns)
     small, ada, w_qkv = gather_first(small, ada_weight, query_key_value_weight, 0)
-
-    small = small.reshape(ways, -1).astype(F32)
-    smalls, lower = [], 0
-    for v in vectors:
-        smalls.append(small[:, lower : lower + v.shape[0]].reshape(1, -1))
-        lower += v.shape[0]
-    bias_ada, embed, gain_one, gain_two, bias_down, bias_up = smalls
+    vectors = jnp.sum(small[1:9].astype(F32).reshape(8, ways, columns), axis=1)
     features = time_features(timestep, time_width)
-    modulation = jnp.einsum(
-        "sf,wfc->swc",
-        features,
-        ada.reshape(ways, time_width, columns).astype(F32),
-        precision=FULL_PRECISION,
-    ).reshape(seqs, -1) + bias_ada
+    modulation = jnp.dot(features, ada.astype(F32), precision=FULL_PRECISION) + small[0:1].astype(F32)
     tables = rotary_tables(seq_length)
 
     qkv, turned_one = project(
-        tokens, span_start, span_length, embed, gain_one, modulation, w_qkv, tables, seqs
+        tokens, span_start, span_length, vectors, vectors, modulation, w_qkv, tables, seqs
     )
     thirds = [
         (which, third * size, (third + 1) * size)
@@ -1464,15 +1480,15 @@
         1,
         seqs,
     )
-    bias_up = jnp.swapaxes(bias_up.reshape(ways, GROUPS, part), 0, 1).reshape(1, -1)
+    gain_two, bias_down = [vectors[row : row + 1, :width] for row in (GAIN_TWO, BIAS_DOWN)]
     head_times = paced([8, 9, 10, 11], [1, 5, 2, 2, 2, 1]) + paced([17, 17, 18, 19], [1, 4])
     active, d_upper, g_bias, d_gate_two, g_sum, *swaps = hidden_units(
-        mixture, tokens, cotangent, span_start, span_length, embed, gain_two, modulation, w_out,
-        w_up, bias_up, w_down, head_times, 2, seqs,
+        mixture, tokens, cotangent, span_start, span_length, vectors, vectors, modulation, w_out,
+        w_up, vectors, w_down, head_times, 2, seqs,
     )
     d_gate_two += bias_down * g_sum
     d_middle, d_mixture, g_out, sums_two = middle_back(
-        mixture, tokens, cotangent, span_start, span_length, embed, gain_two, modulation, w_out,
+        mixture, tokens, cotangent, span_start, span_length, vectors, vectors, modulation, w_out,
         d_upper, w_up, seqs,
     )
     d_q, d_k, d_v, *done = attend_back(
@@ -1500,14 +1516,14 @@
         + [jnp.zeros((ways, 2 * PAIR), F32)],
         axis=1,
     )
-    grad_tokens, block_out, grad_ada_weight, grad_ada_bias, vectors, *g_qkv = finish(
-        turned_one, (d_q, d_k, d_v), tokens, d_middle, mixture, span_start, span_length, embed,
-        gain_one, modulation, w_qkv, w_out, bias_down, active, w_down, features, rows_two,
+    grad_tokens, block_out, grad_ada_weight, grad_ada_bias, gathered, *g_qkv = finish(
+        turned_one, (d_q, d_k, d_v), tokens, d_middle, mixture, span_start, span_length, vectors,
+        vectors, modulation, w_qkv, w_out, vectors, active, w_down, features, rows_two,
         vectors_two,
         FINISH_TIMES, 4, seqs,
     )
     skip = lax.rem(share * me, PAIR)
-    own = lax.dynamic_slice_in_dim(vectors[:4], skip, share, 1)
+    own = lax.dynamic_slice_in_dim(gathered[:4], skip, share, 1)
     g_ups, g_downs = (swaps[0], *done[0:4:2]), (swaps[1], *done[1:4:2])
     g_up, g_down, g_out, g_qkv = assemble(g_ups, g_downs, done[4], done[5:] + g_qkv)
     return (
@@ -1521,7 +1537,7 @@
         g_out,
         own[2],
         g_up,
-        vectors[4 : 4 + GROUPS].reshape(-1),
+        gathered[4 : 4 + GROUPS].reshape(-1),
         g_down,
         own[3],
     )

time: 385 us -> 384 us (level)
    reshape x7 -> x2, local copies, waits for them, and re-layouts: 5.57 us -> 1.35 us  [the longest x1 0.75 us: per_device(): small = small.reshape(32, columns)]
where the time goes in v5:
time: 384 us; the launch traced here: 383 us
  Pallas kernels  360 us (94%)
  local copies, waits for them, and re-layouts  13.6 us (4%)
  other arithmetic  6.07 us (2%)
    pallas_call x1, Pallas kernels, attend_back(): call(kernel, 'attend_back', (steps, seqs), [part_of(0), part_of(1), part_...  102 us
    pallas_call x1, Pallas kernels, hidden_units(): call(kernel, 'hidden_units', (GROUPS * turn,), [smem(), smem()] + [pl.Blo...  85.2 us
    pallas_call x1, Pallas kernels, finish(): call(kernel, 'finish', (steps,), [smem(), smem(), whole(turned.shape)] +...  50.9 us
    pallas_call x1, Pallas kernels, attend(): call(kernel, 'attend', (seqs, steps), [part_of(0), part_of(1), part_of(2)...  44.5 us
    pallas_call x1, Pallas kernels, middle_back(): call(kernel, 'middle_back', (steps,), [smem(), smem(), row, row, row, who...  31.9 us
    pallas_call x1, Pallas kernels, gather_first(): call(kernel, 'gather_first', (), gathering.in_specs(), gathering.out_spec...  25.6 us
    pallas_call x1, Pallas kernels, project(): call(kernel, 'project', (rows // block,), [smem(), smem(), pl.BlockSpec((...  14.6 us

profile of v5, /device:TPU:0, one launch (start us, length us, event | category | flops | bytes accessed | tf_op | source)
XLA Modules:
  0.0 383.4 jit_solution(2892774446638075525)
XLA Ops:
  0.6 0.8 fusion.23
  1.4 0.9 fusion.14
  2.4 0.7 reshape.53.refs_0_
  3.1 25.6 %gather_first.1 = (bf16[32,4608]{1,0:T(8,128)(2,1)}, bf16[128,4608]{1,0:T(8,128)(2,1)}, bf16[768,2304]{1,0:T(8,128)(2,1)}) custom-call(bf16[32,1152]{1,0:T(8,128)(2,1)} %reshape.53.refs_0_, bf16[128,1152]{1,0:T(8,128)(2,1)} %refs_1_.3, bf16[192,2304]{1,0:T(8,128)(2,1)} %refs_2_.1), custom_call_target="tpu_custom_call" | custom-call | bytes 3538944 | tf_op jit(solution)/shard_map/gather_first/pallas_call | solution.py:1348
  28.7 0.9 slice.102
  30.3 0.7 convert_element_type.60
  31.1 0.9 convert_reduce_fusion.1
  32.1 2.5 convolution_add_fusion.mod.refs_8_.refs_10_
  34.5 14.6 %project.1 = (bf16[2048,2304]{1,0:T(8,128)(2,1)}, bf16[768,2048]{1,0:T(8,128)(2,1)}) custom-call(s32[2]{0:T(128)} %refs_0_.3, s32[2]{0:T(128)} %refs_1_.5, bf16[2048,768]{1,0:T(8,128)(2,1)} %refs_12_.1, f32[8,1152]{1,0:T(8,128)} %convert_reduce_fusion.emb.gn.refs_4_.refs_5_.refs_9_.refs_8_.refs_15_, ...), custom_call_target="tpu_custom_call" | custom-call | flops 7247757312 | bytes 19267584 | tf_op jit(solution)/shard_map/project/pallas_call | solution.py:169
  49.1 44.5 %attend.1 = (bf16[2048,768]{1,0:T(8,128)(2,1)}, f32[2,6,2,1024]{3,2,1,0:T(2,128)}, bf16[768,768]{1,0:T(8,128)(2,1)}, bf16[768,3072]{1,0:T(8,128)(2,1)}, bf16[3072,768]{1,0:T(8,128)(2,1)}) custom-call(bf16[2048,2304]{1,0:T(8,128)(2,1)} %get-tuple-element.65.refs_0_.refs_1_.refs_2_, bf16[2048,2304]{1,0:T(8,128)(2,1)} %get-tuple-element.65.refs_0_.refs_1_.refs_2_, ...), custom_call_target="tpu_custom_call" | custom-call | flops 25769803776 | bytes 12582912 | tf_op jit(solution)/shard_map/attend/pallas_call | solution.py:580
  93.6 85.2 %hidden_units.1 = (bf16[2048,3072]{1,0:T(8,128)(2,1)}, bf16[2048,3072]{1,0:T(8,128)(2,1)}, f32[1,3072]{1,0:T(1,128)}, f32[2,768]{1,0:T(2,128)}, f32[2,768]{1,0:T...) custom-call(s32[2]{0:T(128)} %refs_0_.3, ...), custom_call_target="tpu_custom_call" | custom-call | flops 38654705664 | bytes 62914560 | tf_op jit(solution)/shard_map/hidden_units/pallas_call | solution.py:904
  178.9 31.9 %middle_back.1 = (f32[2048,768]{1,0:T(8,128)}, bf16[2048,768]{1,0:T(8,128)(2,1)}, bf16[4,192,768]{2,1,0:T(8,128)(2,1)}, f32[2,8,768]{2,1,0:T(8,128)}) custom-call(s32[2]{0:T(128)} %refs_0_.3, s32[2]{0:T(128)} %refs_1_.5, bf16[2048,768]{1,0:T(8,128)(2,1)} %get-tuple-element.66.refs_2_.mix.refs_3_.refs_13_, bf16[2048,768]{1,0:T(8,128)(2,1)} %refs_12_.1, ...), custom_call_target="tpu_custom_call" | custom-call | flops 16911433728 | bytes 36175872 | tf_op jit(solution)/shard_map/middle_back/pallas_call | solution.py:1005
  210.8 102.3 %attend_back.1 = (bf16[2048,768]{1,0:T(8,128)(2,1)}, bf16[2048,768]{1,0:T(8,128)(2,1)}, bf16[2048,768]{1,0:T(8,128)(2,1)}, bf16[192,1024]{1,0:T(8,128)(2,1)}, bf...) custom-call(bf16[2048,2304]{1,0:T(8,128)(2,1)} %get-tuple-element.65, ...), custom_call_target="tpu_custom_call" | custom-call | flops 64424509440 | bytes 25165824 | tf_op jit(solution)/shard_map/attend_back/pallas_call | solution.py:708
  313.2 0.8 slice_reduce_fusion.1
  314.1 0.7 fusion.15
  315.6 0.7 stack.63.refs_18_
  316.2 50.9 %finish.1 = (f32[2048,768]{1,0:T(8,128)}, bf16[2048,768]{1,0:T(8,128)(2,1)}, f32[128,1152]{1,0:T(8,128)}, f32[1,1152]{1,0:T(1,128)}, f32[8,256]{1,0:T(8,128)}, /...) custom-call(s32[2]{0:T(128)} %refs_0_.3, s32[2]{0:T(128)} %refs_1_.5, ...), custom_call_target="tpu_custom_call" | custom-call | flops 26575110144 | bytes 50331648 | tf_op jit(solution)/shard_map/finish/pallas_call | solution.py:1277
  367.2 0.8 slice.122
  368.7 1.3 reduce.3
  370.0 5.3 %assemble.1 = (f32[192,3072]{1,0:T(8,128)}, f32[3,256,768]{2,1,0:T(8,128)}, f32[192,768]{1,0:T(8,128)}, f32[192,2304]{1,0:T(8,128)}) custom-call(bf16[192,1024]{1,0:T(8,128)(2,1)} %get-tuple-element.92.refs_0_, bf16[192,1024]{1,0:T(8,128)(2,1)} %get-tuple-element.93.refs_1_, bf16[192,1024]{1,0:T(8,128)(2,1)} %get-tuple-element.94.refs_2_, ...), custom_call_target="tpu_custom_call" | custom-call | bytes 7077888 | tf_op jit(solution)/shard_map/assemble/pallas_call | solution.py:1391
  375.9 1.7 copy.37
  377.6 2.3 copy-done
  379.9 2.7 copy.38
  382.6 0.8 copy.39
  (34 shorter events, 2.8 us)
Async XLA Ops:
  31.1 3.4 copy-start.8
  210.8 102.4 %copy-start.3 = (f32[2,8,768]{2,1,0:T(8,128)S(1)}, f32[2,8,768]{2,1,0:T(8,128)}, u32[]{:S(2)}) copy-start(f32[2,8,768]{2,1,0:T(8,128)} %get-tuple-element.82) | copy-start | bytes 147460
  210.8 103.3 %copy-start.6 = (f32[2,768]{1,0:T(2,128)S(1)}, f32[2,768]{1,0:T(2,128)}, u32[]{:S(2)}) copy-start(f32[2,768]{1,0:T(2,128)} %get-tuple-element.83) | copy-start | bytes 18436
  210.8 103.3 %copy-start.7 = (f32[2,768]{1,0:T(2,128)S(1)}, f32[2,768]{1,0:T(2,128)}, u32[]{:S(2)}) copy-start(f32[2,768]{1,0:T(2,128)} %get-tuple-element.84) | copy-start | bytes 18436
  210.8 104.7 %copy-start.4 = (f32[1,3072]{1,0:T(1,128)S(1)}, f32[1,3072]{1,0:T(1,128)}, u32[]{:S(2)}) copy-start(f32[1,3072]{1,0:T(1,128)} %get-tuple-element.85) | copy-start | bytes 36868
  367.1 8.2 %copy-start.5 = (f32[8,256]{1,0:T(8,128)S(1)}, f32[8,256]{1,0:T(8,128)}, u32[]{:S(2)}) copy-start(f32[8,256]{1,0:T(8,128)} %get-tuple-element.89) | copy-start | bytes 24580
  367.2 8.8 %copy-start.1 = (bf16[2048,768]{1,0:T(8,128)(2,1)S(1)}, bf16[2048,768]{1,0:T(8,128)(2,1)}, u32[]{:S(2)}) copy-start(bf16[2048,768]{1,0:T(8,128)(2,1)} %get-tuple-element.154) | copy-start | bytes 9437188
  375.9 3.9 %copy-start = (f32[2048,768]{1,0:T(8,128)S(1)}, f32[2048,768]{1,0:T(8,128)}, u32[]{:S(2)}) copy-start(f32[2048,768]{1,0:T(8,128)} %get-tuple-element.155) | copy-start | bytes 18874372
  379.9 2.7 copy-start.2

commit v6 on v5

--- a/solution.py
+++ b/solution.py
@@ -1523,7 +1523,7 @@
         FINISH_TIMES, 4, seqs,
     )
     skip = lax.rem(share * me, PAIR)
-    own = lax.dynamic_slice_in_dim(gathered[:4], skip, share, 1)
+    own = lax.dynamic_slice(gathered, (0, skip), (4, share))
     g_ups, g_downs = (swaps[0], *done[0:4:2]), (swaps[1], *done[1:4:2])
     g_up, g_down, g_out, g_qkv = assemble(g_ups, g_downs, done[4], done[5:] + g_qkv)
     return (
@@ -1531,7 +1531,7 @@
         grad_tokens,
         own[0],
         grad_ada_weight,
-        grad_ada_bias[0],
+        grad_ada_bias.reshape(-1),
         own[1],
         g_qkv,
         g_out,

time: 384 us -> 384 us (level)
  no operation moved by 1% of the time
where the time goes in v6:
time: 384 us; the launch traced here: 383 us
  Pallas kernels  360 us (94%)
  local copies, waits for them, and re-layouts  13.7 us (4%)
  other arithmetic  6.07 us (2%)
    pallas_call x1, Pallas kernels, attend_back(): call(kernel, 'attend_back', (steps, seqs), [part_of(0), part_of(1), part_...  102 us
    pallas_call x1, Pallas kernels, hidden_units(): call(kernel, 'hidden_units', (GROUPS * turn,), [smem(), smem()] + [pl.Blo...  85.2 us
    pallas_call x1, Pallas kernels, finish(): call(kernel, 'finish', (steps,), [smem(), smem(), whole(turned.shape)] +...  50.9 us
    pallas_call x1, Pallas kernels, attend(): call(kernel, 'attend', (seqs, steps), [part_of(0), part_of(1), part_of(2)...  44.5 us
    pallas_call x1, Pallas kernels, middle_back(): call(kernel, 'middle_back', (steps,), [smem(), smem(), row, row, row, who...  31.9 us
    pallas_call x1, Pallas kernels, gather_first(): call(kernel, 'gather_first', (), gathering.in_specs(), gathering.out_spec...  25.6 us
    pallas_call x1, Pallas kernels, project(): call(kernel, 'project', (rows // block,), [smem(), smem(), pl.BlockSpec((...  14.6 us

profile of v6, /device:TPU:0, one launch (start us, length us, event | category | flops | bytes accessed | tf_op | source)
XLA Modules:
  0.0 383.4 jit_solution(9621890267393962305)
XLA Ops:
  0.6 0.8 fusion.23
  1.4 0.9 fusion.14
  2.4 0.7 reshape.56.refs_0_
  3.1 25.6 %gather_first.1 = (bf16[32,4608]{1,0:T(8,128)(2,1)}, bf16[128,4608]{1,0:T(8,128)(2,1)}, bf16[768,2304]{1,0:T(8,128)(2,1)}) custom-call(bf16[32,1152]{1,0:T(8,128)(2,1)} %reshape.56.refs_0_, bf16[128,1152]{1,0:T(8,128)(2,1)} %refs_1_.3, bf16[192,2304]{1,0:T(8,128)(2,1)} %refs_2_.1), custom_call_target="tpu_custom_call" | custom-call | bytes 3538944 | tf_op jit(solution)/shard_map/gather_first/pallas_call | solution.py:1348
  28.7 0.9 slice.99
  30.3 0.7 convert_element_type.60
  31.1 0.9 convert_reduce_fusion.1
  32.1 2.5 convolution_add_fusion.mod.refs_8_.refs_10_
  34.5 14.6 %project.1 = (bf16[2048,2304]{1,0:T(8,128)(2,1)}, bf16[768,2048]{1,0:T(8,128)(2,1)}) custom-call(s32[2]{0:T(128)} %refs_0_.3, s32[2]{0:T(128)} %refs_1_.5, bf16[2048,768]{1,0:T(8,128)(2,1)} %refs_12_.1, f32[8,1152]{1,0:T(8,128)} %convert_reduce_fusion.emb.gn.refs_4_.refs_5_.refs_9_.refs_8_.refs_15_, ...), custom_call_target="tpu_custom_call" | custom-call | flops 7247757312 | bytes 19267584 | tf_op jit(solution)/shard_map/project/pallas_call | solution.py:169
  49.1 44.5 %attend.1 = (bf16[2048,768]{1,0:T(8,128)(2,1)}, f32[2,6,2,1024]{3,2,1,0:T(2,128)}, bf16[768,768]{1,0:T(8,128)(2,1)}, bf16[768,3072]{1,0:T(8,128)(2,1)}, bf16[3072,768]{1,0:T(8,128)(2,1)}) custom-call(bf16[2048,2304]{1,0:T(8,128)(2,1)} %get-tuple-element.65.refs_0_.refs_1_.refs_2_, bf16[2048,2304]{1,0:T(8,128)(2,1)} %get-tuple-element.65.refs_0_.refs_1_.refs_2_, ...), custom_call_target="tpu_custom_call" | custom-call | flops 25769803776 | bytes 12582912 | tf_op jit(solution)/shard_map/attend/pallas_call | solution.py:580
  93.6 85.2 %hidden_units.1 = (bf16[2048,3072]{1,0:T(8,128)(2,1)}, bf16[2048,3072]{1,0:T(8,128)(2,1)}, f32[1,3072]{1,0:T(1,128)}, f32[2,768]{1,0:T(2,128)}, f32[2,768]{1,0:T...) custom-call(s32[2]{0:T(128)} %refs_0_.3, ...), custom_call_target="tpu_custom_call" | custom-call | flops 38654705664 | bytes 62914560 | tf_op jit(solution)/shard_map/hidden_units/pallas_call | solution.py:904
  178.9 31.9 %middle_back.1 = (f32[2048,768]{1,0:T(8,128)}, bf16[2048,768]{1,0:T(8,128)(2,1)}, bf16[4,192,768]{2,1,0:T(8,128)(2,1)}, f32[2,8,768]{2,1,0:T(8,128)}) custom-call(s32[2]{0:T(128)} %refs_0_.3, s32[2]{0:T(128)} %refs_1_.5, bf16[2048,768]{1,0:T(8,128)(2,1)} %get-tuple-element.66.refs_2_.mix.refs_3_.refs_13_, bf16[2048,768]{1,0:T(8,128)(2,1)} %refs_12_.1, ...), custom_call_target="tpu_custom_call" | custom-call | flops 16911433728 | bytes 36175872 | tf_op jit(solution)/shard_map/middle_back/pallas_call | solution.py:1005
  210.8 102.3 %attend_back.1 = (bf16[2048,768]{1,0:T(8,128)(2,1)}, bf16[2048,768]{1,0:T(8,128)(2,1)}, bf16[2048,768]{1,0:T(8,128)(2,1)}, bf16[192,1024]{1,0:T(8,128)(2,1)}, bf...) custom-call(bf16[2048,2304]{1,0:T(8,128)(2,1)} %get-tuple-element.65, ...), custom_call_target="tpu_custom_call" | custom-call | flops 64424509440 | bytes 25165824 | tf_op jit(solution)/shard_map/attend_back/pallas_call | solution.py:708
  313.2 0.8 slice_reduce_fusion.1
  314.1 0.7 fusion.15
  315.6 0.7 stack.63.refs_18_
  316.2 50.9 %finish.1 = (f32[2048,768]{1,0:T(8,128)}, bf16[2048,768]{1,0:T(8,128)(2,1)}, f32[128,1152]{1,0:T(8,128)}, f32[1,1152]{1,0:T(1,128)}, f32[8,256]{1,0:T(8,128)}, /...) custom-call(s32[2]{0:T(128)} %refs_0_.3, s32[2]{0:T(128)} %refs_1_.5, ...), custom_call_target="tpu_custom_call" | custom-call | flops 26575110144 | bytes 50331648 | tf_op jit(solution)/shard_map/finish/pallas_call | solution.py:1277
  367.2 1.6 fusion.20
  368.7 1.3 reduce.3
  370.0 5.3 %assemble.1 = (f32[192,3072]{1,0:T(8,128)}, f32[3,256,768]{2,1,0:T(8,128)}, f32[192,768]{1,0:T(8,128)}, f32[192,2304]{1,0:T(8,128)}) custom-call(bf16[192,1024]{1,0:T(8,128)(2,1)} %get-tuple-element.92.refs_0_, bf16[192,1024]{1,0:T(8,128)(2,1)} %get-tuple-element.93.refs_1_, bf16[192,1024]{1,0:T(8,128)(2,1)} %get-tuple-element.94.refs_2_, ...), custom_call_target="tpu_custom_call" | custom-call | bytes 7077888 | tf_op jit(solution)/shard_map/assemble/pallas_call | solution.py:1391
  376.0 1.7 copy.37
  377.7 2.3 copy-done
  379.9 2.7 copy.38
  382.6 0.8 copy.39
  (33 shorter events, 2.2 us)
Async XLA Ops:
  31.1 3.4 copy-start.8
  210.8 102.4 %copy-start.3 = (f32[2,8,768]{2,1,0:T(8,128)S(1)}, f32[2,8,768]{2,1,0:T(8,128)}, u32[]{:S(2)}) copy-start(f32[2,8,768]{2,1,0:T(8,128)} %get-tuple-element.82) | copy-start | bytes 147460
  210.8 103.3 %copy-start.6 = (f32[2,768]{1,0:T(2,128)S(1)}, f32[2,768]{1,0:T(2,128)}, u32[]{:S(2)}) copy-start(f32[2,768]{1,0:T(2,128)} %get-tuple-element.83) | copy-start | bytes 18436
  210.8 103.3 %copy-start.7 = (f32[2,768]{1,0:T(2,128)S(1)}, f32[2,768]{1,0:T(2,128)}, u32[]{:S(2)}) copy-start(f32[2,768]{1,0:T(2,128)} %get-tuple-element.84) | copy-start | bytes 18436
  210.8 104.7 %copy-start.4 = (f32[1,3072]{1,0:T(1,128)S(1)}, f32[1,3072]{1,0:T(1,128)}, u32[]{:S(2)}) copy-start(f32[1,3072]{1,0:T(1,128)} %get-tuple-element.85) | copy-start | bytes 36868
  367.1 8.2 %copy-start.5 = (f32[8,256]{1,0:T(8,128)S(1)}, f32[8,256]{1,0:T(8,128)}, u32[]{:S(2)}) copy-start(f32[8,256]{1,0:T(8,128)} %get-tuple-element.89) | copy-start | bytes 24580
  367.2 8.8 %copy-start.1 = (bf16[2048,768]{1,0:T(8,128)(2,1)S(1)}, bf16[2048,768]{1,0:T(8,128)(2,1)}, u32[]{:S(2)}) copy-start(bf16[2048,768]{1,0:T(8,128)(2,1)} %get-tuple-element.154) | copy-start | bytes 9437188
  376.0 3.9 %copy-start = (f32[2048,768]{1,0:T(8,128)S(1)}, f32[2048,768]{1,0:T(8,128)}, u32[]{:S(2)}) copy-start(f32[2048,768]{1,0:T(8,128)} %get-tuple-element.155) | copy-start | bytes 18874372
  379.9 2.7 copy-start.2
